TPU v7x, 32 devices: a whole 2x2x4 slice. The times are simulated.
32 devices in a mesh: rep: 4 (over x, core), stripe: 8 (over z, y).
Axes of the slice: x: 2, y: 2, z: 4, core: 2. Of those that a mesh axis runs over, the one named last changes fastest.
Arguments:
- activations: bfloat16 [1024, 1024], P('rep'), may hold values from -6 to 6
- out_grads: bfloat16 [1024, 4096], P('rep', 'stripe'), may hold values from -4 to 4
- statistics: float32 [4, 8, 512, 512], P('rep', 'stripe'), may hold values from -48 to 4608, as said below
- owner_blocks: int32 [8, 2], P('stripe'), may hold values from 0 to 1, each once within a row
Outputs:
- preconditioned: float32 [1024, 4096], P(None, 'stripe')
- new_stats: float32 [4, 8, 512, 512], P('rep', 'stripe')
Inputs may be any that keep to these rules, and one draw needn't show every extreme that they name: statistics[p, s] is symmetric positive definite for every p and s. `owner_blocks`: each row lists every row block 0 to 1 exactly once.
All inputs are finite; a program needn't handle non-finite values.
Results may differ from a plain program's by a relative error of at most 0.0003.
Values sent between devices are 32-bit elements; how exact they have to be, the bound alone decides.
No kernel may reach another device: no remote copies, remote signals or barrier semaphores. Data moves between devices by JAX's collectives and lax.ppermute only.
A program may use at most 128 MiB of HBM per device.

v0:
```python
import jax
import jax.numpy as jnp
from jax import lax
from jax.sharding import PartitionSpec as P

BLOCK = 512
ITERS = 2


decay_rate = 0.95
damping = 0.25
epsilon = 1e-06
highest = lax.Precision.HIGHEST


def partner(shard, axis, stride):
    return lax.ppermute(shard, axis, [(i, i ^ 1 << stride) for i in range(lax.axis_size(axis))])


def inverse_root(damped):
    identity = jnp.eye(damped.shape[-1], dtype=damped.dtype)
    frob_norm = jnp.sqrt(jnp.sum(damped * damped, axis=(-2, -1), keepdims=True) + epsilon)
    scaled = damped / frob_norm
    root_now = identity * frob_norm ** (-0.25)
    for sweep in range(ITERS):
        factor = (5.0 * identity - scaled) * 0.25
        root_now = jnp.matmul(root_now, factor, precision=highest)
        if sweep + 1 < ITERS:
            square = jnp.matmul(factor, factor, precision=highest)
            fourth = jnp.matmul(square, square, precision=highest)
            scaled = jnp.matmul(fourth, scaled, precision=highest)
    return root_now


def slot_terms(activations, out_grads, blocks_of, pair_count, piece_rows, row_count):
    tokens_here, in_width = activations.shape
    per_block = BLOCK // piece_rows
    shaped = activations.reshape(tokens_here, in_width // piece_rows, piece_rows)
    slot_count = row_count // piece_rows
    slot_ids = jnp.arange(slot_count, dtype=jnp.int32)
    block_ids = jnp.take(blocks_of, slot_ids % pair_count)
    half_ids = slot_ids // pair_count % per_block
    chosen = jnp.take(shaped, block_ids * per_block + half_ids, axis=1)
    products = jnp.einsum("tkp,tc->kpc", chosen, out_grads, preferred_element_type=jnp.float32)
    return products.reshape(slot_count * piece_rows, out_grads.shape[1])


def per_device(activations, out_grads, statistics, owner_blocks):
    rep_count = lax.axis_size("rep")
    pair_count = rep_count // 2
    pair_bit = rep_count.bit_length() - 2
    half_rows = BLOCK // 2
    my_index = lax.axis_index("rep")
    is_left = my_index < pair_count
    blocks_of = owner_blocks[0]
    own_half = lax.psum_scatter(
        slot_terms(
            activations,
            out_grads,
            blocks_of,
            pair_count,
            half_rows,
            half_rows * lax.axis_size("rep"),
        ),
        "rep",
        scatter_dimension=0,
        tiled=True,
    )
    partner_half = partner(own_half, "rep", pair_bit)
    gradient = jnp.where(
        is_left,
        jnp.concatenate([own_half, partner_half], axis=0),
        jnp.concatenate([partner_half, own_half], axis=0),
    )
    facing = jnp.where(is_left, gradient, gradient.T)
    new_stat = decay_rate * statistics[0, 0] + jnp.dot(facing, facing.T, precision=highest)
    trace_sum = lax.psum(jnp.trace(new_stat), ("rep", "stripe"))
    mean_diag = trace_sum / (rep_count * lax.axis_size("stripe") * BLOCK)
    identity = jnp.eye(BLOCK, dtype=jnp.float32)
    root_now = inverse_root(new_stat + damping * mean_diag * identity)
    partner_root = partner(root_now, "rep", pair_bit)
    left_root = jnp.where(is_left, root_now, partner_root)
    right_root = jnp.where(is_left, partner_root, root_now)
    row_start = jnp.where(is_left, 0, half_rows).astype(jnp.int32)
    my_rows = lax.dynamic_slice_in_dim(left_root, row_start, half_rows, 0)
    grad_rows = lax.dynamic_slice_in_dim(gradient, row_start, half_rows, 0)
    precond_half = jnp.dot(
        jnp.dot(my_rows, gradient, precision=highest), right_root, precision=highest
    )
    grad_sq, prec_sq = lax.psum(
        (jnp.sum(grad_rows * grad_rows), jnp.sum(precond_half * precond_half)), ("rep", "stripe")
    )
    scaled = precond_half * jnp.sqrt(grad_sq / (prec_sq + epsilon))
    gathered = lax.all_gather(scaled[None], "rep", axis=0, tiled=True)
    pair_ids = jnp.arange(pair_count, dtype=jnp.int32)
    inverse = jnp.sum(
        pair_ids[:, None] * (blocks_of[:, None] == pair_ids[None, :]).astype(jnp.int32), axis=0
    )
    row_order = jnp.stack([inverse, inverse + pair_count], axis=1).reshape(-1)
    preconditioned = jnp.take(gathered, row_order, axis=0).reshape(
        pair_count * BLOCK, gathered.shape[2]
    )
    return (preconditioned, new_stat[None, None])


def solution(mesh):
    in_specs = (
        P("rep", None),
        P("rep", "stripe"),
        P("rep", "stripe", None, None),
        P("stripe", None),
    )
    out_specs = (P(None, "stripe"), P("rep", "stripe", None, None))
    return jax.shard_map(
        per_device, mesh=mesh, in_specs=in_specs, out_specs=out_specs, check_vma=False
    )
```

profile of v0, /device:TPU:0, one launch (start us, length us, event | category | flops | bytes accessed | tf_op | source)
XLA Modules:
  0.0 226.6 jit_solution(13297253253330376592)
XLA Ops:
  8.2 1.3 gather_fusion
  9.6 1.2 copy.26
  12.2 1.8 copy.29
  14.1 34.0 %reduce-scatter.2.cloned.1.call-done = f32[256,512]{0,1:T(8,128)} async-done(((f32[1024,512]{0,1:T(8,128)}), f32[256,512]{0,1:T(8,128)}) %reduce-scatter.2.cloned.1.call-update) | async-done | bytes 524304 | tf_op jit(solution)/shard_map/reduce_scatter | solution.py:56
  48.5 13.4 %collective-permute-done = f32[256,512]{0,1:T(8,128)S(1)} collective-permute-done((f32[256,512]{0,1:T(8,128)}, f32[256,512]{0,1:T(8,128)S(1)}, u32[]{:S(2)}, u32[]{:S(2)}) %collective-permute-start) | collective-permute-done | bytes 524320 | tf_op jit(solution)/shard_map/ppermute | solution.py:17
  61.8 1.6 maximum_select_fusion
  63.8 5.6 %select_reduce_fusion = (f32[]{:T(128)}, f32[512,512]{1,0:T(8,128)S(1)}) fusion(f32[512,512]{1,0:T(8,128)S(1)} %copy.31, pred[]{:T(512)S(6)} %lt.75, f32[256,512]{0,1:T(8,128)} %reduce-scatter.2.cloned.1.call-done, f32[256,512]{0,1:T(8,128)} %copy-done.2, f32[1,1,512,512]{3,2,1,0:T(8,128)} %param.6), kind=kOutput, calls=%fused_computation.17 | convolution fusion | flops 1612972032 | bytes 4194309 | tf_op jit(solution)/shard_map/dot_general | solution.py:76
  69.4 39.7 %psum.21 = f32[]{:T(128)} all-reduce(f32[]{:T(128)} %get-tuple-element.4), channel_id=1, replica_groups=mesh['rep'=4,'stripe'=8] {'rep','stripe'}, use_global_device_ids=true, to_apply=%region_3.4 | all-reduce | flops 1 | bytes 8 | tf_op jit(solution)/shard_map/psum | solution.py:77
  109.6 1.0 multiply_reduce_fusion
  111.3 2.0 fusion.7
  113.4 1.9 fusion.4
  115.3 1.8 fusion.47
  117.2 1.9 fusion
  119.1 1.9 fusion.48
  121.0 2.3 %collective-permute-start.1 = (f32[512,512]{1,0:T(8,128)S(1)}, f32[512,512]{1,0:T(8,128)S(1)}, u32[]{:S(2)}, u32[]{:S(2)}) collective-permute-start(f32[512,512]{1,0:T(8,128)S(1)} %fusion.48), channel_id=1, source_target_pairs={{0,16},{8,24},{16,0},{24,8},{1,17},{9,25},{17,1},{25,9},{2,18},{10... | collective-permute-start | bytes 3145736 | tf_op jit(solution)/shard_map/ppermute | solution.py:17
  123.3 0.8 multiply_reduce_fusion.2
  124.1 21.7 %collective-permute-done.1 = f32[512,512]{1,0:T(8,128)S(1)} collective-permute-done((f32[512,512]{1,0:T(8,128)S(1)}, f32[512,512]{1,0:T(8,128)S(1)}, u32[]{:S(2)}, u32[]{:S(2)}) %collective-permute-start.1) | collective-permute-done | bytes 1048608 | tf_op jit(solution)/shard_map/ppermute | solution.py:17
  145.8 2.7 %fusion.10 = f32[256,512]{1,0:T(8,128)S(1)} fusion(f32[512,512]{1,0:T(8,128)S(1)} %collective-permute-done.1, s32[]{:T(128)S(6)} %select_n.184, f32[512,512]{1,0:T(8,128)S(1)} %fusion.48, pred[]{:T(512)S(6)} %lt.75, f32[256,512]{0,1:T(8,128)} %copy-done.2, f32[256,512]{0,1:T(8,128)} %reduce-scatter.2.cloned.1.call-done), kind=kOutput, calls=%fused_computation.22 | convolution fusion | flops 806223872 | bytes 2622976 | tf_op jit(solution)/shard_map/dot_general | solution.py:88
  148.5 1.8 multiply_reduce_fusion.1
  150.3 39.7 %all-reduce = (f32[]{:T(128)}, f32[]{:T(128)}) all-reduce(f32[]{:T(128)} %multiply_reduce_fusion.2, f32[]{:T(128)} %get-tuple-element.6), channel_id=1, replica_groups=mesh['rep'=4,'stripe'=8] {'rep','stripe'}, use_global_device_ids=true, to_apply=%region_6.7 | all-reduce | flops 2 | bytes 16 | tf_op jit(solution)/shard_map/psum | solution.py:90
  191.4 0.8 broadcast_multiply_fusion
  192.4 23.6 %all-gather.3.cloned.1.call-done = f32[1024,512]{1,0:T(8,128)} async-done(((f32[256,512]{1,0:T(8,128)}), f32[1024,512]{1,0:T(8,128)}) %all-gather.3.cloned.1.call-update) | async-done | bytes 2097168 | tf_op jit(solution)/shard_map/all_gather | solution.py:94
  216.0 2.3 %gather_fusion.2 = f32[4,256,512]{2,1,0:T(8,128)S(1)} fusion(f32[4,256,512]{2,1,0:T(8,128)} %bitcast.41, s32[1024]{0:T(1024)S(1)} %pad_clamp_fusion), kind=kCustom, calls=%fused_computation.2 | custom fusion | bytes 4194320 | tf_op jit(solution)/shard_map/jit(_take)/gather | solution.py:100
  218.2 1.5 bitcast_select_fusion
  (30 shorter events, 3.4 us)
Async XLA Ops:
  7.2 4.4 %copy-start = (bf16[256,512]{1,0:T(8,128)(2,1)S(1)}, bf16[256,512]{1,0:T(8,128)(2,1)}, u32[]{:S(2)}) copy-start(bf16[256,512]{1,0:T(8,128)(2,1)} %param.5) | copy-start | bytes 786436
  7.2 40.9 %reduce-scatter.2.cloned.1.call-start = ((), (), s32[]{:S(2)}) async-start(), calls=%async_computation.1 | async-start | bytes 2621440 | tf_op jit(solution)/shard_map/reduce_scatter | solution.py:56
  14.0 201.9 %all-gather.3.cloned.1.call-start = ((), (), s32[]{:S(2)}) async-start(), calls=%async_computation.2 | async-start | bytes 2621440 | tf_op jit(solution)/shard_map/all_gather | solution.py:94
  48.1 13.7 %collective-permute-start = (f32[256,512]{0,1:T(8,128)}, f32[256,512]{0,1:T(8,128)S(1)}, u32[]{:S(2)}, u32[]{:S(2)}) collective-permute-start(f32[256,512]{0,1:T(8,128)} %reduce-scatter.2.cloned.1.call-done), channel_id=1, source_target_pairs={{0,16},{8,24},{16,0},{24,8},{1,17},{9,25},{17,1},{25,9},{2,18},{10... | collective-permute-start | bytes 1572872 | tf_op jit(solution)/shard_map/ppermute | solution.py:17
  61.8 1.6 copy-start.2
  69.4 47.8 %copy-start.1 = (f32[512,512]{1,0:T(8,128)}, f32[512,512]{1,0:T(8,128)S(1)}, u32[]{:S(2)}) copy-start(f32[512,512]{1,0:T(8,128)S(1)} %get-tuple-element.5) | copy-start | bytes 3145732
  121.0 24.9 %collective-permute-start.1 = (f32[512,512]{1,0:T(8,128)S(1)}, f32[512,512]{1,0:T(8,128)S(1)}, u32[]{:S(2)}, u32[]{:S(2)}) collective-permute-start(f32[512,512]{1,0:T(8,128)S(1)} %fusion.48), channel_id=1, source_target_pairs={{0,16},{8,24},{16,0},{24,8},{1,17},{9,25},{17,1},{25,9},{2,18},{10... | collective-permute-start | bytes 3145736 | tf_op jit(solution)/shard_map/ppermute | solution.py:17
Sparse Core Ops, SparseCore 0:
  14.2 33.8 reduce-scatter.1
  192.3 23.5 all-gather.2
where the time goes:
time: 227 us
  waiting for transfers between devices  92.7 us (41%)
  blocking collectives  79.4 us (35%)
  matrix products  20.2 us (9%)
  between operations  17 us (7%)
  local copies, waits for them, and re-layouts  8.1 us (4%)
  other arithmetic  6.57 us (3%)
  starting transfers between devices  2.79 us (1%)
    psum x1, blocking collectives, per_device(): lax.psum((jnp.sum(grad_rows * grad_rows), jnp.sum(precond_half * precond_...  39.7 us
    psum x1, blocking collectives, per_device(): trace_sum = lax.psum(jnp.trace(new_stat), ('rep', 'stripe'))  39.7 us
    ppermute x2, waiting for transfers between devices, partner(): lax.ppermute(shard, axis, [(i, i ^ 1 << stride) for i in range(lax.axis_s...  35.1 us
    reduce_scatter x1, waiting for transfers between devices, per_device(): lax.psum_scatter(slot_terms(activations, out_grads, blocks_of, pair_count...  34 us
    all_gather x1, waiting for transfers between devices, per_device(): gathered = lax.all_gather(scaled[None], 'rep', axis=0, tiled=True)  23.6 us
    dot_general x1, matrix products, per_device(): jnp.dot(facing, facing.T, precision=highest)  5.62 us
  transfers between devices with their start and end apart: 4, of which 4 were waited for; matrix products, arithmetic and copies ran while one was open for 0% of the time, Pallas kernels for 0%

commit v1 on v0

v1 whole, which is shorter than its diff:
```python
import math

import jax
import jax.numpy as jnp
from jax import lax
from jax.sharding import PartitionSpec as P

BLOCK = 512
HALF = BLOCK // 2

decay_rate = 0.95
damping = 0.25
epsilon = 1e-06
high = lax.Precision.HIGH
AXES = ("rep", "stripe")

ROOT_COEFFS = (
    25 / 16,
    -5 / 16 - 3125 / 4096,
    3125 / 4096,
    -1250 / 4096,
    250 / 4096,
    -25 / 4096,
    1 / 4096,
)


def flip(x, mask):
    return lax.ppermute(x, "rep", [(i, i ^ mask) for i in range(lax.axis_size("rep"))])


def share(partials):
    devices = lax.axis_size("rep") * lax.axis_size("stripe")
    spread = jnp.broadcast_to(partials[None], (devices,) + partials.shape)
    return lax.all_to_all(spread, AXES, 0, 0)


def lane_sums(x):
    return jnp.sum(x.reshape(-1, x.shape[-1] // 128, 128), axis=(0, 1))


def powers(stat):
    norm_sq = jnp.sum(stat * stat)
    trace = jnp.trace(stat)
    norm = jnp.sqrt(norm_sq + epsilon)
    t1 = stat * (1.0 / norm)
    t2 = jnp.dot(t1, t1, precision=high)
    t3 = jnp.dot(t1, t2, precision=high)
    return (t1, t2, t3), norm, norm_sq, trace


def shifted(norm, norm_sq, trace, shift):
    frob = jnp.sqrt(norm_sq + 2.0 * shift * trace + BLOCK * shift * shift + epsilon)
    a, e = norm / frob, shift / frob
    outer = frob ** (-0.25)
    out = []
    for i in range(7):
        total = 0.0
        for j in range(6, i - 1, -1):
            total = total * e + math.comb(j, i) * ROOT_COEFFS[j]
        out.append(outer * total)
        outer = outer * a
    return out


def root_of(t, t3_rows, rows, eye_rows, k):
    inner = k[4] * t[0] + k[5] * t[1] + k[6] * t[2]
    return k[0] * eye_rows + k[1] * rows[0] + k[2] * rows[1] + k[3] * t3_rows + jnp.dot(t3_rows, inner, precision=high)


def per_device(activations, out_grads, statistics, owner_blocks):
    rep_count = lax.axis_size("rep")
    pairs = rep_count // 2
    devices = rep_count * lax.axis_size("stripe")
    me = lax.axis_index("rep")
    chip, core = me // 2, me % 2
    first = core == 0
    owners = owner_blocks[0]
    stat_in = statistics[0, 0]
    tokens = activations.shape[0]

    def term(j, half):
        block = jnp.take(owners, chip ^ j)
        cols = lax.dynamic_slice(activations, (jnp.int32(0), block * BLOCK + half * HALF), (tokens, HALF))
        return lax.dot_general(cols, out_grads, (((0,), (0,)), ((), ())), preferred_element_type=jnp.float32)

    send = jnp.stack([term(j, 1 - core) for j in range(pairs)])
    keep = jnp.stack([term(j, core) for j in range(pairs)])
    acc = keep + flip(send, 1)
    shuffle = [(s * pairs + p, 2 * p + s) for s in range(2) for p in range(pairs)]
    stat_own = lax.ppermute(stat_in, "rep", shuffle)
    stat_other = flip(stat_own, 1)
    m = pairs // 2
    while m:
        acc = acc[:m] + flip(acc[m : 2 * m], 2 * m)
        m //= 2
    g_half = acc[0]
    g_other = flip(g_half, 1)
    grad = jnp.where(first, jnp.concatenate([g_half, g_other]), jnp.concatenate([g_other, g_half]))
    eye = jnp.eye(BLOCK, dtype=jnp.float32)
    diag = jnp.sum(stat_in * eye, axis=0).reshape(-1, 128).sum(axis=0)
    sums = jnp.sum(share(jnp.stack([lane_sums(g_half * g_half), diag])), axis=(0, 2))
    grad_sq = sums[0]
    shift = damping * (decay_rate * sums[1] + 2.0 * grad_sq) / (devices * BLOCK)

    stat_left = decay_rate * jnp.where(first, stat_own, stat_other) + jnp.dot(grad, grad.T, precision=high)
    stat_right = decay_rate * jnp.where(first, stat_other, stat_own) + jnp.dot(grad.T, grad, precision=high)
    new_stat = lax.ppermute(jnp.where(first, stat_left, stat_right), "rep", [(b, a) for a, b in shuffle])
    t_left, *left = powers(stat_left)
    t_right, *right = powers(stat_right)

    k_left = shifted(*left, shift)
    k_right = shifted(*right, shift)
    rows = [lax.dynamic_slice_in_dim(x, core * HALF, HALF, 0) for x in t_left]
    left_rows = root_of(t_left, rows[2], rows, lax.dynamic_slice_in_dim(eye, core * HALF, HALF, 0), k_left)
    right_root = root_of(t_right, t_right[2], t_right, eye, k_right)
    mine = jnp.dot(jnp.dot(left_rows, grad, precision=high), right_root, precision=high)
    prec_sq = jnp.sum(share(lane_sums(mine * mine)[None]))
    scale = jnp.sqrt(grad_sq / (prec_sq + epsilon))

    direct = mine[None]
    across = flip(direct, 1)
    m = 1
    while m < pairs:
        got = flip(direct, 2 * m)
        across = jnp.concatenate([across, flip(got, 1)])
        direct = jnp.concatenate([direct, got])
        m *= 2
    pieces = jnp.concatenate([direct, across])
    ids = jnp.arange(pairs, dtype=jnp.int32)
    inverse = jnp.sum(ids[:, None] * (owners[:, None] == ids[None, :]).astype(jnp.int32), axis=0)
    order = (chip ^ inverse)[:, None] + pairs * (jnp.arange(2, dtype=jnp.int32)[None] != core)
    placed = jnp.take(pieces, order.reshape(-1), axis=0) * scale
    return placed.reshape(pairs * BLOCK, -1), new_stat[None, None]


def solution(mesh):
    in_specs = (
        P("rep", None),
        P("rep", "stripe"),
        P("rep", "stripe", None, None),
        P("stripe", None),
    )
    out_specs = (P(None, "stripe"), P("rep", "stripe", None, None))
    return jax.shard_map(per_device, mesh=mesh, in_specs=in_specs, out_specs=out_specs, check_vma=False)
```

time: 227 us -> 112 us (0.49)
  blocking collectives: 79.4 us -> 0 us
  waiting for transfers between devices: 92.7 us -> 29.3 us
  starting transfers between devices: 2.79 us -> 34 us
  between operations: 17 us -> 9.14 us
  other arithmetic: 6.57 us -> 10.2 us
    psum x2 -> x0, blocking collectives: 79.4 us -> none  [the longest x1 39.7 us: per_device(): lax.psum((jnp.sum(grad_rows * grad_rows), jnp.sum(precond_half * precond_...]
    reduce_scatter x1 -> x0, waiting for transfers between devices: 34 us -> none  [per_device(): lax.psum_scatter(slot_terms(activations, out_grads, blocks_of, pair_count...]
    all_gather x1 -> x0, waiting for transfers between devices: 23.6 us -> none  [per_device(): gathered = lax.all_gather(scaled[None], 'rep', axis=0, tiled=True)]
    ppermute x2 -> x9, starting transfers between devices: 2.71 us -> 25.3 us  [the longest x7 14 us: flip(): lax.ppermute(x, 'rep', [(i, i ^ mask) for i in range(lax.axis_size('rep'))])]
    ppermute x2 -> x9, waiting for transfers between devices: 35.1 us -> 14.6 us  [the longest x7 14.6 us: flip(): lax.ppermute(x, 'rep', [(i, i ^ mask) for i in range(lax.axis_size('rep'))])]
    all_to_all x0 -> x2, waiting for transfers between devices: none -> 14.6 us  [share(): return lax.all_to_all(spread, AXES, 0, 0)]
    all_to_all x0 -> x2, starting transfers between devices: none -> 8.71 us  [share(): return lax.all_to_all(spread, AXES, 0, 0)]
    select_n x5 -> x1, other arithmetic: 3.15 us -> 0.01 us  [per_device(): placed = jnp.take(pieces, order.reshape(-1), axis=0) * scale]
  transfers between devices with their start and end apart: 4 -> 11, of which waited for: 4 -> 4; matrix products, arithmetic and copies ran while one was open for 0% -> 6% of each run, Pallas kernels for 0% -> 0%
where the time goes in v1:
time: 112 us; the launch traced here: 110 us
  starting transfers between devices  34 us (30%)
  waiting for transfers between devices  29.3 us (26%)
  matrix products  18.6 us (17%)
  other arithmetic  10.2 us (9%)
  between operations  9.14 us (8%)
  local copies, waits for them, and re-layouts  9.04 us (8%)
    all_to_all x2, waiting for transfers between devices, share(): return lax.all_to_all(spread, AXES, 0, 0)  14.6 us
    ppermute x7, waiting for transfers between devices, flip(): lax.ppermute(x, 'rep', [(i, i ^ mask) for i in range(lax.axis_size('rep'))])  14.6 us
    ppermute x7, starting transfers between devices, flip(): lax.ppermute(x, 'rep', [(i, i ^ mask) for i in range(lax.axis_size('rep'))])  14 us
    ppermute x1, starting transfers between devices, per_device(): stat_own = lax.ppermute(stat_in, 'rep', shuffle)  9.46 us
    all_to_all x2, starting transfers between devices, share(): return lax.all_to_all(spread, AXES, 0, 0)  8.71 us
    dot_general x1, matrix products, per_device(): jnp.dot(grad.T, grad, precision=high)  4.73 us
    dot_general x1, matrix products, per_device(): jnp.dot(grad, grad.T, precision=high)  3.33 us
    unnamed x21, local copies, waits for them, and re-layouts  3.32 us
  transfers between devices with their start and end apart: 11, of which 4 were waited for; matrix products, arithmetic and copies ran while one was open for 6% of the time, Pallas kernels for 0%

profile of v1, /device:TPU:0, one launch (start us, length us, event | category | flops | bytes accessed | tf_op | source)
XLA Modules:
  0.0 110.3 jit_solution(17412842269274839415)
XLA Ops:
  0.7 1.3 %constant_dynamic-slice_fusion = (s32[1,1]{1,0:T(1,128)}, s32[1,1]{1,0:T(1,128)}) fusion(s32[1,2]{1,0:T(1,128)} %param.7, s32[]{:T(128)S(6)} %select_n.101, s32[]{:T(128)S(6)} %select_n.104), kind=kLoop, calls=%fused_computation.62 | loop fusion | bytes 24 | solution.py:83
  3.3 1.2 %convolution_bitcast_fusion.1 = f32[1,256,512]{2,1,0:T(8,128)S(1)} fusion(bf16[256,512]{1,0:T(8,128)(2,1)} %param.5, bf16[256,1024]{1,0:T(8,128)(2,1)S(1)} %copy-done, s32[]{:T(128)S(6)} %select_n.107), kind=kOutput, calls=%fused_computation.7 | convolution fusion | flops 67108864 | bytes 917508 | tf_op jit(solution)/shard_map/dot_general | solution.py:85
  4.6 1.2 %convolution_bitcast_fusion = f32[1,256,512]{2,1,0:T(8,128)S(1)} fusion(bf16[256,512]{1,0:T(8,128)(2,1)} %param.5, bf16[256,1024]{1,0:T(8,128)(2,1)S(1)} %copy-done, s32[]{:T(128)S(6)} %select_n.108), kind=kOutput, calls=%fused_computation.6 | convolution fusion | flops 67108864 | bytes 917508 | tf_op jit(solution)/shard_map/dot_general | solution.py:85
  5.8 1.0 pad_maximum_fusion.1
  7.3 9.5 %collective-permute-start = (f32[512,512]{1,0:T(8,128)}, f32[512,512]{1,0:T(8,128)}, u32[]{:S(2)}, u32[]{:S(2)}) collective-permute-start(f32[512,512]{1,0:T(8,128)} %bitcast.1), channel_id=1, source_target_pairs={{0,0},{8,16},{16,8},{24,24},{1,1},{9,17},{17,9},{25,25},{2,2},{10,... | collective-permute-start | bytes 3145736 | tf_op jit(solution)/shard_map/ppermute | solution.py:91
  17.6 11.1 %collective-permute-start.1 = (f32[512,512]{1,0:T(8,128)}, f32[512,512]{1,0:T(8,128)S(1)}, u32[]{:S(2)}, u32[]{:S(2)}) collective-permute-start(f32[512,512]{1,0:T(8,128)} %collective-permute-done), channel_id=1, source_target_pairs={{0,8},{8,0},{16,24},{24,16},{1,9},{9,1},{17,25},{25,17},{2,10},{10... | collective-permute-start | bytes 3145736 | tf_op jit(solution)/shard_map/ppermute | solution.py:29
  28.9 1.3 %select_reduce_fusion.2 = f32[512]{0:T(512)S(1)} fusion(f32[1,1,512,512]{3,2,1,0:T(8,128)} %param.6), kind=kLoop, calls=%fused_computation.27 | loop fusion | flops 785920 | bytes 1050624 | tf_op jit(solution)/shard_map/reduce_sum | solution.py:101
  30.1 5.9 %collective-permute-done.3 = f32[1,256,512]{2,1,0:T(8,128)} collective-permute-done((f32[1,256,512]{2,1,0:T(8,128)S(1)}, f32[1,256,512]{2,1,0:T(8,128)}, u32[]{:S(2)}, u32[]{:S(2)}) %collective-permute-start.3) | collective-permute-done | bytes 524320 | tf_op jit(solution)/shard_map/ppermute | solution.py:29
  36.0 1.1 %multiply_reduce_fusion.3 = (f32[512]{0:T(512)S(1)}, f32[256,512]{1,0:T(8,128)S(1)}) fusion(f32[1,256,512]{2,1,0:T(8,128)} %collective-permute-done.3, f32[2,256,512]{2,1,0:T(8,128)S(1)} %maximum_add_fusion), kind=kLoop, calls=%fused_computation.49 | loop fusion | flops 392704 | bytes 1574912 | tf_op jit(solution)/shard_map/reduce_sum | solution.py:39
  37.9 5.7 %all-to-all-start = ((f32[32,2,128]{2,1,0:T(2,128)}), f32[32,2,128]{2,1,0:T(2,128)S(1)}, u32[]{:S(2)}, u32[]{:S(2)}) async-start(f32[32,2,128]{2,1,0:T(2,128)} %broadcast_in_dim.52), calls=%async_computation | async-start | bytes 65536 | tf_op jit(solution)/shard_map/all_to_all | solution.py:35
  43.7 7.1 %all-to-all-done = f32[32,2,128]{2,1,0:T(2,128)S(1)} async-done(((f32[32,2,128]{2,1,0:T(2,128)}), f32[32,2,128]{2,1,0:T(2,128)S(1)}, u32[]{:S(2)}, u32[]{:S(2)}) %all-to-all-start) | async-done | bytes 32800 | tf_op jit(solution)/shard_map/all_to_all | solution.py:35
  52.8 3.3 %select_reduce_fusion.1 = (f32[]{:T(128)}, f32[]{:T(128)}, f32[512,512]{1,0:T(8,128)S(1)}) fusion(f32[256,512]{1,0:T(8,128)S(1)} %collective-permute-done.4, f32[256,512]{1,0:T(8,128)S(1)} %get-tuple-element.29, pred[]{:T(512)S(6)} %eq.38, f32[512,512]{1,0:T(8,128)} %collective-permute-done, f32[512,512]{1,0:T(8,128)S(1)} %collective-permute-done.1), kind=kOutput, calls=%fused_computation.26 | convolution fusion | flops 808189952 | bytes 4194313 | tf_op jit(solution)/shard_map/dot_general | solution.py:106
  56.1 4.7 %select_reduce_fusion = (f32[]{:T(128)}, f32[]{:T(128)}, f32[512,512]{1,0:T(8,128)}, f32[512,512]{1,0:T(8,128)S(1)}) fusion(f32[512,512]{1,0:T(8,128)S(1)} %get-tuple-element.35, pred[]{:T(512)S(6)} %eq.38, f32[256,512]{1,0:T(8,128)} %copy-done.7, f32[256,512]{1,0:T(8,128)S(1)} %get-tuple-element.29, f32[512,512]{1,0:T(8,128)S(1)} %collective-permute-done.1, ...), kind=kOutput, calls=%fused_computation.18 | convolution fusion | flops 808452096 | bytes 6291465 | tf_op jit(solution)/shard_map/dot_general | solution.py:107
  68.2 1.3 %broadcast_multiply_fusion = f32[512,512]{1,0:T(8,128)S(1)} fusion(f32[512,512]{1,0:T(8,128)} %copy-done.4, f32[]{:T(128)S(6)} %div.38), kind=kLoop, calls=%fused_computation.48 | loop fusion | flops 262144 | bytes 2097156 | tf_op jit(solution)/shard_map/mul | solution.py:46
  69.5 1.0 fusion.45
  71.8 1.3 %convolution_add_fusion = f32[512,512]{1,0:T(8,128)S(1)} fusion(f32[512,512]{1,0:T(8,128)S(1)} %fusion.11, f32[512,512]{1,0:T(8,128)S(1)} %copy-done.2, f32[512,512]{1,0:T(8,128)S(1)} %get-tuple-element.36, f32[]{:T(128)S(6)} %mul.514, f32[]{:T(128)S(6)} %mul.510, f32[]{:T(128)S(6)} %mul.506, f32[]{:T(128)S(6)} %mul.501, f32[]{:T(128)S(6)} %mul.494, ...), kind=kOutput, calls=%fused_computation.4 | convolution fusion | flops 809500672 | bytes 4194336 | tf_op jit(solution)/shard_map/dot_general | solution.py:68
  76.2 1.9 %collective-permute-start.8 = (f32[512,512]{1,0:T(8,128)}, f32[512,512]{1,0:T(8,128)S(1)}, u32[]{:S(2)}, u32[]{:S(2)}) collective-permute-start(f32[512,512]{1,0:T(8,128)} %get-tuple-element.30), channel_id=1, source_target_pairs={{0,0},{16,8},{8,16},{24,24},{1,1},{17,9},{9,17},{25,25},{2,2},{18,... | collective-permute-start | bytes 3145736 | tf_op jit(solution)/shard_map/ppermute | solution.py:108
  78.2 1.6 %collective-permute-start.6 = (f32[1,256,512]{2,1,0:T(8,128)S(1)}, f32[1,256,512]{2,1,0:T(8,128)S(1)}, u32[]{:S(2)}, u32[]{:S(2)}) collective-permute-start(f32[1,256,512]{2,1,0:T(8,128)S(1)} %bitcast.52), channel_id=1, source_target_pairs={{0,8},{8,0},{16,24},{24,16},{1,9},{9,1},{17,25},{25,17},{2,10},{10... | collective-permute-start | bytes 1572872 | tf_op jit(solution)/shard_map/ppermute | solution.py:29
  79.8 8.7 %collective-permute-done.5 = f32[1,256,512]{2,1,0:T(8,128)S(1)} collective-permute-done((f32[1,256,512]{2,1,0:T(8,128)S(1)}, f32[1,256,512]{2,1,0:T(8,128)S(1)}, u32[]{:S(2)}, u32[]{:S(2)}) %collective-permute-start.5) | collective-permute-done | bytes 524320 | tf_op jit(solution)/shard_map/ppermute | solution.py:29
  89.2 3.0 %all-to-all-start.1 = ((f32[32,1,128]{2,1,0:T(1,128)}), f32[32,1,128]{2,1,0:T(1,128)S(1)}, u32[]{:S(2)}, u32[]{:S(2)}) async-start(f32[32,1,128]{2,1,0:T(1,128)} %broadcast_in_dim.55), calls=%async_computation.1 | async-start | bytes 32768 | tf_op jit(solution)/shard_map/all_to_all | solution.py:35
  92.4 7.6 %all-to-all-done.1 = f32[32,1,128]{2,1,0:T(1,128)S(1)} async-done(((f32[32,1,128]{2,1,0:T(1,128)}), f32[32,1,128]{2,1,0:T(1,128)S(1)}, u32[]{:S(2)}, u32[]{:S(2)}) %all-to-all-start.1) | async-done | bytes 16416 | tf_op jit(solution)/shard_map/all_to_all | solution.py:35
  102.8 2.6 %pad_maximum_fusion = f32[4,256,512]{2,1,0:T(8,128)} fusion(f32[1,256,512]{2,1,0:T(8,128)} %collective-permute-done.7, f32[1,256,512]{2,1,0:T(8,128)S(1)} %collective-permute-done.6, f32[1,256,512]{2,1,0:T(8,128)S(1)} %collective-permute-done.5, f32[1,256,512]{2,1,0:T(8,128)S(1)} %bitcast.53), kind=kLoop, calls=%fused_computation.1 | loop fusion | flops 1572864 | bytes 4194304 | tf_op jit(solution)/shard_map/concatenate | solution.py:129
  105.5 2.3 %gather_fusion = f32[4,256,512]{2,1,0:T(8,128)S(1)} fusion(f32[4,256,512]{2,1,0:T(8,128)} %pad_maximum_fusion, s32[1024]{0:T(1024)S(1)} %pad_clamp_fusion), kind=kCustom, calls=%fused_computation | custom fusion | bytes 4194320 | tf_op jit(solution)/shard_map/jit(_take)/gather | solution.py:133
  107.8 1.6 %fusion = f32[1024,512]{1,0:T(8,128)} fusion(f32[4,256,512]{2,1,0:T(8,128)S(1)} %gather_fusion, f32[]{:T(128)S(6)} %sqrt.19, pred[1024]{0:T(1024)(128)(4,1)S(1)} %broadcast_in_dim.48), kind=kLoop, calls=%fused_computation.3 | loop fusion | flops 1048576 | bytes 4195332 | tf_op jit(solution)/shard_map/mul | solution.py:133
  (64 shorter events, 13.8 us)
Async XLA Ops:
  0.6 2.7 %copy-start = (bf16[256,1024]{1,0:T(8,128)(2,1)S(1)}, bf16[256,1024]{1,0:T(8,128)(2,1)}, u32[]{:S(2)}) copy-start(bf16[256,1024]{1,0:T(8,128)(2,1)} %param.4) | copy-start | bytes 1572868
  0.6 16.1 %copy-start.3 = (bf16[256,512]{1,0:T(8,128)(2,1)S(1)}, bf16[256,512]{1,0:T(8,128)(2,1)}, u32[]{:S(2)}) copy-start(bf16[256,512]{1,0:T(8,128)(2,1)} %param.5) | copy-start | bytes 786436
  6.8 10.4 %collective-permute-start.2 = (f32[2,256,512]{2,1,0:T(8,128)}, f32[2,256,512]{2,1,0:T(8,128)S(1)}, u32[]{:S(2)}, u32[]{:S(2)}) collective-permute-start(f32[2,256,512]{2,1,0:T(8,128)} %pad_maximum_fusion.1), channel_id=1, source_target_pairs={{0,8},{8,0},{16,24},{24,16},{1,9},{9,1},{17,25},{25,17},{2,10},{10... | collective-permute-start | bytes 3145736 | tf_op jit(solution)/shard_map/ppermute | solution.py:29
  7.3 10.3 %collective-permute-start = (f32[512,512]{1,0:T(8,128)}, f32[512,512]{1,0:T(8,128)}, u32[]{:S(2)}, u32[]{:S(2)}) collective-permute-start(f32[512,512]{1,0:T(8,128)} %bitcast.1), channel_id=1, source_target_pairs={{0,0},{8,16},{16,8},{24,24},{1,1},{9,17},{17,9},{25,25},{2,2},{10,... | collective-permute-start | bytes 3145736 | tf_op jit(solution)/shard_map/ppermute | solution.py:91
  17.5 26.1 %copy-start.9 = (s32[1,2]{1,0:T(1,128)S(1)}, s32[1,2]{1,0:T(1,128)}, u32[]{:S(2)}) copy-start(s32[1,2]{1,0:T(1,128)} %param.7) | copy-start | bytes 28
  17.6 18.5 %collective-permute-start.3 = (f32[1,256,512]{2,1,0:T(8,128)S(1)}, f32[1,256,512]{2,1,0:T(8,128)}, u32[]{:S(2)}, u32[]{:S(2)}) collective-permute-start(f32[1,256,512]{2,1,0:T(8,128)S(1)} %slice.29), channel_id=1, source_target_pairs={{0,16},{8,24},{16,0},{24,8},{1,17},{9,25},{17,1},{25,9},{2,18},{10... | collective-permute-start | bytes 1572872 | tf_op jit(solution)/shard_map/ppermute | solution.py:29
  17.6 35.1 %collective-permute-start.1 = (f32[512,512]{1,0:T(8,128)}, f32[512,512]{1,0:T(8,128)S(1)}, u32[]{:S(2)}, u32[]{:S(2)}) collective-permute-start(f32[512,512]{1,0:T(8,128)} %collective-permute-done), channel_id=1, source_target_pairs={{0,8},{8,0},{16,24},{24,16},{1,9},{9,1},{17,25},{25,17},{2,10},{10... | collective-permute-start | bytes 3145736 | tf_op jit(solution)/shard_map/ppermute | solution.py:29
  37.2 15.6 %collective-permute-start.4 = (f32[256,512]{1,0:T(8,128)S(1)}, f32[256,512]{1,0:T(8,128)S(1)}, u32[]{:S(2)}, u32[]{:S(2)}) collective-permute-start(f32[256,512]{1,0:T(8,128)S(1)} %get-tuple-element.29), channel_id=1, source_target_pairs={{0,8},{8,0},{16,24},{24,16},{1,9},{9,1},{17,25},{25,17},{2,10},{10... | collective-permute-start | bytes 1572872 | tf_op jit(solution)/shard_map/ppermute | solution.py:29
  37.9 12.9 %all-to-all-start = ((f32[32,2,128]{2,1,0:T(2,128)}), f32[32,2,128]{2,1,0:T(2,128)S(1)}, u32[]{:S(2)}, u32[]{:S(2)}) async-start(f32[32,2,128]{2,1,0:T(2,128)} %broadcast_in_dim.52), calls=%async_computation | async-start | bytes 65536 | tf_op jit(solution)/shard_map/all_to_all | solution.py:35
  52.8 3.4 %copy-start.7 = (f32[256,512]{1,0:T(8,128)}, f32[256,512]{1,0:T(8,128)S(1)}, u32[]{:S(2)}) copy-start(f32[256,512]{1,0:T(8,128)S(1)} %collective-permute-done.4) | copy-start | bytes 1572868
  56.1 4.7 %copy-start.4 = (f32[512,512]{1,0:T(8,128)}, f32[512,512]{1,0:T(8,128)S(1)}, u32[]{:S(2)}) copy-start(f32[512,512]{1,0:T(8,128)S(1)} %get-tuple-element.35) | copy-start | bytes 3145732
  66.1 1.0 copy-start.1
  70.5 1.2 %copy-start.2 = (f32[512,512]{1,0:T(8,128)S(1)}, f32[512,512]{1,0:T(8,128)}, u32[]{:S(2)}) copy-start(f32[512,512]{1,0:T(8,128)} %copy-done.1) | copy-start | bytes 3145732
  73.1 1.0 copy-start.8
  75.5 13.0 %collective-permute-start.5 = (f32[1,256,512]{2,1,0:T(8,128)S(1)}, f32[1,256,512]{2,1,0:T(8,128)S(1)}, u32[]{:S(2)}, u32[]{:S(2)}) collective-permute-start(f32[1,256,512]{2,1,0:T(8,128)S(1)} %bitcast.51), channel_id=1, source_target_pairs={{0,16},{8,24},{16,0},{24,8},{1,17},{9,25},{17,1},{25,9},{2,18},{10... | collective-permute-start | bytes 1572872 | tf_op jit(solution)/shard_map/ppermute | solution.py:29
  76.2 25.7 %collective-permute-start.8 = (f32[512,512]{1,0:T(8,128)}, f32[512,512]{1,0:T(8,128)S(1)}, u32[]{:S(2)}, u32[]{:S(2)}) collective-permute-start(f32[512,512]{1,0:T(8,128)} %get-tuple-element.30), channel_id=1, source_target_pairs={{0,0},{16,8},{8,16},{24,24},{1,1},{17,9},{9,17},{25,25},{2,2},{18,... | collective-permute-start | bytes 3145736 | tf_op jit(solution)/shard_map/ppermute | solution.py:108
  78.2 23.7 %collective-permute-start.6 = (f32[1,256,512]{2,1,0:T(8,128)S(1)}, f32[1,256,512]{2,1,0:T(8,128)S(1)}, u32[]{:S(2)}, u32[]{:S(2)}) collective-permute-start(f32[1,256,512]{2,1,0:T(8,128)S(1)} %bitcast.52), channel_id=1, source_target_pairs={{0,8},{8,0},{16,24},{24,16},{1,9},{9,1},{17,25},{25,17},{2,10},{10... | collective-permute-start | bytes 1572872 | tf_op jit(solution)/shard_map/ppermute | solution.py:29
  88.5 13.4 %collective-permute-start.7 = (f32[1,256,512]{2,1,0:T(8,128)S(1)}, f32[1,256,512]{2,1,0:T(8,128)}, u32[]{:S(2)}, u32[]{:S(2)}) collective-permute-start(f32[1,256,512]{2,1,0:T(8,128)S(1)} %collective-permute-done.5), channel_id=1, source_target_pairs={{0,8},{8,0},{16,24},{24,16},{1,9},{9,1},{17,25},{25,17},{2,10},{10... | collective-permute-start | bytes 1572872 | tf_op jit(solution)/shard_map/ppermute | solution.py:29
  89.2 10.7 %all-to-all-start.1 = ((f32[32,1,128]{2,1,0:T(1,128)}), f32[32,1,128]{2,1,0:T(1,128)S(1)}, u32[]{:S(2)}, u32[]{:S(2)}) async-start(f32[32,1,128]{2,1,0:T(1,128)} %broadcast_in_dim.55), calls=%async_computation.1 | async-start | bytes 32768 | tf_op jit(solution)/shard_map/all_to_all | solution.py:35
  101.9 1.0 copy-start.5
  107.7 1.6 %copy-start.6 = (f32[512,512]{1,0:T(8,128)S(1)}, f32[512,512]{1,0:T(8,128)}, u32[]{:S(2)}) copy-start(f32[512,512]{1,0:T(8,128)} %copy-done.5) | copy-start | bytes 3145732

commit v2 on v1

v2 whole, which is shorter than its diff:
```python
import functools
import math

import jax
import jax.numpy as jnp
from jax import lax
from jax.experimental import pallas as pl
from jax.experimental.pallas import tpu as pltpu
from jax.sharding import PartitionSpec as P

BLOCK = 512
HALF = BLOCK // 2
PACKED = HALF + 8

decay_rate = 0.95
damping = 0.25
epsilon = 1e-06
AXES = ("rep", "stripe")
f32 = jnp.float32
bf16 = jnp.bfloat16

ROOT_COEFFS = (
    25 / 16,
    -5 / 16 - 3125 / 4096,
    3125 / 4096,
    -1250 / 4096,
    250 / 4096,
    -25 / 4096,
    1 / 4096,
)

VMEM = pl.BlockSpec(memory_space=pltpu.VMEM)
SMEM = pl.BlockSpec(memory_space=pltpu.SMEM)
ANY = pl.BlockSpec(memory_space=pl.ANY)
LOW = pl.ds(0, HALF)
TOP = pl.ds(HALF, HALF)


def call(body, out_shapes, in_specs, scratch=(), limit=24, flops=0, out_specs=None, **kwargs):
    return pl.pallas_call(
        body,
        out_shape=[jax.ShapeDtypeStruct(s, f32) for s in out_shapes],
        in_specs=in_specs,
        out_specs=out_specs or [VMEM] * len(out_shapes),
        scratch_shapes=list(scratch),
        compiler_params=pltpu.CompilerParams(vmem_limit_bytes=limit << 20),
        cost_estimate=pl.CostEstimate(flops=flops, bytes_accessed=1 << 20, transcendentals=0),
        name=body.func.__name__ if isinstance(body, functools.partial) else body.__name__,
        **kwargs,
    )


def flip(x, mask):
    return lax.ppermute(x, "rep", [(i, i ^ mask) for i in range(lax.axis_size("rep"))])


def chip_core():
    me = lax.axis_index("rep")
    return lax.shift_right_logical(me, 1), lax.bitwise_and(me, 1)


def split(x):
    hi = x.astype(bf16)
    return hi, (x - hi.astype(f32)).astype(bf16)


def mm(a, b):
    return jnp.dot(a, b, preferred_element_type=f32)


def dot3(a, b):
    return mm(a[0], b[0]) + (mm(a[0], b[1]) + mm(a[1], b[0]))


def triangle():
    i = lax.broadcasted_iota(jnp.int32, (HALF, HALF), 0)
    j = lax.broadcasted_iota(jnp.int32, (HALF, HALF), 1)
    return i, j


def lanes(x):
    rows = jnp.sum(x, axis=0, keepdims=True)
    return sum(rows[:, k : k + 128] for k in range(0, x.shape[1], 128))


def pack_into(out, a, b, c):
    i, j = triangle()
    out[LOW, LOW] = jnp.where(i <= j, a, c)
    out[LOW, TOP] = b
    out[HALF:, LOW] = jnp.broadcast_to(jnp.sum(jnp.where(i == j, c, 0.0), axis=0, keepdims=True), (8, HALF))


def unpack(u, diag):
    i, j = triangle()
    ut = u.T
    return jnp.where(i <= j, u, ut), jnp.where(i > j, u, jnp.where(i < j, ut, diag))


def pack_stat(stat, out, trace):
    i, j = triangle()
    a, c = stat[LOW, LOW], stat[TOP, TOP]
    pack_into(out, a, stat[LOW, TOP], c)
    trace[...] = lanes(jnp.where(i == j, a + c, 0.0))


def grad_terms(pairs, acts, grads, owners, send, keep):
    chip, core = chip_core()
    cotangent = grads[...]
    for out, half in ((send, 1 - core), (keep, core)):
        for j in range(pairs):
            start = owners[0, chip ^ j] * BLOCK + half * HALF
            cols = acts[:, pl.ds(pl.multiple_of(start, HALF), HALF)]
            out[j] = lax.dot_general(cols, cotangent, (((0,), (0,)), ((), ())), preferred_element_type=f32)


def finish_half(devices, a, b, c, trace, half, sums):
    total = a[0] + b[0] + c[0]
    half[...] = total
    both = jnp.concatenate([lanes(total * total), trace[...]], axis=0)
    sums[...] = jnp.broadcast_to(both[None], (devices, 2, 128))


def update_stats(half, other, near, far, left, right, out, g, gt):
    _, core = chip_core()
    mine = pl.ds(pl.multiple_of(core * HALF, HALF), HALF)
    theirs = pl.ds(pl.multiple_of(HALF - core * HALF, HALF), HALF)
    for rows, src in ((mine, half), (theirs, other)):
        g[0, rows], g[1, rows] = split(src[...])
    for k in range(2):
        gt[k] = g[k].T
    for side, res, a, b in ((0, left, g, gt), (1, right, gt, g)):
        old = lambda r, c: jnp.where(core == side, far[r, c], near[r, c])
        a0 = (a[0, LOW], a[1, LOW])
        a1 = (a[0, TOP], a[1, TOP])
        top = dot3(a0, (b[0], b[1]))
        corner = dot3(a1, (b[0, :, TOP], b[1, :, TOP]))
        sa, sc = unpack(old(LOW, LOW), old(pl.ds(HALF, 1), LOW))
        res[LOW, LOW] = decay_rate * sa + top[:, :HALF]
        off = decay_rate * old(LOW, TOP) + top[:, HALF:]
        res[LOW, TOP] = off
        res[TOP, LOW] = off.T
        res[TOP, TOP] = decay_rate * sc + corner

    @pl.when(core == 1)
    def _():
        pack_into(out, left[LOW, LOW], left[LOW, TOP], left[TOP, TOP])

    @pl.when(core == 0)
    def _():
        pack_into(out, right[LOW, LOW], right[LOW, TOP], right[TOP, TOP])


def symmetric_product(a, b, out):
    top = dot3((a[0, LOW], a[1, LOW]), (b[0], b[1]))
    out[LOW] = top
    out[TOP, TOP] = dot3((a[0, TOP], a[1, TOP]), (b[0, :, TOP], b[1, :, TOP]))
    out[TOP, LOW] = top[:, HALF:].T


def stat_powers(left, right, left_t, right_t, facts, s1, s2):
    i, j = triangle()
    norms, traces = [], []
    for stat, t in ((left, left_t), (right, right_t)):
        x = stat[...]
        norm_sq = jnp.sum(jnp.sum(x * x, axis=0, keepdims=True), axis=1, keepdims=True)
        diag = jnp.where(i == j, stat[LOW, LOW] + stat[TOP, TOP], 0.0)
        norms.append(norm_sq)
        traces.append(jnp.sum(jnp.sum(diag, axis=0, keepdims=True), axis=1, keepdims=True))
        t1 = x * (1.0 / jnp.sqrt(norm_sq + epsilon))
        t[0] = t1
        s1[0], s1[1] = split(t1)
        symmetric_product(s1, s1, t.at[1])
        s2[0], s2[1] = split(t[1])
        symmetric_product(s1, s2, t.at[2])
    facts[...] = jnp.concatenate([jnp.broadcast_to(x, (1, 128)) for x in norms + traces], axis=0)


def precondition(devices, half, other, left_t, right_t, facts, sums, mine, spread, totals, g):
    _, core = chip_core()
    own = pl.ds(pl.multiple_of(core * HALF, HALF), HALF)
    theirs = pl.ds(pl.multiple_of(HALF - core * HALF, HALF), HALF)
    for rows, src in ((own, half), (theirs, other)):
        g[0, rows], g[1, rows] = split(src[...])
    both = jnp.sum(jnp.sum(sums[...], axis=0), axis=1, keepdims=True)
    grad_sq, trace = both[0:1], both[1:2]
    shift = (decay_rate * trace + 2.0 * grad_sq) * (damping / (devices * BLOCK))
    norm_sq, traces = facts[0:2, :], facts[2:4, :]
    shift = jnp.broadcast_to(shift, (2, 128))
    frob = jnp.sqrt(norm_sq + 2.0 * shift * traces + BLOCK * shift * shift + epsilon)
    a = jnp.sqrt(norm_sq + epsilon) / frob
    e = shift / frob
    outer = 1.0 / jnp.sqrt(jnp.sqrt(frob))
    k = []
    for i in range(7):
        total = jnp.full_like(e, ROOT_COEFFS[6] * math.comb(6, i))
        for j in range(5, i - 1, -1):
            total = total * e + math.comb(j, i) * ROOT_COEFFS[j]
        k.append(outer * total)
        outer = outer * a

    def inner(t, s):
        return k[4][s : s + 1, 0:1] * t[0] + k[5][s : s + 1, 0:1] * t[1] + k[6][s : s + 1, 0:1] * t[2]

    def outside(t, rows, start, s):
        i = lax.broadcasted_iota(jnp.int32, (HALF, BLOCK), 0) + start
        j = lax.broadcasted_iota(jnp.int32, (HALF, BLOCK), 1)
        lin = k[1][s : s + 1, 0:1] * t[0, rows] + k[2][s : s + 1, 0:1] * t[1, rows] + k[3][s : s + 1, 0:1] * t[2, rows]
        return lin + jnp.where(i == j, k[0][s : s + 1, 0:1], 0.0)

    left_rows = outside(left_t, own, core * HALF, 0) + dot3(split(left_t[2, own]), split(inner(left_t, 0)))
    y = dot3(split(left_rows), (g[0], g[1]))
    right_in = split(inner(right_t, 1))
    r0 = outside(right_t, LOW, 0, 1) + dot3(split(right_t[2, LOW]), right_in)
    r1 = outside(right_t, TOP, HALF, 1) + dot3(split(right_t[2, TOP]), right_in)
    z = dot3(split(y[:, :HALF]), split(r0)) + dot3(split(y[:, HALF:]), split(r1))
    mine[...] = z
    spread[...] = jnp.broadcast_to(lanes(z * z)[None], (devices, 1, 128))
    totals[...] = jnp.broadcast_to(grad_sq, (1, 128))


def unpack_stat(packed, out):
    sa, sc = unpack(packed[LOW, LOW], packed[HALF : HALF + 1, LOW])
    off = packed[LOW, TOP]
    out[LOW, LOW] = sa
    out[LOW, TOP] = off
    out[TOP, LOW] = off.T
    out[TOP, TOP] = sc


def place(pairs, *refs):
    direct, across = refs[:pairs], refs[pairs : 2 * pairs]
    sums, totals, owners, out, scaled, sems = refs[2 * pairs :]
    chip, core = chip_core()
    prec_sq = jnp.sum(jnp.sum(sums[...], axis=0), axis=1, keepdims=True)
    scale = jnp.sqrt(totals[0:1, 0:1] / (prec_sq + epsilon))
    copies = []
    for j in range(pairs):
        for half, src in ((core, direct[j]), (1 - core, across[j])):
            n = len(copies)
            scaled[n] = src[...] * scale
            start = pl.multiple_of(owners[0, chip ^ j] * BLOCK + half * HALF, HALF)
            copies.append(pltpu.make_async_copy(scaled.at[n], out.at[pl.ds(start, HALF)], sems.at[n]))
            copies[-1].start()
    for copy in copies:
        copy.wait()


def per_device(activations, out_grads, statistics, owner_blocks):
    rep_count = lax.axis_size("rep")
    pairs = rep_count // 2
    devices = rep_count * lax.axis_size("stripe")
    tokens = activations.shape[0]
    piece, square = (HALF, BLOCK), (BLOCK, BLOCK)
    unit = 6 * BLOCK**3

    shuffle = [(s * pairs + p, 2 * p + 1 - s) for s in range(2) for p in range(pairs)]
    send, keep = call(
        functools.partial(grad_terms, pairs),
        [(pairs,) + piece] * 2,
        [VMEM, VMEM, SMEM],
        flops=2 * tokens * pairs * BLOCK * BLOCK,
    )(activations, out_grads, owner_blocks)
    got = flip(send, 1)
    packed, trace = call(pack_stat, [(PACKED, BLOCK), (1, 128)], [VMEM])(statistics[0, 0])
    near = lax.ppermute(packed, "rep", shuffle)
    held = [(keep[j], got[j]) for j in range(pairs)]
    m = pairs // 2
    while m:
        arrived = [flip(sum(held[m + j]), 2 * m) for j in range(m)]
        held = [held[j] + (arrived[j],) for j in range(m)]
        m //= 2
    terms = held[0]
    a, b, c = terms[0], terms[1], sum(terms[2:])
    half, sums = call(
        functools.partial(finish_half, devices), [piece, (devices, 2, 128)], [VMEM] * 4
    )(a[None], b[None], c[None], trace)
    far = flip(near, 1)
    other = flip(half, 1)
    sums = lax.all_to_all(sums, AXES, 0, 0)
    left, right, out_packed = call(
        update_stats,
        [square, square, (PACKED, BLOCK)],
        [VMEM] * 4,
        [pltpu.VMEM((2,) + square, bf16)] * 2,
        flops=2 * unit,
    )(half, other, near, far)
    new_packed = lax.ppermute(out_packed, "rep", [(t, s) for s, t in shuffle])
    left_t, right_t, facts = call(
        stat_powers,
        [(3,) + square] * 2 + [(4, 128)],
        [VMEM] * 2,
        [pltpu.VMEM((2,) + square, bf16)] * 2,
        flops=4 * unit,
    )(left, right)
    mine, spread, totals = call(
        functools.partial(precondition, devices),
        [piece, (devices, 1, 128), (1, 128)],
        [VMEM] * 6,
        [pltpu.VMEM((2,) + square, bf16)],
        flops=3 * unit,
    )(half, other, left_t, right_t, facts, sums)

    direct, m = [mine], 1
    while m < pairs:
        direct = direct + [flip(x, 2 * m) for x in direct]
        m *= 2
    prec = lax.all_to_all(spread, AXES, 0, 0)
    across = [flip(x, 1) for x in direct]
    (new_stat,) = call(unpack_stat, [square], [VMEM])(new_packed)
    (placed,) = call(
        functools.partial(place, pairs),
        [(pairs * BLOCK, out_grads.shape[1])],
        [VMEM] * (2 * pairs + 2) + [SMEM],
        [pltpu.VMEM((2 * pairs,) + piece, f32), pltpu.SemaphoreType.DMA((2 * pairs,))],
        out_specs=[ANY],
    )(*direct, *across, prec, totals, owner_blocks)
    return placed, new_stat[None, None]


def solution(mesh):
    in_specs = (
        P("rep", None),
        P("rep", "stripe"),
        P("rep", "stripe", None, None),
        P("stripe", None),
    )
    out_specs = (P(None, "stripe"), P("rep", "stripe", None, None))
    return jax.shard_map(per_device, mesh=mesh, in_specs=in_specs, out_specs=out_specs, check_vma=False)
```

time: 112 us -> 79.2 us (0.71); the launches traced: 110 us -> 78.9 us
  matrix products: 18.6 us -> 0 us
  starting transfers between devices: 34 us -> 16.6 us
  Pallas kernels: 0 us -> 14 us
  other arithmetic: 10.2 us -> 0.19 us
  between operations: 9.14 us -> 0.73 us
  waiting for transfers between devices: 29.3 us -> 36.4 us
  local copies, waits for them, and re-layouts: 9.04 us -> 10.9 us
    dot_general x14 -> x0, matrix products: 18.6 us -> none  [the longest x1 4.73 us: per_device(): jnp.dot(grad.T, grad, precision=high)]
    pallas_call x0 -> x8, Pallas kernels: none -> 14 us  [the longest x1 3.62 us: per_device(): call(functools.partial(precondition, devices), [piece, (devices, 1, 128),...]
    ppermute x2, starting transfers between devices: 11.3 us -> 0.29 us  [the longest x1 0.26 us: per_device(): new_packed = lax.ppermute(out_packed, 'rep', [(t, s) for s, t in shuffle])]
    ppermute x2, waiting for transfers between devices: 0.01 us -> 10 us  [the longest x1 9.99 us: per_device(): near = lax.ppermute(packed, 'rep', shuffle)]
    all_to_all x2, waiting for transfers between devices: 14.6 us -> 5.89 us  [the longest x1 5.88 us: per_device(): prec = lax.all_to_all(spread, AXES, 0, 0)]
    ppermute x7, starting transfers between devices: 14 us -> 5.5 us  [flip(): lax.ppermute(x, 'rep', [(i, i ^ mask) for i in range(lax.axis_size('rep'))])]
    unnamed x21 -> x18, local copies, waits for them, and re-layouts: 3.32 us -> 10.9 us
    ppermute x7, waiting for transfers between devices: 14.6 us -> 20.5 us  [flip(): lax.ppermute(x, 'rep', [(i, i ^ mask) for i in range(lax.axis_size('rep'))])]
  transfers between devices with their start and end apart: 11 -> 11, of which waited for: 4 -> 5; matrix products, arithmetic and copies ran while one was open for 6% -> 0% of each run, Pallas kernels for 0% -> 9%
where the time goes in v2:
time: 79.2 us; the launch traced here: 78.9 us
  waiting for transfers between devices  36.4 us (46%)
  starting transfers between devices  16.6 us (21%)
  Pallas kernels  14 us (18%)
  local copies, waits for them, and re-layouts  10.9 us (14%)
    ppermute x7, waiting for transfers between devices, flip(): lax.ppermute(x, 'rep', [(i, i ^ mask) for i in range(lax.axis_size('rep'))])  20.5 us
    unnamed x18, local copies, waits for them, and re-layouts  10.9 us
    ppermute x1, waiting for transfers between devices, per_device(): near = lax.ppermute(packed, 'rep', shuffle)  9.99 us
    all_to_all x1, waiting for transfers between devices, per_device(): prec = lax.all_to_all(spread, AXES, 0, 0)  5.88 us
    all_to_all x1, starting transfers between devices, per_device(): sums = lax.all_to_all(sums, AXES, 0, 0)  5.72 us
    ppermute x7, starting transfers between devices, flip(): lax.ppermute(x, 'rep', [(i, i ^ mask) for i in range(lax.axis_size('rep'))])  5.5 us
    all_to_all x1, starting transfers between devices, per_device(): prec = lax.all_to_all(spread, AXES, 0, 0)  5.09 us
    pallas_call x1, Pallas kernels, per_device(): call(functools.partial(precondition, devices), [piece, (devices, 1, 128),...  3.62 us
  transfers between devices with their start and end apart: 11, of which 5 were waited for; matrix products, arithmetic and copies ran while one was open for 0% of the time, Pallas kernels for 9%

profile of v2, /device:TPU:0, one launch (start us, length us, event | category | flops | bytes accessed | tf_op | source)
XLA Modules:
  0.0 78.9 jit_solution(15861819509963334019)
XLA Ops:
  0.6 0.6 copy-done.1
  1.3 1.0 %copy-done.3 = bf16[256,1024]{1,0:T(8,128)(2,1)S(1)} copy-done((bf16[256,1024]{1,0:T(8,128)(2,1)S(1)}, bf16[256,1024]{1,0:T(8,128)(2,1)}, u32[]{:S(2)}) %copy-start.3) | copy-done | bytes 524312
  2.3 0.9 %copy-done.4 = bf16[256,512]{1,0:T(8,128)(2,1)S(1)} copy-done((bf16[256,512]{1,0:T(8,128)(2,1)S(1)}, bf16[256,512]{1,0:T(8,128)(2,1)}, u32[]{:S(2)}) %copy-start.4) | copy-done | bytes 262168
  3.3 1.0 %grad_terms.1 = (f32[2,256,512]{2,1,0:T(8,128)S(1)}, f32[2,256,512]{2,1,0:T(8,128)S(1)}) custom-call(bf16[256,1024]{1,0:T(8,128)(2,1)S(1)} %copy-done.3, bf16[256,512]{1,0:T(8,128)(2,1)S(1)} %copy-done.4, s32[1,2]{1,0:T(1,128)S(1)} %copy-done.1), custom_call_target="tpu_custom_call" | custom-call | flops 268435456 | bytes 1048576 | tf_op jit(solution)/shard_map/grad_terms/pallas_call | solution.py:257
  4.9 1.2 %copy-done = f32[1,1,512,512]{3,2,1,0:T(8,128)S(1)} copy-done((f32[1,1,512,512]{3,2,1,0:T(8,128)S(1)}, f32[1,1,512,512]{3,2,1,0:T(8,128)}, u32[]{:S(2)}) %copy-start) | copy-done | bytes 1048600
  6.2 1.0 %collective-permute-done = f32[2,256,512]{2,1,0:T(8,128)S(1)} collective-permute-done((f32[2,256,512]{2,1,0:T(8,128)S(1)}, f32[2,256,512]{2,1,0:T(8,128)S(1)}, u32[]{:S(2)}, u32[]{:S(2)}) %collective-permute-start) | collective-permute-done | bytes 1048608 | tf_op jit(solution)/shard_map/ppermute | solution.py:54
  7.4 2.9 %collective-permute-start.1 = (f32[256,512]{1,0:T(8,128)S(1)}, f32[256,512]{1,0:T(8,128)S(1)}, u32[]{:S(2)}, u32[]{:S(2)}) collective-permute-start(f32[256,512]{1,0:T(8,128)S(1)} %get-tuple-element.32), channel_id=1, source_target_pairs={{0,16},{8,24},{16,0},{24,8},{1,17},{9,25},{17,1},{25,9},{2,18},{10... | collective-permute-start | bytes 1572872 | tf_op jit(solution)/shard_map/ppermute | solution.py:54
  10.3 10.0 %collective-permute-done.3.near = f32[264,512]{1,0:T(8,128)S(1)} collective-permute-done((f32[264,512]{1,0:T(8,128)S(1)}, f32[264,512]{1,0:T(8,128)S(1)}, u32[]{:S(2)}, u32[]{:S(2)}) %collective-permute-start.3) | collective-permute-done | bytes 540704 | tf_op jit(solution)/shard_map/ppermute | solution.py:265
  20.3 7.0 %collective-permute-done.1 = f32[256,512]{1,0:T(8,128)S(1)} collective-permute-done((f32[256,512]{1,0:T(8,128)S(1)}, f32[256,512]{1,0:T(8,128)S(1)}, u32[]{:S(2)}, u32[]{:S(2)}) %collective-permute-start.1) | collective-permute-done | bytes 524320 | tf_op jit(solution)/shard_map/ppermute | solution.py:54
  27.2 0.8 finish_half.1
  28.0 5.7 %all-to-all-start = ((f32[32,2,128]{2,1,0:T(2,128)}), f32[32,2,128]{2,1,0:T(2,128)S(1)}, u32[]{:S(2)}, u32[]{:S(2)}) async-start(f32[32,2,128]{2,1,0:T(2,128)} %get-tuple-element.27), calls=%async_computation | async-start | bytes 65536 | tf_op jit(solution)/shard_map/all_to_all | solution.py:279
  33.8 1.8 %update_stats.1 = (f32[512,512]{1,0:T(8,128)S(1)}, f32[512,512]{1,0:T(8,128)S(1)}, f32[264,512]{1,0:T(8,128)S(1)}) custom-call(f32[256,512]{1,0:T(8,128)S(1)} %get-tuple-element.20.half, f32[256,512]{1,0:T(8,128)S(1)} %collective-permute-done.2.other, f32[264,512]{1,0:T(8,128)S(1)} %collective-permute-done.3.near, f32[264,512]{1,0:T(8,128)S(1)} %collective-permute-done.4.far), custom_call_target="tpu_custom_call" | custom-call | flops 1610612736 | bytes 1048576 | tf_op jit(solution)/shard_map/update_stats/pallas_call | solution.py:280
  35.6 3.5 %stat_powers.1 = (f32[3,512,512]{2,1,0:T(8,128)S(1)}, f32[3,512,512]{2,1,0:T(8,128)S(1)}, f32[4,128]{1,0:T(4,128)S(1)}) custom-call(f32[512,512]{1,0:T(8,128)S(1)} %get-tuple-element.22.left, f32[512,512]{1,0:T(8,128)S(1)} %get-tuple-element.23.right), custom_call_target="tpu_custom_call" | custom-call | flops 3221225472 | bytes 1048576 | tf_op jit(solution)/shard_map/stat_powers/pallas_call | solution.py:288
  39.1 1.6 %copy-done.5 = f32[3,512,512]{2,1,0:T(8,128)} copy-done((f32[3,512,512]{2,1,0:T(8,128)}, f32[3,512,512]{2,1,0:T(8,128)S(1)}, u32[]{:S(2)}) %copy-start.5) | copy-done | bytes 3145752
  40.7 1.7 %copy-done.7 = f32[3,512,512]{2,1,0:T(8,128)} copy-done((f32[3,512,512]{2,1,0:T(8,128)}, f32[3,512,512]{2,1,0:T(8,128)S(1)}, u32[]{:S(2)}) %copy-start.7) | copy-done | bytes 3145752
  42.4 1.9 %copy-done.6 = f32[3,512,512]{2,1,0:T(8,128)S(1)} copy-done((f32[3,512,512]{2,1,0:T(8,128)S(1)}, f32[3,512,512]{2,1,0:T(8,128)}, u32[]{:S(2)}) %copy-start.6) | copy-done | bytes 3145752
  44.3 1.9 %copy-done.8 = f32[3,512,512]{2,1,0:T(8,128)S(1)} copy-done((f32[3,512,512]{2,1,0:T(8,128)S(1)}, f32[3,512,512]{2,1,0:T(8,128)}, u32[]{:S(2)}) %copy-start.8) | copy-done | bytes 3145752
  46.1 3.6 %precondition.1 = (f32[256,512]{1,0:T(8,128)S(1)}, f32[32,1,128]{2,1,0:T(1,128)}, f32[1,128]{1,0:T(1,128)S(1)}) custom-call(f32[256,512]{1,0:T(8,128)S(1)} %get-tuple-element.20.half, f32[256,512]{1,0:T(8,128)S(1)} %collective-permute-done.2.other, f32[3,512,512]{2,1,0:T(8,128)S(1)} %copy-done.6, f32[3,512,512]{2,1,0:T(8,128)S(1)} %copy-done.8, ...), custom_call_target="tpu_custom_call" | custom-call | flops 2415919104 | bytes 1048576 | tf_op jit(solution)/shard_map/precondition/pallas_call | solution.py:295
  49.8 1.8 %collective-permute-start.5 = (f32[256,512]{1,0:T(8,128)S(1)}, f32[256,512]{1,0:T(8,128)S(1)}, u32[]{:S(2)}, u32[]{:S(2)}) collective-permute-start(f32[256,512]{1,0:T(8,128)S(1)} %get-tuple-element.28.refs_0_), channel_id=1, source_target_pairs={{0,16},{8,24},{16,0},{24,8},{1,17},{9,25},{17,1},{25,9},{2,18},{10... | collective-permute-start | bytes 1572872 | tf_op jit(solution)/shard_map/ppermute | solution.py:54
  52.0 12.5 %collective-permute-done.5.refs_1_ = f32[256,512]{1,0:T(8,128)S(1)} collective-permute-done((f32[256,512]{1,0:T(8,128)S(1)}, f32[256,512]{1,0:T(8,128)S(1)}, u32[]{:S(2)}, u32[]{:S(2)}) %collective-permute-start.5) | collective-permute-done | bytes 524320 | tf_op jit(solution)/shard_map/ppermute | solution.py:54
  64.6 5.1 %all-to-all-start.1 = ((f32[32,1,128]{2,1,0:T(1,128)}), f32[32,1,128]{2,1,0:T(1,128)S(1)}, u32[]{:S(2)}, u32[]{:S(2)}) async-start(f32[32,1,128]{2,1,0:T(1,128)} %get-tuple-element.29), calls=%async_computation.1 | async-start | bytes 32768 | tf_op jit(solution)/shard_map/all_to_all | solution.py:307
  69.7 1.2 %unpack_stat.1 = f32[512,512]{1,0:T(8,128)} custom-call(f32[264,512]{1,0:T(8,128)S(1)} %collective-permute-done.8.packed), custom_call_target="tpu_custom_call" | custom-call | bytes 1048576 | tf_op jit(solution)/shard_map/unpack_stat/pallas_call | solution.py:309
  70.9 5.9 %all-to-all-done.1.refs_4_ = f32[32,1,128]{2,1,0:T(1,128)S(1)} async-done(((f32[32,1,128]{2,1,0:T(1,128)}), f32[32,1,128]{2,1,0:T(1,128)S(1)}, u32[]{:S(2)}, u32[]{:S(2)}) %all-to-all-start.1) | async-done | bytes 16416 | tf_op jit(solution)/shard_map/all_to_all | solution.py:307
  76.8 2.1 %place.1 = f32[1024,512]{1,0:T(8,128)} custom-call(f32[256,512]{1,0:T(8,128)S(1)} %get-tuple-element.28.refs_0_, f32[256,512]{1,0:T(8,128)S(1)} %collective-permute-done.5.refs_1_, f32[256,512]{1,0:T(8,128)S(1)} %collective-permute-done.6.refs_2_, f32[256,512]{1,0:T(8,128)S(1)} %collective-permute-done.7.refs_3_, f32[32,1,128]{2,1,0:T(1,128)S(1)} %all-to-all-done.1.refs_4_, ...), custom_call_target="tpu_custom_call" | custom-call | bytes 1048576 | tf_op jit(solution)/shard_map/place/pallas_call | solution.py:310
  (25 shorter events, 1.4 us)
Async XLA Ops:
  0.6 0.7 copy-start.1
  1.3 1.0 %copy-start.3 = (bf16[256,1024]{1,0:T(8,128)(2,1)S(1)}, bf16[256,1024]{1,0:T(8,128)(2,1)}, u32[]{:S(2)}) copy-start(bf16[256,1024]{1,0:T(8,128)(2,1)} %acts.1) | copy-start | bytes 1572868
  2.3 0.9 %copy-start.4 = (bf16[256,512]{1,0:T(8,128)(2,1)S(1)}, bf16[256,512]{1,0:T(8,128)(2,1)}, u32[]{:S(2)}) copy-start(bf16[256,512]{1,0:T(8,128)(2,1)} %grads.1) | copy-start | bytes 786436
  4.3 2.8 %collective-permute-start = (f32[2,256,512]{2,1,0:T(8,128)S(1)}, f32[2,256,512]{2,1,0:T(8,128)S(1)}, u32[]{:S(2)}, u32[]{:S(2)}) collective-permute-start(f32[2,256,512]{2,1,0:T(8,128)S(1)} %get-tuple-element.18), channel_id=1, source_target_pairs={{0,8},{8,0},{16,24},{24,16},{1,9},{9,1},{17,25},{25,17},{2,10},{10... | collective-permute-start | bytes 3145736 | tf_op jit(solution)/shard_map/ppermute | solution.py:54
  4.9 1.2 %copy-start = (f32[1,1,512,512]{3,2,1,0:T(8,128)S(1)}, f32[1,1,512,512]{3,2,1,0:T(8,128)}, u32[]{:S(2)}) copy-start(f32[1,1,512,512]{3,2,1,0:T(8,128)} %param.6) | copy-start | bytes 3145732
  6.2 14.1 %collective-permute-start.3 = (f32[264,512]{1,0:T(8,128)S(1)}, f32[264,512]{1,0:T(8,128)S(1)}, u32[]{:S(2)}, u32[]{:S(2)}) collective-permute-start(f32[264,512]{1,0:T(8,128)S(1)} %get-tuple-element.21), channel_id=1, source_target_pairs={{0,8},{8,24},{16,0},{24,16},{1,9},{9,25},{17,1},{25,17},{2,10},{10... | collective-permute-start | bytes 1622024 | tf_op jit(solution)/shard_map/ppermute | solution.py:265
  7.4 19.9 %collective-permute-start.1 = (f32[256,512]{1,0:T(8,128)S(1)}, f32[256,512]{1,0:T(8,128)S(1)}, u32[]{:S(2)}, u32[]{:S(2)}) collective-permute-start(f32[256,512]{1,0:T(8,128)S(1)} %get-tuple-element.32), channel_id=1, source_target_pairs={{0,16},{8,24},{16,0},{24,8},{1,17},{9,25},{17,1},{25,9},{2,18},{10... | collective-permute-start | bytes 1572872 | tf_op jit(solution)/shard_map/ppermute | solution.py:54
  20.3 13.5 %collective-permute-start.4 = (f32[264,512]{1,0:T(8,128)S(1)}, f32[264,512]{1,0:T(8,128)S(1)}, u32[]{:S(2)}, u32[]{:S(2)}) collective-permute-start(f32[264,512]{1,0:T(8,128)S(1)} %collective-permute-done.3.near), channel_id=1, source_target_pairs={{0,8},{8,0},{16,24},{24,16},{1,9},{9,1},{17,25},{25,17},{2,10},{10... | collective-permute-start | bytes 1622024 | tf_op jit(solution)/shard_map/ppermute | solution.py:54
  28.0 5.7 %collective-permute-start.2 = (f32[256,512]{1,0:T(8,128)S(1)}, f32[256,512]{1,0:T(8,128)S(1)}, u32[]{:S(2)}, u32[]{:S(2)}) collective-permute-start(f32[256,512]{1,0:T(8,128)S(1)} %get-tuple-element.20.half), channel_id=1, source_target_pairs={{0,8},{8,0},{16,24},{24,16},{1,9},{9,1},{17,25},{25,17},{2,10},{10... | collective-permute-start | bytes 1572872 | tf_op jit(solution)/shard_map/ppermute | solution.py:54
  28.0 14.3 %all-to-all-start = ((f32[32,2,128]{2,1,0:T(2,128)}), f32[32,2,128]{2,1,0:T(2,128)S(1)}, u32[]{:S(2)}, u32[]{:S(2)}) async-start(f32[32,2,128]{2,1,0:T(2,128)} %get-tuple-element.27), calls=%async_computation | async-start | bytes 65536 | tf_op jit(solution)/shard_map/all_to_all | solution.py:279
  39.1 1.6 %copy-start.5 = (f32[3,512,512]{2,1,0:T(8,128)}, f32[3,512,512]{2,1,0:T(8,128)S(1)}, u32[]{:S(2)}) copy-start(f32[3,512,512]{2,1,0:T(8,128)S(1)} %get-tuple-element.24.left_t) | copy-start | bytes 9437188
  40.7 1.7 %copy-start.7 = (f32[3,512,512]{2,1,0:T(8,128)}, f32[3,512,512]{2,1,0:T(8,128)S(1)}, u32[]{:S(2)}) copy-start(f32[3,512,512]{2,1,0:T(8,128)S(1)} %get-tuple-element.25.right_t) | copy-start | bytes 9437188
  42.4 1.9 %copy-start.6 = (f32[3,512,512]{2,1,0:T(8,128)S(1)}, f32[3,512,512]{2,1,0:T(8,128)}, u32[]{:S(2)}) copy-start(f32[3,512,512]{2,1,0:T(8,128)} %copy-done.5) | copy-start | bytes 9437188
  44.3 1.9 %copy-start.8 = (f32[3,512,512]{2,1,0:T(8,128)S(1)}, f32[3,512,512]{2,1,0:T(8,128)}, u32[]{:S(2)}) copy-start(f32[3,512,512]{2,1,0:T(8,128)} %copy-done.7) | copy-start | bytes 9437188
  46.1 30.6 %copy-start.2 = (s32[1,2]{1,0:T(1,128)S(1)}, s32[1,2]{1,0:T(1,128)}, u32[]{:S(2)}) copy-start(s32[1,2]{1,0:T(1,128)} %refs_6_.1) | copy-start | bytes 28
  49.8 14.8 %collective-permute-start.5 = (f32[256,512]{1,0:T(8,128)S(1)}, f32[256,512]{1,0:T(8,128)S(1)}, u32[]{:S(2)}, u32[]{:S(2)}) collective-permute-start(f32[256,512]{1,0:T(8,128)S(1)} %get-tuple-element.28.refs_0_), channel_id=1, source_target_pairs={{0,16},{8,24},{16,0},{24,8},{1,17},{9,25},{17,1},{25,9},{2,18},{10... | collective-permute-start | bytes 1572872 | tf_op jit(solution)/shard_map/ppermute | solution.py:54
  51.5 18.1 %collective-permute-start.8 = (f32[264,512]{1,0:T(8,128)S(1)}, f32[264,512]{1,0:T(8,128)S(1)}, u32[]{:S(2)}, u32[]{:S(2)}) collective-permute-start(f32[264,512]{1,0:T(8,128)S(1)} %get-tuple-element.31), channel_id=1, source_target_pairs={{8,0},{24,8},{0,16},{16,24},{9,1},{25,9},{1,17},{17,25},{10,2},{26... | collective-permute-start | bytes 1622024 | tf_op jit(solution)/shard_map/ppermute | solution.py:287
  51.8 24.9 %collective-permute-start.6 = (f32[256,512]{1,0:T(8,128)S(1)}, f32[256,512]{1,0:T(8,128)S(1)}, u32[]{:S(2)}, u32[]{:S(2)}) collective-permute-start(f32[256,512]{1,0:T(8,128)S(1)} %get-tuple-element.28.refs_0_), channel_id=1, source_target_pairs={{0,8},{8,0},{16,24},{24,16},{1,9},{9,1},{17,25},{25,17},{2,10},{10... | collective-permute-start | bytes 1572872 | tf_op jit(solution)/shard_map/ppermute | solution.py:54
  64.6 12.2 %collective-permute-start.7 = (f32[256,512]{1,0:T(8,128)S(1)}, f32[256,512]{1,0:T(8,128)S(1)}, u32[]{:S(2)}, u32[]{:S(2)}) collective-permute-start(f32[256,512]{1,0:T(8,128)S(1)} %collective-permute-done.5.refs_1_), channel_id=1, source_target_pairs={{0,8},{8,0},{16,24},{24,16},{1,9},{9,1},{17,25},{25,17},{2,10},{10... | collective-permute-start | bytes 1572872 | tf_op jit(solution)/shard_map/ppermute | solution.py:54
  64.6 12.2 %all-to-all-start.1 = ((f32[32,1,128]{2,1,0:T(1,128)}), f32[32,1,128]{2,1,0:T(1,128)S(1)}, u32[]{:S(2)}, u32[]{:S(2)}) async-start(f32[32,1,128]{2,1,0:T(1,128)} %get-tuple-element.29), calls=%async_computation.1 | async-start | bytes 32768 | tf_op jit(solution)/shard_map/all_to_all | solution.py:307

commit v3 on v2

--- a/solution.py
+++ b/solution.py
@@ -7,6 +7,7 @@
 from jax.experimental import pallas as pl
 from jax.experimental.pallas import tpu as pltpu
 from jax.sharding import PartitionSpec as P
+
 
 BLOCK = 512
 HALF = BLOCK // 2
@@ -31,7 +32,7 @@
 
 VMEM = pl.BlockSpec(memory_space=pltpu.VMEM)
 SMEM = pl.BlockSpec(memory_space=pltpu.SMEM)
-ANY = pl.BlockSpec(memory_space=pl.ANY)
+HBM = pl.BlockSpec(memory_space=pltpu.HBM)
 LOW = pl.ds(0, HALF)
 TOP = pl.ds(HALF, HALF)
 
@@ -39,19 +40,22 @@
 def call(body, out_shapes, in_specs, scratch=(), limit=24, flops=0, out_specs=None, **kwargs):
     return pl.pallas_call(
         body,
-        out_shape=[jax.ShapeDtypeStruct(s, f32) for s in out_shapes],
+        out_shape=[s if isinstance(s, pl.MemoryRef) else jax.ShapeDtypeStruct(s, f32) for s in out_shapes],
         in_specs=in_specs,
         out_specs=out_specs or [VMEM] * len(out_shapes),
         scratch_shapes=list(scratch),
         compiler_params=pltpu.CompilerParams(vmem_limit_bytes=limit << 20),
         cost_estimate=pl.CostEstimate(flops=flops, bytes_accessed=1 << 20, transcendentals=0),
-        name=body.func.__name__ if isinstance(body, functools.partial) else body.__name__,
         **kwargs,
     )
 
 
 def flip(x, mask):
     return lax.ppermute(x, "rep", [(i, i ^ mask) for i in range(lax.axis_size("rep"))])
+
+
+def in_hbm(x):
+    return pltpu.with_memory_space_constraint(x, pltpu.HBM)
 
 
 def chip_core():
@@ -96,25 +100,31 @@
     return jnp.where(i <= j, u, ut), jnp.where(i > j, u, jnp.where(i < j, ut, diag))
 
 
-def pack_stat(stat, out, trace):
+def open_step(pairs, acts, grads, stat, owners, send, keep, out, trace, av, gv, sv, ov, sems):
+    chip, core = chip_core()
+    copies = [
+        pltpu.make_async_copy(src, dst, sems.at[k])
+        for k, (src, dst) in enumerate(((owners, ov), (acts, av), (grads, gv), (stat, sv)))
+    ]
+    for copy in copies:
+        copy.start()
+    for copy in copies[:3]:
+        copy.wait()
+    cotangent = gv[...]
+    for res, half in ((send, 1 - core), (keep, core)):
+        for j in range(pairs):
+            start = ov[0, chip ^ j] * BLOCK + half * HALF
+            cols = av[:, pl.ds(pl.multiple_of(start, HALF), HALF)]
+            res[j] = lax.dot_general(cols, cotangent, (((0,), (0,)), ((), ())), preferred_element_type=f32)
+    copies[3].wait()
     i, j = triangle()
-    a, c = stat[LOW, LOW], stat[TOP, TOP]
-    pack_into(out, a, stat[LOW, TOP], c)
+    a, c = sv[LOW, LOW], sv[TOP, TOP]
+    pack_into(out, a, sv[LOW, TOP], c)
     trace[...] = lanes(jnp.where(i == j, a + c, 0.0))
 
 
-def grad_terms(pairs, acts, grads, owners, send, keep):
-    chip, core = chip_core()
-    cotangent = grads[...]
-    for out, half in ((send, 1 - core), (keep, core)):
-        for j in range(pairs):
-            start = owners[0, chip ^ j] * BLOCK + half * HALF
-            cols = acts[:, pl.ds(pl.multiple_of(start, HALF), HALF)]
-            out[j] = lax.dot_general(cols, cotangent, (((0,), (0,)), ((), ())), preferred_element_type=f32)
-
-
-def finish_half(devices, a, b, c, trace, half, sums):
-    total = a[0] + b[0] + c[0]
+def finish_half(devices, keep, got, rest, trace, half, sums):
+    total = keep[0] + got[0] + rest[...]
     half[...] = total
     both = jnp.concatenate([lanes(total * total), trace[...]], axis=0)
     sums[...] = jnp.broadcast_to(both[None], (devices, 2, 128))
@@ -157,10 +167,15 @@
     out[TOP, LOW] = top[:, HALF:].T
 
 
-def stat_powers(left, right, left_t, right_t, facts, s1, s2):
+def stat_powers(left, right, left_out, right_out, facts, left_t, right_t, s1, s2, sems):
     i, j = triangle()
-    norms, traces = [], []
-    for stat, t in ((left, left_t), (right, right_t)):
+    norms, traces, copies = [], [], []
+
+    def keep(t, k, dst):
+        copies.append(pltpu.make_async_copy(t.at[k], dst.at[k], sems.at[len(copies)]))
+        copies[-1].start()
+
+    for stat, t, dst in ((left, left_t, left_out), (right, right_t, right_out)):
         x = stat[...]
         norm_sq = jnp.sum(jnp.sum(x * x, axis=0, keepdims=True), axis=1, keepdims=True)
         diag = jnp.where(i == j, stat[LOW, LOW] + stat[TOP, TOP], 0.0)
@@ -168,15 +183,27 @@
         traces.append(jnp.sum(jnp.sum(diag, axis=0, keepdims=True), axis=1, keepdims=True))
         t1 = x * (1.0 / jnp.sqrt(norm_sq + epsilon))
         t[0] = t1
+        keep(t, 0, dst)
         s1[0], s1[1] = split(t1)
         symmetric_product(s1, s1, t.at[1])
+        keep(t, 1, dst)
         s2[0], s2[1] = split(t[1])
         symmetric_product(s1, s2, t.at[2])
+        keep(t, 2, dst)
     facts[...] = jnp.concatenate([jnp.broadcast_to(x, (1, 128)) for x in norms + traces], axis=0)
-
-
-def precondition(devices, half, other, left_t, right_t, facts, sums, mine, spread, totals, g):
+    for copy in copies:
+        copy.wait()
+
+
+def precondition(devices, half, other, left_in, right_in_hbm, facts, sums, mine, spread, totals, g, left_t, right_t, sems):
     _, core = chip_core()
+    copies = [
+        pltpu.make_async_copy(src.at[k], dst.at[k], sems.at[3 * n + k])
+        for n, (src, dst) in enumerate(((left_in, left_t), (right_in_hbm, right_t)))
+        for k in range(3)
+    ]
+    for copy in copies:
+        copy.start()
     own = pl.ds(pl.multiple_of(core * HALF, HALF), HALF)
     theirs = pl.ds(pl.multiple_of(HALF - core * HALF, HALF), HALF)
     for rows, src in ((own, half), (theirs, other)):
@@ -207,8 +234,12 @@
         lin = k[1][s : s + 1, 0:1] * t[0, rows] + k[2][s : s + 1, 0:1] * t[1, rows] + k[3][s : s + 1, 0:1] * t[2, rows]
         return lin + jnp.where(i == j, k[0][s : s + 1, 0:1], 0.0)
 
+    for copy in copies[:3]:
+        copy.wait()
     left_rows = outside(left_t, own, core * HALF, 0) + dot3(split(left_t[2, own]), split(inner(left_t, 0)))
     y = dot3(split(left_rows), (g[0], g[1]))
+    for copy in copies[3:]:
+        copy.wait()
     right_in = split(inner(right_t, 1))
     r0 = outside(right_t, LOW, 0, 1) + dot3(split(right_t[2, LOW]), right_in)
     r1 = outside(right_t, TOP, HALF, 1) + dot3(split(right_t[2, TOP]), right_in)
@@ -227,22 +258,32 @@
     out[TOP, TOP] = sc
 
 
-def place(pairs, *refs):
-    direct, across = refs[:pairs], refs[pairs : 2 * pairs]
-    sums, totals, owners, out, scaled, sems = refs[2 * pairs :]
+def write_pieces(chip, core, pieces, scale, owners, out, scaled, sems):
+    copies = []
+    for n, (j, swapped, src) in enumerate(pieces):
+        scaled[n] = src[...] * scale
+        half = 1 - core if swapped else core
+        start = pl.multiple_of(owners[0, chip ^ j] * BLOCK + half * HALF, HALF)
+        copies.append(pltpu.make_async_copy(scaled.at[n], out.at[pl.ds(start, HALF)], sems.at[n]))
+        copies[-1].start()
+    for copy in copies:
+        copy.wait()
+
+
+def place_near(direct, across, sums, totals, owners, out, scale, scaled, sems):
     chip, core = chip_core()
     prec_sq = jnp.sum(jnp.sum(sums[...], axis=0), axis=1, keepdims=True)
-    scale = jnp.sqrt(totals[0:1, 0:1] / (prec_sq + epsilon))
-    copies = []
-    for j in range(pairs):
-        for half, src in ((core, direct[j]), (1 - core, across[j])):
-            n = len(copies)
-            scaled[n] = src[...] * scale
-            start = pl.multiple_of(owners[0, chip ^ j] * BLOCK + half * HALF, HALF)
-            copies.append(pltpu.make_async_copy(scaled.at[n], out.at[pl.ds(start, HALF)], sems.at[n]))
-            copies[-1].start()
-    for copy in copies:
-        copy.wait()
+    factor = jnp.sqrt(totals[0:1, 0:1] / (prec_sq + epsilon))
+    scale[...] = jnp.broadcast_to(factor, (1, 128))
+    write_pieces(chip, core, ((0, False, direct), (0, True, across)), factor, owners, out, scaled, sems)
+
+
+def place_far(count, *refs):
+    direct, across = refs[:count], refs[count : 2 * count]
+    scale, owners, _, out, scaled, sems = refs[2 * count :]
+    chip, core = chip_core()
+    pieces = [(j + 1, False, x) for j, x in enumerate(direct)] + [(j + 1, True, x) for j, x in enumerate(across)]
+    write_pieces(chip, core, pieces, scale[0:1, 0:1], owners, out, scaled, sems)
 
 
 def per_device(activations, out_grads, statistics, owner_blocks):
@@ -254,26 +295,32 @@
     unit = 6 * BLOCK**3
 
     shuffle = [(s * pairs + p, 2 * p + 1 - s) for s in range(2) for p in range(pairs)]
-    send, keep = call(
-        functools.partial(grad_terms, pairs),
-        [(pairs,) + piece] * 2,
-        [VMEM, VMEM, SMEM],
+    send, keep, packed, trace = call(
+        functools.partial(open_step, pairs),
+        [(pairs,) + piece] * 2 + [(PACKED, BLOCK), (1, 128)],
+        [HBM] * 4,
+        [
+            pltpu.VMEM(activations.shape, bf16),
+            pltpu.VMEM(out_grads.shape, bf16),
+            pltpu.VMEM(square, f32),
+            pltpu.SMEM(owner_blocks.shape, jnp.int32),
+            pltpu.SemaphoreType.DMA((4,)),
+        ],
         flops=2 * tokens * pairs * BLOCK * BLOCK,
-    )(activations, out_grads, owner_blocks)
+    )(*(in_hbm(x) for x in (activations, out_grads, statistics[0, 0], owner_blocks)))
     got = flip(send, 1)
-    packed, trace = call(pack_stat, [(PACKED, BLOCK), (1, 128)], [VMEM])(statistics[0, 0])
     near = lax.ppermute(packed, "rep", shuffle)
-    held = [(keep[j], got[j]) for j in range(pairs)]
     m = pairs // 2
+    held = [None] * pairs
     while m:
-        arrived = [flip(sum(held[m + j]), 2 * m) for j in range(m)]
-        held = [held[j] + (arrived[j],) for j in range(m)]
+        outgoing = [keep[m + j] + got[m + j] for j in range(m)]
+        outgoing = [x if held[m + j] is None else x + held[m + j] for j, x in enumerate(outgoing)]
+        arrived = [flip(x, 2 * m) for x in outgoing]
+        held = [x if held[j] is None else x + held[j] for j, x in enumerate(arrived)]
         m //= 2
-    terms = held[0]
-    a, b, c = terms[0], terms[1], sum(terms[2:])
     half, sums = call(
         functools.partial(finish_half, devices), [piece, (devices, 2, 128)], [VMEM] * 4
-    )(a[None], b[None], c[None], trace)
+    )(keep, got, held[0], trace)
     far = flip(near, 1)
     other = flip(half, 1)
     sums = lax.all_to_all(sums, AXES, 0, 0)
@@ -287,33 +334,45 @@
     new_packed = lax.ppermute(out_packed, "rep", [(t, s) for s, t in shuffle])
     left_t, right_t, facts = call(
         stat_powers,
-        [(3,) + square] * 2 + [(4, 128)],
+        [pltpu.HBM((3,) + square, f32)] * 2 + [(4, 128)],
         [VMEM] * 2,
-        [pltpu.VMEM((2,) + square, bf16)] * 2,
+        [pltpu.VMEM((3,) + square, f32)] * 2 + [pltpu.VMEM((2,) + square, bf16)] * 2 + [pltpu.SemaphoreType.DMA((6,))],
         flops=4 * unit,
+        out_specs=[HBM, HBM, VMEM],
     )(left, right)
     mine, spread, totals = call(
         functools.partial(precondition, devices),
         [piece, (devices, 1, 128), (1, 128)],
-        [VMEM] * 6,
-        [pltpu.VMEM((2,) + square, bf16)],
+        [VMEM, VMEM, HBM, HBM, VMEM, VMEM],
+        [pltpu.VMEM((2,) + square, bf16)] + [pltpu.VMEM((3,) + square, f32)] * 2 + [pltpu.SemaphoreType.DMA((6,))],
         flops=3 * unit,
-    )(half, other, left_t, right_t, facts, sums)
+    )(half, other, in_hbm(left_t), in_hbm(right_t), facts, sums)
 
     direct, m = [mine], 1
     while m < pairs:
         direct = direct + [flip(x, 2 * m) for x in direct]
         m *= 2
+    across = [flip(mine, 1)]
     prec = lax.all_to_all(spread, AXES, 0, 0)
-    across = [flip(x, 1) for x in direct]
     (new_stat,) = call(unpack_stat, [square], [VMEM])(new_packed)
+    slab = (pairs * BLOCK, out_grads.shape[1])
+    placed, scale = call(
+        place_near,
+        [slab, (1, 128)],
+        [VMEM] * 4 + [SMEM],
+        [pltpu.VMEM((2,) + piece, f32), pltpu.SemaphoreType.DMA((2,))],
+        out_specs=[HBM, VMEM],
+    )(mine, across[0], prec, totals, owner_blocks)
+    across = [flip(x, 1) for x in direct[1:]]
+    count = pairs - 1
     (placed,) = call(
-        functools.partial(place, pairs),
-        [(pairs * BLOCK, out_grads.shape[1])],
-        [VMEM] * (2 * pairs + 2) + [SMEM],
-        [pltpu.VMEM((2 * pairs,) + piece, f32), pltpu.SemaphoreType.DMA((2 * pairs,))],
-        out_specs=[ANY],
-    )(*direct, *across, prec, totals, owner_blocks)
+        functools.partial(place_far, count),
+        [slab],
+        [VMEM] * (2 * count + 1) + [SMEM, HBM],
+        [pltpu.VMEM((2 * count,) + piece, f32), pltpu.SemaphoreType.DMA((2 * count,))],
+        out_specs=[HBM],
+        input_output_aliases={2 * count + 2: 0},
+    )(*direct[1:], *across, scale, owner_blocks, placed)
     return placed, new_stat[None, None]
 
 

time: 79.2 us -> 73.5 us (0.928)
  blocking collectives: 0 us -> 11.3 us
  local copies, waits for them, and re-layouts: 10.9 us -> 0.01 us
  starting transfers between devices: 16.6 us -> 11.3 us
  waiting for transfers between devices: 36.4 us -> 31.6 us
  Pallas kernels: 14 us -> 18.3 us
    all_to_all x0 -> x1, blocking collectives: none -> 11.3 us  [per_device(): prec = lax.all_to_all(spread, AXES, 0, 0)]
    unnamed x18 -> x2, local copies, waits for them, and re-layouts: 10.9 us -> 0.01 us
    all_to_all x1 -> x0, waiting for transfers between devices: 5.88 us -> none  [per_device(): prec = lax.all_to_all(spread, AXES, 0, 0)]
    all_to_all x1 -> x0, starting transfers between devices: 5.09 us -> none  [per_device(): prec = lax.all_to_all(spread, AXES, 0, 0)]
    pallas_call x4, Pallas kernels: 6.68 us -> 9.65 us  [the longest x1 4.58 us: per_device(): call(stat_powers, [pltpu.HBM((3,) + square, f32)] * 2 + [(4, 128)], [VMEM...]
    ppermute x7, waiting for transfers between devices: 20.5 us -> 22.7 us  [flip(): lax.ppermute(x, 'rep', [(i, i ^ mask) for i in range(lax.axis_size('rep'))])]
    ppermute x1, waiting for transfers between devices: 9.99 us -> 8.11 us  [per_device(): near = lax.ppermute(packed, 'rep', shuffle)]
    pallas_call x1, Pallas kernels: 3.62 us -> 4.9 us  [per_device(): call(functools.partial(precondition, devices), [piece, (devices, 1, 128),...]
  transfers between devices with their start and end apart: 11 -> 10, of which waited for: 5 -> 5; matrix products, arithmetic and copies ran while one was open for 0% -> 0% of each run, Pallas kernels for 9% -> 14%
where the time goes in v3:
time: 73.5 us; the launch traced here: 73.3 us
  waiting for transfers between devices  31.6 us (43%)
  Pallas kernels  18.3 us (25%)
  starting transfers between devices  11.3 us (15%)
  blocking collectives  11.3 us (15%)
    ppermute x7, waiting for transfers between devices, flip(): lax.ppermute(x, 'rep', [(i, i ^ mask) for i in range(lax.axis_size('rep'))])  22.7 us
    all_to_all x1, blocking collectives, per_device(): prec = lax.all_to_all(spread, AXES, 0, 0)  11.3 us
    ppermute x1, waiting for transfers between devices, per_device(): near = lax.ppermute(packed, 'rep', shuffle)  8.11 us
    all_to_all x1, starting transfers between devices, per_device(): sums = lax.all_to_all(sums, AXES, 0, 0)  5.71 us
    pallas_call x1, Pallas kernels, per_device(): call(functools.partial(precondition, devices), [piece, (devices, 1, 128),...  4.9 us
    pallas_call x1, Pallas kernels, per_device(): call(stat_powers, [pltpu.HBM((3,) + square, f32)] * 2 + [(4, 128)], [VMEM...  4.58 us
    ppermute x7, starting transfers between devices, flip(): lax.ppermute(x, 'rep', [(i, i ^ mask) for i in range(lax.axis_size('rep'))])  4.55 us
    pallas_call x1, Pallas kernels, per_device(): call(update_stats, [square, square, (PACKED, BLOCK)], [VMEM] * 4, [pltpu....  1.8 us
  transfers between devices with their start and end apart: 10, of which 5 were waited for; matrix products, arithmetic and copies ran while one was open for 0% of the time, Pallas kernels for 14%

profile of v3, /device:TPU:0, one launch (start us, length us, event | category | flops | bytes accessed | tf_op | source)
XLA Modules:
  0.0 73.3 jit_solution(12662077267072689523)
XLA Ops:
  0.6 1.7 %shard_map.59 = (f32[2,256,512]{2,1,0:T(8,128)S(1)}, f32[2,256,512]{2,1,0:T(8,128)S(1)}, f32[264,512]{1,0:T(8,128)S(1)}, f32[1,128]{1,0:T(1,128)S(1)}) custom-call(bf16[256,1024]{1,0:T(8,128)(2,1)} %acts.1, bf16[256,512]{1,0:T(8,128)(2,1)} %grads.1, f32[512,512]{1,0:T(8,128)} %bitcast.5, s32[1,2]{1,0:T(1,128)} %refs_3_.1), custom_call_target="tpu_custom_call" | custom-call | flops 268435456 | bytes 1048576 | tf_op jit(solution)/shard_map/pallas_call | solution.py:298
  2.3 0.6 collective-permute-start
  2.9 0.0 collective-permute-start.3
  2.9 2.3 %collective-permute-done.got = f32[2,256,512]{2,1,0:T(8,128)S(1)} collective-permute-done((f32[2,256,512]{2,1,0:T(8,128)S(1)}, f32[2,256,512]{2,1,0:T(8,128)S(1)}, u32[]{:S(2)}, u32[]{:S(2)}) %collective-permute-start) | collective-permute-done | bytes 1048608 | tf_op jit(solution)/shard_map/ppermute | solution.py:54
  5.2 0.1 fusion
  5.3 2.9 %collective-permute-start.1 = (f32[256,512]{1,0:T(8,128)S(1)}, f32[256,512]{1,0:T(8,128)S(1)}, u32[]{:S(2)}, u32[]{:S(2)}) collective-permute-start(f32[256,512]{1,0:T(8,128)S(1)} %fusion), channel_id=1, source_target_pairs={{0,16},{8,24},{16,0},{24,8},{1,17},{9,25},{17,1},{25,9},{2,18},{10... | collective-permute-start | bytes 1572872 | tf_op jit(solution)/shard_map/ppermute | solution.py:54
  8.2 8.1 %collective-permute-done.3.near = f32[264,512]{1,0:T(8,128)S(1)} collective-permute-done((f32[264,512]{1,0:T(8,128)S(1)}, f32[264,512]{1,0:T(8,128)S(1)}, u32[]{:S(2)}, u32[]{:S(2)}) %collective-permute-start.3) | collective-permute-done | bytes 540704 | tf_op jit(solution)/shard_map/ppermute | solution.py:312
  16.3 7.7 %collective-permute-done.1.rest = f32[256,512]{1,0:T(8,128)S(1)} collective-permute-done((f32[256,512]{1,0:T(8,128)S(1)}, f32[256,512]{1,0:T(8,128)S(1)}, u32[]{:S(2)}, u32[]{:S(2)}) %collective-permute-start.1) | collective-permute-done | bytes 524320 | tf_op jit(solution)/shard_map/ppermute | solution.py:54
  24.0 0.8 %shard_map.60 = (f32[256,512]{1,0:T(8,128)S(1)}, f32[32,2,128]{2,1,0:T(2,128)}) custom-call(f32[2,256,512]{2,1,0:T(8,128)S(1)} %get-tuple-element.19.keep, f32[2,256,512]{2,1,0:T(8,128)S(1)} %collective-permute-done.got, f32[256,512]{1,0:T(8,128)S(1)} %collective-permute-done.1.rest, f32[1,128]{1,0:T(1,128)S(1)} %get-tuple-element.21.trace), custom_call_target="tpu_custom_call" | custom-call | bytes 1048576 | tf_op jit(solution)/shard_map/pallas_call | solution.py:321
  24.8 5.7 %all-to-all-start = ((f32[32,2,128]{2,1,0:T(2,128)}), f32[32,2,128]{2,1,0:T(2,128)S(1)}, u32[]{:S(2)}, u32[]{:S(2)}) async-start(f32[32,2,128]{2,1,0:T(2,128)} %get-tuple-element.29), calls=%async_computation | async-start | bytes 65536 | tf_op jit(solution)/shard_map/all_to_all | solution.py:326
  30.5 0.0 collective-permute-done.4.far
  30.5 1.8 %shard_map.61 = (f32[512,512]{1,0:T(8,128)S(1)}, f32[512,512]{1,0:T(8,128)S(1)}, f32[264,512]{1,0:T(8,128)S(1)}) custom-call(f32[256,512]{1,0:T(8,128)S(1)} %get-tuple-element.22.half, f32[256,512]{1,0:T(8,128)S(1)} %collective-permute-done.2.other, f32[264,512]{1,0:T(8,128)S(1)} %collective-permute-done.3.near, f32[264,512]{1,0:T(8,128)S(1)} %collective-permute-done.4.far), custom_call_target="tpu_custom_call" | custom-call | flops 1610612736 | bytes 1048576 | tf_op jit(solution)/shard_map/pallas_call | solution.py:327
  32.3 4.6 %shard_map.62 = (f32[3,512,512]{2,1,0:T(8,128)}, f32[3,512,512]{2,1,0:T(8,128)}, f32[4,128]{1,0:T(4,128)S(1)}) custom-call(f32[512,512]{1,0:T(8,128)S(1)} %get-tuple-element.24.left, f32[512,512]{1,0:T(8,128)S(1)} %get-tuple-element.25.right), custom_call_target="tpu_custom_call" | custom-call | flops 3221225472 | bytes 1048576 | tf_op jit(solution)/shard_map/pallas_call | solution.py:335
  36.9 0.8 %all-to-all-done.sums = f32[32,2,128]{2,1,0:T(2,128)S(1)} async-done(((f32[32,2,128]{2,1,0:T(2,128)}), f32[32,2,128]{2,1,0:T(2,128)S(1)}, u32[]{:S(2)}, u32[]{:S(2)}) %all-to-all-start) | async-done | bytes 32800 | tf_op jit(solution)/shard_map/all_to_all | solution.py:326
  37.7 4.9 %shard_map.63 = (f32[256,512]{1,0:T(8,128)S(1)}, f32[32,1,128]{2,1,0:T(1,128)S(1)}, f32[1,128]{1,0:T(1,128)S(1)}) custom-call(f32[256,512]{1,0:T(8,128)S(1)} %get-tuple-element.22.half, f32[256,512]{1,0:T(8,128)S(1)} %collective-permute-done.2.other, f32[3,512,512]{2,1,0:T(8,128)} %get-tuple-element.26.left_in, ...), custom_call_target="tpu_custom_call" | custom-call | flops 2415919104 | bytes 1048576 | tf_op jit(solution)/shard_map/pallas_call | solution.py:343
  42.6 1.1 %collective-permute-start.5 = (f32[256,512]{1,0:T(8,128)S(1)}, f32[256,512]{1,0:T(8,128)S(1)}, u32[]{:S(2)}, u32[]{:S(2)}) collective-permute-start(f32[256,512]{1,0:T(8,128)S(1)} %get-tuple-element.30.direct), channel_id=1, source_target_pairs={{0,16},{8,24},{16,0},{24,8},{1,17},{9,25},{17,1},{25,9},{2,18},{10... | collective-permute-start | bytes 1572872 | tf_op jit(solution)/shard_map/ppermute | solution.py:54
  43.6 1.0 %collective-permute-start.8 = (f32[264,512]{1,0:T(8,128)S(1)}, f32[264,512]{1,0:T(8,128)S(1)}, u32[]{:S(2)}, u32[]{:S(2)}) collective-permute-start(f32[264,512]{1,0:T(8,128)S(1)} %get-tuple-element.35), channel_id=1, source_target_pairs={{8,0},{24,8},{0,16},{16,24},{9,1},{25,9},{1,17},{17,25},{10,2},{26... | collective-permute-start | bytes 1622024 | tf_op jit(solution)/shard_map/ppermute | solution.py:334
  44.7 0.0 collective-permute-start.7
  44.7 12.8 %collective-permute-done.5.refs_0_ = f32[256,512]{1,0:T(8,128)S(1)} collective-permute-done((f32[256,512]{1,0:T(8,128)S(1)}, f32[256,512]{1,0:T(8,128)S(1)}, u32[]{:S(2)}, u32[]{:S(2)}) %collective-permute-start.5) | collective-permute-done | bytes 524320 | tf_op jit(solution)/shard_map/ppermute | solution.py:54
  57.4 11.3 %all_to_all.10.sums = f32[32,1,128]{2,1,0:T(1,128)S(1)} all-to-all(f32[32,1,128]{2,1,0:T(1,128)S(1)} %get-tuple-element.31), channel_id=1, replica_groups=mesh['rep'=4,'stripe'=8] {'rep','stripe'}, dimensions={0} | all-to-all | bytes 32768 | tf_op jit(solution)/shard_map/all_to_all | solution.py:356
  68.7 1.8 %shard_map.64 = (f32[1024,512]{1,0:T(8,128)}, f32[1,128]{1,0:T(1,128)S(1)}) custom-call(f32[256,512]{1,0:T(8,128)S(1)} %get-tuple-element.30.direct, f32[256,512]{1,0:T(8,128)S(1)} %collective-permute-done.7.across, f32[32,1,128]{2,1,0:T(1,128)S(1)} %all_to_all.10.sums, f32[1,128]{1,0:T(1,128)S(1)} %get-tuple-element.32.totals, s32[1,2]{1,0:T(1,128)S(1)} %copy-done), custom_call_target="tpu_custom_call" | custom-call | bytes 1048576 | tf_op jit(solution)/shard_map/pallas_call | solution.py:359
  70.5 0.0 collective-permute-done.8.packed
  70.5 1.2 %shard_map.66 = f32[512,512]{1,0:T(8,128)} custom-call(f32[264,512]{1,0:T(8,128)S(1)} %collective-permute-done.8.packed), custom_call_target="tpu_custom_call" | custom-call | bytes 1048576 | tf_op jit(solution)/shard_map/pallas_call | solution.py:357
  71.7 1.6 %shard_map.65 = f32[1024,512]{1,0:T(8,128)} custom-call(f32[256,512]{1,0:T(8,128)S(1)} %collective-permute-done.5.refs_0_, f32[256,512]{1,0:T(8,128)S(1)} %collective-permute-done.6.refs_1_, f32[1,128]{1,0:T(1,128)S(1)} %get-tuple-element.33.refs_2_, s32[1,2]{1,0:T(1,128)S(1)} %copy-done, ...), custom_call_target="tpu_custom_call", output_to_operand_aliasing={{}: (4, {})} | custom-call | bytes 1048576 | tf_op jit(solution)/shard_map/pallas_call | solution.py:368
  (8 shorter events, 0.0 us)
Async XLA Ops:
  2.3 2.8 %collective-permute-start = (f32[2,256,512]{2,1,0:T(8,128)S(1)}, f32[2,256,512]{2,1,0:T(8,128)S(1)}, u32[]{:S(2)}, u32[]{:S(2)}) collective-permute-start(f32[2,256,512]{2,1,0:T(8,128)S(1)} %get-tuple-element.20), channel_id=1, source_target_pairs={{0,8},{8,0},{16,24},{24,16},{1,9},{9,1},{17,25},{25,17},{2,10},{10... | collective-permute-start | bytes 3145736 | tf_op jit(solution)/shard_map/ppermute | solution.py:54
  2.9 13.4 %collective-permute-start.3 = (f32[264,512]{1,0:T(8,128)S(1)}, f32[264,512]{1,0:T(8,128)S(1)}, u32[]{:S(2)}, u32[]{:S(2)}) collective-permute-start(f32[264,512]{1,0:T(8,128)S(1)} %get-tuple-element.23), channel_id=1, source_target_pairs={{0,8},{8,24},{16,0},{24,16},{1,9},{9,25},{17,1},{25,17},{2,10},{10... | collective-permute-start | bytes 1622024 | tf_op jit(solution)/shard_map/ppermute | solution.py:312
  5.3 18.7 %collective-permute-start.1 = (f32[256,512]{1,0:T(8,128)S(1)}, f32[256,512]{1,0:T(8,128)S(1)}, u32[]{:S(2)}, u32[]{:S(2)}) collective-permute-start(f32[256,512]{1,0:T(8,128)S(1)} %fusion), channel_id=1, source_target_pairs={{0,16},{8,24},{16,0},{24,8},{1,17},{9,25},{17,1},{25,9},{2,18},{10... | collective-permute-start | bytes 1572872 | tf_op jit(solution)/shard_map/ppermute | solution.py:54
  16.3 14.2 %collective-permute-start.4 = (f32[264,512]{1,0:T(8,128)S(1)}, f32[264,512]{1,0:T(8,128)S(1)}, u32[]{:S(2)}, u32[]{:S(2)}) collective-permute-start(f32[264,512]{1,0:T(8,128)S(1)} %collective-permute-done.3.near), channel_id=1, source_target_pairs={{0,8},{8,0},{16,24},{24,16},{1,9},{9,1},{17,25},{25,17},{2,10},{10... | collective-permute-start | bytes 1622024 | tf_op jit(solution)/shard_map/ppermute | solution.py:54
  24.8 5.7 %collective-permute-start.2 = (f32[256,512]{1,0:T(8,128)S(1)}, f32[256,512]{1,0:T(8,128)S(1)}, u32[]{:S(2)}, u32[]{:S(2)}) collective-permute-start(f32[256,512]{1,0:T(8,128)S(1)} %get-tuple-element.22.half), channel_id=1, source_target_pairs={{0,8},{8,0},{16,24},{24,16},{1,9},{9,1},{17,25},{25,17},{2,10},{10... | collective-permute-start | bytes 1572872 | tf_op jit(solution)/shard_map/ppermute | solution.py:54
  24.8 12.9 %all-to-all-start = ((f32[32,2,128]{2,1,0:T(2,128)}), f32[32,2,128]{2,1,0:T(2,128)S(1)}, u32[]{:S(2)}, u32[]{:S(2)}) async-start(f32[32,2,128]{2,1,0:T(2,128)} %get-tuple-element.29), calls=%async_computation | async-start | bytes 65536 | tf_op jit(solution)/shard_map/all_to_all | solution.py:326
  37.7 31.0 %copy-start = (s32[1,2]{1,0:T(1,128)S(1)}, s32[1,2]{1,0:T(1,128)}, u32[]{:S(2)}) copy-start(s32[1,2]{1,0:T(1,128)} %refs_3_.1) | copy-start | bytes 28
  42.6 14.9 %collective-permute-start.5 = (f32[256,512]{1,0:T(8,128)S(1)}, f32[256,512]{1,0:T(8,128)S(1)}, u32[]{:S(2)}, u32[]{:S(2)}) collective-permute-start(f32[256,512]{1,0:T(8,128)S(1)} %get-tuple-element.30.direct), channel_id=1, source_target_pairs={{0,16},{8,24},{16,0},{24,8},{1,17},{9,25},{17,1},{25,9},{2,18},{10... | collective-permute-start | bytes 1572872 | tf_op jit(solution)/shard_map/ppermute | solution.py:54
  43.6 26.8 %collective-permute-start.8 = (f32[264,512]{1,0:T(8,128)S(1)}, f32[264,512]{1,0:T(8,128)S(1)}, u32[]{:S(2)}, u32[]{:S(2)}) collective-permute-start(f32[264,512]{1,0:T(8,128)S(1)} %get-tuple-element.35), channel_id=1, source_target_pairs={{8,0},{24,8},{0,16},{16,24},{9,1},{25,9},{1,17},{17,25},{10,2},{26... | collective-permute-start | bytes 1622024 | tf_op jit(solution)/shard_map/ppermute | solution.py:334
  44.7 24.0 %collective-permute-start.7 = (f32[256,512]{1,0:T(8,128)S(1)}, f32[256,512]{1,0:T(8,128)S(1)}, u32[]{:S(2)}, u32[]{:S(2)}) collective-permute-start(f32[256,512]{1,0:T(8,128)S(1)} %get-tuple-element.30.direct), channel_id=1, source_target_pairs={{0,8},{8,0},{16,24},{24,16},{1,9},{9,1},{17,25},{25,17},{2,10},{10... | collective-permute-start | bytes 1572872 | tf_op jit(solution)/shard_map/ppermute | solution.py:54
  57.4 14.2 %collective-permute-start.6 = (f32[256,512]{1,0:T(8,128)S(1)}, f32[256,512]{1,0:T(8,128)S(1)}, u32[]{:S(2)}, u32[]{:S(2)}) collective-permute-start(f32[256,512]{1,0:T(8,128)S(1)} %collective-permute-done.5.refs_0_), channel_id=1, source_target_pairs={{0,8},{8,0},{16,24},{24,16},{1,9},{9,1},{17,25},{25,17},{2,10},{10... | collective-permute-start | bytes 1572872 | tf_op jit(solution)/shard_map/ppermute | solution.py:54

commit v4 on v3

v4 whole, which is shorter than its diff:
```python
import functools
import math

import jax
import jax.numpy as jnp
from jax import lax
from jax.experimental import pallas as pl
from jax.experimental.pallas import tpu as pltpu
from jax.sharding import PartitionSpec as P


BLOCK = 512
HALF = BLOCK // 2
PACKED = HALF + 8

decay_rate = 0.95
damping = 0.25
epsilon = 1e-06
AXES = ("rep", "stripe")
f32 = jnp.float32
bf16 = jnp.bfloat16

ROOT_COEFFS = (
    25 / 16,
    -5 / 16 - 3125 / 4096,
    3125 / 4096,
    -1250 / 4096,
    250 / 4096,
    -25 / 4096,
    1 / 4096,
)

VMEM = pl.BlockSpec(memory_space=pltpu.VMEM)
SMEM = pl.BlockSpec(memory_space=pltpu.SMEM)
HBM = pl.BlockSpec(memory_space=pltpu.HBM)
LOW = pl.ds(0, HALF)
TOP = pl.ds(HALF, HALF)


def call(body, out_shapes, in_specs, scratch=(), limit=16, flops=0, out_specs=None, **kwargs):
    return pl.pallas_call(
        body,
        out_shape=[jax.ShapeDtypeStruct(s, f32) if isinstance(s, tuple) else s for s in out_shapes],
        in_specs=in_specs,
        out_specs=out_specs or [VMEM] * len(out_shapes),
        scratch_shapes=list(scratch),
        compiler_params=pltpu.CompilerParams(vmem_limit_bytes=limit << 20),
        cost_estimate=pl.CostEstimate(flops=flops, bytes_accessed=1 << 20, transcendentals=0),
        **kwargs,
    )


def flip(x, mask):
    return lax.ppermute(x, "rep", [(i, i ^ mask) for i in range(lax.axis_size("rep"))])


def in_hbm(x):
    return pltpu.with_memory_space_constraint(x, pltpu.HBM)


def chip_core():
    me = lax.axis_index("rep")
    return lax.shift_right_logical(me, 1), lax.bitwise_and(me, 1)


def split(x):
    hi = x.astype(bf16)
    return hi, (x - hi.astype(f32)).astype(bf16)


def mm(a, b):
    return jnp.dot(a, b, preferred_element_type=f32)


def dot3(a, b):
    return mm(a[0], b[0]) + (mm(a[0], b[1]) + mm(a[1], b[0]))


def triangle():
    i = lax.broadcasted_iota(jnp.int32, (HALF, HALF), 0)
    j = lax.broadcasted_iota(jnp.int32, (HALF, HALF), 1)
    return i, j


def lanes(x):
    rows = jnp.sum(x, axis=0, keepdims=True)
    return sum(rows[:, k : k + 128] for k in range(0, x.shape[1], 128))


def pack_into(out, a, b, c):
    i, j = triangle()
    out[LOW, LOW] = jnp.where(i <= j, a, c)
    out[LOW, TOP] = b
    out[HALF:, LOW] = jnp.broadcast_to(jnp.sum(jnp.where(i == j, c, 0.0), axis=0, keepdims=True), (8, HALF))


def unpack(u, diag):
    i, j = triangle()
    ut = u.T
    return jnp.where(i <= j, u, ut), jnp.where(i > j, u, jnp.where(i < j, ut, diag))


def pack_stat(stat, out, trace):
    i, j = triangle()
    a, c = stat[LOW, LOW], stat[TOP, TOP]
    pack_into(out, a, stat[LOW, TOP], c)
    trace[...] = lanes(jnp.where(i == j, a + c, 0.0))


def grad_terms(plan, acts, grads, owners, *refs):
    outs, (av, gv, ov, sems) = refs[: len(plan)], refs[len(plan) :]
    chip, core = chip_core()
    copies = [
        pltpu.make_async_copy(src, dst, sems.at[k]) for k, (src, dst) in enumerate(((owners, ov), (acts, av), (grads, gv)))
    ]
    for copy in copies:
        copy.start()
    for copy in copies:
        copy.wait()
    cotangent = gv[...]
    for out, (chips, swapped) in zip(outs, plan):
        half = 1 - core if swapped else core
        for n, j in enumerate(chips):
            start = ov[0, chip ^ j] * BLOCK + half * HALF
            cols = av[:, pl.ds(pl.multiple_of(start, HALF), HALF)]
            out[n] = lax.dot_general(cols, cotangent, (((0,), (0,)), ((), ())), preferred_element_type=f32)


def finish_half(devices, keep, got, rest, trace, half, sums):
    value = keep[0] + got[0] + rest[...]
    half[...] = value
    both = jnp.concatenate([lanes(value * value), trace[...]], axis=0)
    sums[...] = jnp.broadcast_to(both[None], (devices, 2, 128))


def spread(top, corner, out):
    out[0, LOW], out[1, LOW] = split(top)
    out[0, TOP, TOP], out[1, TOP, TOP] = split(corner)
    for k in range(2):
        out[k, TOP, LOW] = out[k, LOW, TOP].T


def upper_product(a, b):
    top = dot3((a[0, LOW], a[1, LOW]), (b[0], b[1]))
    return top, dot3((a[0, TOP], a[1, TOP]), (b[0, :, TOP], b[1, :, TOP]))


def total(x):
    return jnp.sum(jnp.sum(x, axis=0, keepdims=True), axis=1, keepdims=True)


def load_gradient(core, half, other, g):
    mine = pl.ds(pl.multiple_of(core * HALF, HALF), HALF)
    theirs = pl.ds(pl.multiple_of(HALF - core * HALF, HALF), HALF)
    for rows, src in ((mine, half), (theirs, other)):
        g[0, rows], g[1, rows] = split(src[...])


def update_powers(half, other, old, tops, corners, facts, out, g_out, gg, s1, s2, stage, sems):
    _, core = chip_core()
    load_gradient(core, half, other, gg.at[0])
    keep = pltpu.make_async_copy(gg.at[0], g_out, sems.at[0])
    keep.start()
    for k in range(2):
        gg[1, k] = gg[0, k].T
    top, corner = upper_product(gg.at[1 - core], gg.at[core])
    sa, sc = unpack(old[LOW, LOW], old[HALF : HALF + 1, LOW])
    s00 = decay_rate * sa + top[:, :HALF]
    s01 = decay_rate * old[LOW, TOP] + top[:, HALF:]
    s11 = decay_rate * sc + corner
    pack_into(stage, s00, s01, s11)
    copy = pltpu.make_async_copy(stage, out, sems.at[1])
    copy.start()
    i, j = triangle()
    trace = total(jnp.where(i == j, s00 + s11, 0.0))
    norm_sq = total(s00 * s00 + s11 * s11 + 2.0 * (s01 * s01))
    inv = 1.0 / jnp.sqrt(norm_sq + epsilon)
    tops[0, :, LOW], tops[0, :, TOP], corners[0] = s00 * inv, s01 * inv, s11 * inv
    spread(tops[0], corners[0], s1)
    tops[1], corners[1] = upper_product(s1, s1)
    spread(tops[1], corners[1], s2)
    tops[2], corners[2] = upper_product(s1, s2)
    facts[...] = jnp.concatenate([jnp.broadcast_to(x, (1, 128)) for x in (norm_sq, trace)], axis=0)
    keep.wait()
    copy.wait()


def coefficients(devices, facts, sums):
    both = jnp.sum(jnp.sum(sums[...], axis=0), axis=1, keepdims=True)
    grad_sq, trace_all = both[0:1], both[1:2]
    shift = (decay_rate * trace_all + 2.0 * grad_sq) * (damping / (devices * BLOCK))
    shift = jnp.broadcast_to(shift, (1, 128))
    norm_sq, trace = facts[0:1, :], facts[1:2, :]
    frob = jnp.sqrt(norm_sq + 2.0 * shift * trace + BLOCK * shift * shift + epsilon)
    a = jnp.sqrt(norm_sq + epsilon) / frob
    e = shift / frob
    outer = 1.0 / jnp.sqrt(jnp.sqrt(frob))
    k = []
    for i in range(7):
        value = jnp.full_like(e, ROOT_COEFFS[6] * math.comb(6, i))
        for j in range(5, i - 1, -1):
            value = value * e + math.comb(j, i) * ROOT_COEFFS[j]
        k.append((outer * value)[:, 0:1])
        outer = outer * a
    return k, grad_sq


def root(devices, tops, corners, facts, sums, out, totals, inner, cube):
    k, grad_sq = coefficients(devices, facts, sums)
    spread(tops[2], corners[2], cube)
    spread(*(k[4] * t[0] + k[5] * t[1] + k[6] * t[2] for t in (tops, corners)), inner)
    top, corner = upper_product(cube, inner)
    i, j = triangle()
    diag = jnp.where(i == j, k[0], 0.0)
    low = k[1] * tops[0] + k[2] * tops[1] + k[3] * tops[2] + top
    out[LOW, LOW] = low[:, :HALF] + diag
    out[LOW, TOP] = low[:, HALF:]
    corner = k[1] * corners[0] + k[2] * corners[1] + k[3] * corners[2] + corner + diag
    out[HALF:, LOW] = corner[: HALF // 2]
    out[HALF:, TOP] = corner[HALF // 2 :]
    totals[...] = jnp.broadcast_to(grad_sq, (1, 128))


def root_corner(packed):
    return jnp.concatenate([packed[HALF:, LOW], packed[HALF:, TOP]], axis=0)


def half_way(g_in, packed, out, g, x, sem):
    _, core = chip_core()
    copy = pltpu.make_async_copy(g_in, g, sem)
    copy.start()
    spread(packed[LOW], root_corner(packed), x)
    copy.wait()

    @pl.when(core == 1)
    def _():
        y = dot3((x[0, TOP], x[1, TOP]), (g[0], g[1]))
        out[0, LOW], out[1, LOW] = split(y)

    @pl.when(core == 0)
    def _():
        out[0], out[1] = split(dot3((g[0], g[1]), (x[0], x[1])))


def last_product(middle, packed, mine, sums, x):
    _, core = chip_core()

    @pl.when(core == 1)
    def _():
        spread(packed[LOW], root_corner(packed), x)
        mine[...] = dot3((middle[0, LOW], middle[1, LOW]), (x[0], x[1]))

    @pl.when(core == 0)
    def _():
        mine[...] = dot3(split(packed[LOW]), (middle[0], middle[1]))

    sums[...] = lanes(mine[...] * mine[...])


def unpack_stat(source, out, packed, sem):
    copy = pltpu.make_async_copy(source, packed, sem)
    copy.start()
    copy.wait()
    sa, sc = unpack(packed[LOW, LOW], packed[HALF : HALF + 1, LOW])
    off = packed[LOW, TOP]
    out[LOW, LOW] = sa
    out[LOW, TOP] = off
    out[TOP, LOW] = off.T
    out[TOP, TOP] = sc


def write_pieces(chip, core, pieces, scale, owners, out, scaled, sems):
    copies = []
    for n, (j, swapped, src) in enumerate(pieces):
        scaled[n] = src[...] * scale
        half = 1 - core if swapped else core
        start = pl.multiple_of(owners[0, chip ^ j] * BLOCK + half * HALF, HALF)
        copies.append(pltpu.make_async_copy(scaled.at[n], out.at[pl.ds(start, HALF)], sems.at[n]))
        copies[-1].start()
    for copy in copies:
        copy.wait()


def place_near(direct, across, sums, totals, owners, out, scale, scaled, sems):
    chip, core = chip_core()
    prec_sq = jnp.sum(jnp.sum(sums[...], axis=0), axis=1, keepdims=True)
    factor = jnp.sqrt(totals[0:1, 0:1] / (prec_sq + epsilon))
    scale[...] = jnp.broadcast_to(factor, (1, 128))
    write_pieces(chip, core, ((0, False, direct), (0, True, across)), factor, owners, out, scaled, sems)


def place_far(count, *refs):
    direct, across = refs[:count], refs[count : 2 * count]
    scale, owners, _, out, scaled, sems = refs[2 * count :]
    chip, core = chip_core()
    pieces = [(j + 1, False, x) for j, x in enumerate(direct)] + [(j + 1, True, x) for j, x in enumerate(across)]
    write_pieces(chip, core, pieces, scale[0:1, 0:1], owners, out, scaled, sems)


def per_device(activations, out_grads, statistics, owner_blocks):
    rep_count = lax.axis_size("rep")
    pairs = rep_count // 2
    devices = rep_count * lax.axis_size("stripe")
    tokens = activations.shape[0]
    piece, square = (HALF, BLOCK), (BLOCK, BLOCK)
    unit = 6 * BLOCK**3

    whole = jax.ShapeDtypeStruct((2,) + square, bf16)
    split_square = pltpu.VMEM((2,) + square, bf16)
    packed_buffer = pltpu.VMEM((PACKED, BLOCK), f32)
    m = pairs // 2

    def terms(*plan):
        return call(
            functools.partial(grad_terms, plan),
            [(len(chips),) + piece for chips, _ in plan],
            [HBM] * 3,
            [
                pltpu.VMEM(activations.shape, bf16),
                pltpu.VMEM(out_grads.shape, bf16),
                pltpu.SMEM(owner_blocks.shape, jnp.int32),
                pltpu.SemaphoreType.DMA((3,)),
            ],
            flops=2 * tokens * HALF * BLOCK * sum(len(chips) for chips, _ in plan),
        )(*(in_hbm(x) for x in (activations, out_grads, owner_blocks)))

    upper, lower = range(m, pairs), range(m)
    (send_far,) = terms((upper, True))
    got_far = flip(send_far, 1)
    keep_far, send_near, keep_near = terms((upper, False), (lower, True), (lower, False))
    got_near = flip(send_near, 1)
    arrived = [flip(keep_far[j] + got_far[j], 2 * m) for j in range(m)]
    while m > 1:
        m //= 2
        held = [keep_near[j] + got_near[j] + arrived[j] for j in range(m, 2 * m)]
        arrived = [x + flip(y, 2 * m) for x, y in zip(arrived, held)]
    shuffle = [(s * pairs + p, 2 * p + 1 - s) for s in range(2) for p in range(pairs)]
    packed, trace = call(pack_stat, [(PACKED, BLOCK), (1, 128)], [VMEM])(statistics[0, 0])
    old = lax.ppermute(packed, "rep", shuffle)
    half, sums = call(
        functools.partial(finish_half, devices), [piece, (devices, 2, 128)], [VMEM] * 4
    )(keep_near, got_near, arrived[0], trace)
    other = flip(half, 1)
    sums = lax.all_to_all(sums, AXES, 0, 0)
    tops, corners, facts, out_packed, g_split = call(
        update_powers,
        [(3,) + piece, (3, HALF, HALF), (2, 128), pltpu.HBM((PACKED, BLOCK), f32), pltpu.HBM((2,) + square, bf16)],
        [VMEM] * 3,
        [pltpu.VMEM((2, 2) + square, bf16), split_square, split_square]
        + [packed_buffer, pltpu.SemaphoreType.DMA((2,))],
        flops=3 * unit,
        out_specs=[VMEM] * 3 + [HBM] * 2,
    )(half, other, old)
    new_packed = lax.ppermute(out_packed, "rep", [(t, s) for s, t in shuffle])
    mine_root, totals = call(
        functools.partial(root, devices),
        [(HALF + HALF // 2, BLOCK), (1, 128)],
        [VMEM] * 4,
        [split_square] * 2,
        flops=unit,
    )(tops, corners, facts, sums)
    other_root = flip(mine_root, 1)
    (middle,) = call(half_way, [whole], [HBM, VMEM], [split_square] * 2 + [pltpu.SemaphoreType.DMA], flops=unit)(
        in_hbm(g_split), mine_root
    )
    mine, prec = call(last_product, [piece, (1, 128)], [VMEM] * 2, [split_square], flops=unit)(middle, other_root)

    bit = 1
    while bit < rep_count:
        masks = [x for x in (3 * bit, 2 * bit, bit) if x < rep_count]
        prec = sum((flip(prec, x) for x in masks), prec)
        bit *= 4
    direct, m = [mine], 1
    while m < pairs:
        direct = direct + [flip(x, 2 * m) for x in direct]
        m *= 2
    across = [flip(mine, 1)]
    stripes = lax.axis_size("stripe")
    prec = lax.all_to_all(jnp.broadcast_to(prec[None], (stripes, 1, 128)), "stripe", 0, 0)
    (new_stat,) = call(unpack_stat, [square], [HBM], [packed_buffer, pltpu.SemaphoreType.DMA])(in_hbm(new_packed))
    slab = (pairs * BLOCK, out_grads.shape[1])
    placed, scale = call(
        place_near,
        [slab, (1, 128)],
        [VMEM] * 4 + [SMEM],
        [pltpu.VMEM((2,) + piece, f32), pltpu.SemaphoreType.DMA((2,))],
        out_specs=[HBM, VMEM],
    )(mine, across[0], prec, totals, owner_blocks)
    across = [flip(x, 1) for x in direct[1:]]
    count = pairs - 1
    (placed,) = call(
        functools.partial(place_far, count),
        [slab],
        [VMEM] * (2 * count + 1) + [SMEM, HBM],
        [pltpu.VMEM((2 * count,) + piece, f32), pltpu.SemaphoreType.DMA((2 * count,))],
        out_specs=[HBM],
        input_output_aliases={2 * count + 2: 0},
    )(*direct[1:], *across, scale, owner_blocks, placed)
    return placed, new_stat[None, None]


def solution(mesh):
    in_specs = (
        P("rep", None),
        P("rep", "stripe"),
        P("rep", "stripe", None, None),
        P("stripe", None),
    )
    out_specs = (P(None, "stripe"), P("rep", "stripe", None, None))
    return jax.shard_map(per_device, mesh=mesh, in_specs=in_specs, out_specs=out_specs, check_vma=False)
```

time: 73.5 us -> 76.6 us (1.042)
  blocking collectives: 11.3 us -> 0 us
  starting transfers between devices: 11.3 us -> 18 us
  waiting for transfers between devices: 31.6 us -> 36.1 us
  local copies, waits for them, and re-layouts: 0.01 us -> 3.95 us
  Pallas kernels: 18.3 us -> 17.3 us
    all_to_all x1 -> x0, blocking collectives: 11.3 us -> none  [per_device(): prec = lax.all_to_all(spread, AXES, 0, 0)]
    ppermute x1, waiting for transfers between devices: 8.11 us -> 0.01 us  [per_device(): old = lax.ppermute(packed, 'rep', shuffle)]
    ppermute x7 -> x11, waiting for transfers between devices: 22.7 us -> 30.5 us  [flip(): lax.ppermute(x, 'rep', [(i, i ^ mask) for i in range(lax.axis_size('rep'))])]
    all_to_all x0 -> x1, starting transfers between devices: none -> 3.96 us  [per_device(): lax.all_to_all(jnp.broadcast_to(prec[None], (stripes, 1, 128)), 'stripe',...]
    all_to_all x0 -> x1, waiting for transfers between devices: none -> 3.45 us  [per_device(): lax.all_to_all(jnp.broadcast_to(prec[None], (stripes, 1, 128)), 'stripe',...]
    unnamed x2 -> x12, local copies, waits for them, and re-layouts: 0.01 us -> 3.35 us
    all_to_all x1, waiting for transfers between devices: 0.77 us -> 2.19 us  [per_device(): sums = lax.all_to_all(sums, AXES, 0, 0)]
    all_to_all x1, starting transfers between devices: 5.71 us -> 6.95 us  [per_device(): sums = lax.all_to_all(sums, AXES, 0, 0)]
  transfers between devices with their start and end apart: 10 -> 15, of which waited for: 5 -> 6; matrix products, arithmetic and copies ran while one was open for 0% -> 1% of each run, Pallas kernels for 14% -> 16%
where the time goes in v4:
time: 76.6 us; the launch traced here: 76.3 us
  waiting for transfers between devices  36.1 us (47%)
  starting transfers between devices  18 us (23%)
  Pallas kernels  17.3 us (23%)
  local copies, waits for them, and re-layouts  3.95 us (5%)
  between operations  0.81 us (1%)
    ppermute x11, waiting for transfers between devices, flip(): lax.ppermute(x, 'rep', [(i, i ^ mask) for i in range(lax.axis_size('rep'))])  30.5 us
    all_to_all x1, starting transfers between devices, per_device(): sums = lax.all_to_all(sums, AXES, 0, 0)  6.95 us
    ppermute x11, starting transfers between devices, flip(): lax.ppermute(x, 'rep', [(i, i ^ mask) for i in range(lax.axis_size('rep'))])  5.55 us
    all_to_all x1, starting transfers between devices, per_device(): lax.all_to_all(jnp.broadcast_to(prec[None], (stripes, 1, 128)), 'stripe',...  3.96 us
    pallas_call x1, Pallas kernels, per_device(): call(update_powers, [(3,) + piece, (3, HALF, HALF), (2, 128), pltpu.HBM((...  3.83 us
    all_to_all x1, waiting for transfers between devices, per_device(): lax.all_to_all(jnp.broadcast_to(prec[None], (stripes, 1, 128)), 'stripe',...  3.45 us
    unnamed x12, local copies, waits for them, and re-layouts  3.35 us
    pallas_call x2, Pallas kernels, terms(): call(functools.partial(grad_terms, plan), [(len(chips),) + piece for chip...  3.04 us
  transfers between devices with their start and end apart: 15, of which 6 were waited for; matrix products, arithmetic and copies ran while one was open for 1% of the time, Pallas kernels for 16%

profile of v4, /device:TPU:0, one launch (start us, length us, event | category | flops | bytes accessed | tf_op | source)
XLA Modules:
  0.0 76.3 jit_solution(12089876846863904073)
XLA Ops:
  0.6 1.5 %shard_map.60 = f32[1,256,512]{2,1,0:T(8,128)S(1)} custom-call(bf16[256,1024]{1,0:T(8,128)(2,1)} %acts.3, bf16[256,512]{1,0:T(8,128)(2,1)} %grads.3, s32[1,2]{1,0:T(1,128)} %refs_3_.1), custom_call_target="tpu_custom_call" | custom-call | flops 67108864 | bytes 1048576 | tf_op jit(solution)/shard_map/pallas_call | solution.py:314
  2.7 1.5 %shard_map.59 = (f32[1,256,512]{2,1,0:T(8,128)S(1)}, f32[1,256,512]{2,1,0:T(8,128)S(1)}, f32[1,256,512]{2,1,0:T(8,128)S(1)}) custom-call(bf16[256,1024]{1,0:T(8,128)(2,1)} %acts.3, bf16[256,512]{1,0:T(8,128)(2,1)} %grads.3, s32[1,2]{1,0:T(1,128)} %refs_3_.1), custom_call_target="tpu_custom_call" | custom-call | flops 201326592 | bytes 1048576 | tf_op jit(solution)/shard_map/pallas_call | solution.py:314
  4.4 3.0 %collective-permute-start.2 = (f32[256,512]{1,0:T(8,128)S(1)}, f32[256,512]{1,0:T(8,128)S(1)}, u32[]{:S(2)}, u32[]{:S(2)}) collective-permute-start(f32[256,512]{1,0:T(8,128)S(1)} %add_bitcast_fusion), channel_id=1, source_target_pairs={{0,16},{8,24},{16,0},{24,8},{1,17},{9,25},{17,1},{25,9},{2,18},{10... | collective-permute-start | bytes 1572872 | tf_op jit(solution)/shard_map/ppermute | solution.py:54
  7.5 12.2 %collective-permute-done.2.rest = f32[256,512]{1,0:T(8,128)S(1)} collective-permute-done((f32[256,512]{1,0:T(8,128)S(1)}, f32[256,512]{1,0:T(8,128)S(1)}, u32[]{:S(2)}, u32[]{:S(2)}) %collective-permute-start.2) | collective-permute-done | bytes 524320 | tf_op jit(solution)/shard_map/ppermute | solution.py:54
  19.8 0.8 %shard_map.62 = (f32[256,512]{1,0:T(8,128)S(1)}, f32[32,2,128]{2,1,0:T(2,128)}) custom-call(f32[1,256,512]{2,1,0:T(8,128)S(1)} %get-tuple-element.20.keep, f32[1,256,512]{2,1,0:T(8,128)S(1)} %collective-permute-done.got, f32[256,512]{1,0:T(8,128)S(1)} %collective-permute-done.2.rest, f32[1,128]{1,0:T(1,128)S(1)} %get-tuple-element.23.trace), custom_call_target="tpu_custom_call" | custom-call | bytes 1048576 | tf_op jit(solution)/shard_map/pallas_call | solution.py:340
  20.5 7.0 %all-to-all-start = ((f32[32,2,128]{2,1,0:T(2,128)}), f32[32,2,128]{2,1,0:T(2,128)S(1)}, u32[]{:S(2)}, u32[]{:S(2)}) async-start(f32[32,2,128]{2,1,0:T(2,128)} %get-tuple-element.30), calls=%async_computation | async-start | bytes 65536 | tf_op jit(solution)/shard_map/all_to_all | solution.py:344
  27.5 3.8 %shard_map.63 = (f32[3,256,512]{2,1,0:T(8,128)S(1)}, f32[3,256,256]{2,1,0:T(8,128)S(1)}, f32[2,128]{1,0:T(2,128)S(1)}, f32[264,512]{1,0:T(8,128)}, bf16[2,512,512]{2,1,0:T(8,128)(2,1)}) custom-call(f32[256,512]{1,0:T(8,128)S(1)} %get-tuple-element.24.half, f32[256,512]{1,0:T(8,128)S(1)} %collective-permute-done.3.other, ...), custom_call_target="tpu_custom_call" | custom-call | flops 2415919104 | bytes 1048576 | tf_op jit(solution)/shard_map/pallas_call | solution.py:345
  31.4 1.1 %copy-done.2 = f32[3,256,512]{2,1,0:T(8,128)} copy-done((f32[3,256,512]{2,1,0:T(8,128)}, f32[3,256,512]{2,1,0:T(8,128)S(1)}, u32[]{:S(2)}) %copy-start.2) | copy-done | bytes 1572888
  32.5 2.2 %all-to-all-done.sums = f32[32,2,128]{2,1,0:T(2,128)S(1)} async-done(((f32[32,2,128]{2,1,0:T(2,128)}), f32[32,2,128]{2,1,0:T(2,128)S(1)}, u32[]{:S(2)}, u32[]{:S(2)}) %all-to-all-start) | async-done | bytes 32800 | tf_op jit(solution)/shard_map/all_to_all | solution.py:344
  34.7 1.4 %copy-done.3 = f32[3,256,512]{2,1,0:T(8,128)S(1)} copy-done((f32[3,256,512]{2,1,0:T(8,128)S(1)}, f32[3,256,512]{2,1,0:T(8,128)}, u32[]{:S(2)}) %copy-start.3) | copy-done | bytes 1572888
  36.1 1.2 %shard_map.64 = (f32[384,512]{1,0:T(8,128)S(1)}, f32[1,128]{1,0:T(1,128)S(1)}) custom-call(f32[3,256,512]{2,1,0:T(8,128)S(1)} %copy-done.3, f32[3,256,256]{2,1,0:T(8,128)S(1)} %get-tuple-element.28.corners, f32[2,128]{1,0:T(2,128)S(1)} %get-tuple-element.29.facts, f32[32,2,128]{2,1,0:T(2,128)S(1)} %all-to-all-done.sums), custom_call_target="tpu_custom_call" | custom-call | flops 805306368 | bytes 1048576 | tf_op jit(solution)/shard_map/pallas_call | solution.py:355
  37.5 2.2 %shard_map.65.middle = bf16[2,512,512]{2,1,0:T(8,128)(2,1)S(1)} custom-call(bf16[2,512,512]{2,1,0:T(8,128)(2,1)} %get-tuple-element.26.g_in, f32[384,512]{1,0:T(8,128)S(1)} %get-tuple-element.31.packed), custom_call_target="tpu_custom_call" | custom-call | flops 805306368 | bytes 1048576 | tf_op jit(solution)/shard_map/pallas_call | solution.py:363
  39.7 0.7 shard_map.66
  40.4 0.6 collective-permute-start.6
  41.0 1.5 %collective-permute-start.12 = (f32[264,512]{1,0:T(8,128)S(1)}, f32[264,512]{1,0:T(8,128)S(1)}, u32[]{:S(2)}, u32[]{:S(2)}) collective-permute-start(f32[264,512]{1,0:T(8,128)S(1)} %copy-done.5), channel_id=1, source_target_pairs={{8,0},{24,8},{0,16},{16,24},{9,1},{25,9},{1,17},{17,25},{10,2},{26... | collective-permute-start | bytes 1622024 | tf_op jit(solution)/shard_map/ppermute | solution.py:354
  42.5 12.8 %collective-permute-done.6.refs_0_ = f32[256,512]{1,0:T(8,128)S(1)} collective-permute-done((f32[256,512]{1,0:T(8,128)S(1)}, f32[256,512]{1,0:T(8,128)S(1)}, u32[]{:S(2)}, u32[]{:S(2)}) %collective-permute-start.6) | collective-permute-done | bytes 524320 | tf_op jit(solution)/shard_map/ppermute | solution.py:54
  55.8 3.1 %collective-permute-done.10 = f32[1,128]{1,0:T(1,128)S(1)} collective-permute-done((f32[1,128]{1,0:T(1,128)S(1)}, f32[1,128]{1,0:T(1,128)S(1)}, u32[]{:S(2)}, u32[]{:S(2)}) %collective-permute-start.10) | collective-permute-done | bytes 544 | tf_op jit(solution)/shard_map/ppermute | solution.py:54
  59.4 2.4 %collective-permute-done.9 = f32[1,128]{1,0:T(1,128)S(1)} collective-permute-done((f32[1,128]{1,0:T(1,128)S(1)}, f32[1,128]{1,0:T(1,128)S(1)}, u32[]{:S(2)}, u32[]{:S(2)}) %collective-permute-start.9) | collective-permute-done | bytes 544 | tf_op jit(solution)/shard_map/ppermute | solution.py:54
  62.4 4.0 %all-to-all-start.1 = ((f32[8,1,128]{2,1,0:T(1,128)}), f32[8,1,128]{2,1,0:T(1,128)S(1)}, u32[]{:S(2)}, u32[]{:S(2)}) async-start(f32[8,1,128]{2,1,0:T(1,128)} %broadcast_in_dim.12), calls=%async_computation.1 | async-start | bytes 8192 | tf_op jit(solution)/shard_map/all_to_all | solution.py:379
  66.4 0.8 %copy-done.4 = f32[264,512]{1,0:T(8,128)} copy-done((f32[264,512]{1,0:T(8,128)}, f32[264,512]{1,0:T(8,128)S(1)}, u32[]{:S(2)}) %copy-start.4) | copy-done | bytes 540696
  67.2 2.2 %shard_map.69 = f32[512,512]{1,0:T(8,128)} custom-call(f32[264,512]{1,0:T(8,128)} %copy-done.4), custom_call_target="tpu_custom_call" | custom-call | bytes 1048576 | tf_op jit(solution)/shard_map/pallas_call | solution.py:380
  69.4 3.4 %all-to-all-done.1.sums = f32[8,1,128]{2,1,0:T(1,128)S(1)} async-done(((f32[8,1,128]{2,1,0:T(1,128)}), f32[8,1,128]{2,1,0:T(1,128)S(1)}, u32[]{:S(2)}, u32[]{:S(2)}) %all-to-all-start.1) | async-done | bytes 4128 | tf_op jit(solution)/shard_map/all_to_all | solution.py:379
  72.9 1.7 %shard_map.67 = (f32[1024,512]{1,0:T(8,128)}, f32[1,128]{1,0:T(1,128)S(1)}) custom-call(f32[256,512]{1,0:T(8,128)S(1)} %get-tuple-element.32.direct, f32[256,512]{1,0:T(8,128)S(1)} %collective-permute-done.8.across, f32[8,1,128]{2,1,0:T(1,128)S(1)} %all-to-all-done.1.sums, f32[1,128]{1,0:T(1,128)S(1)} %get-tuple-element.34.totals, s32[1,2]{1,0:T(1,128)S(1)} %copy-done.1), custom_call_target="tpu_custom_call" | custom-call | bytes 1048576 | tf_op jit(solution)/shard_map/pallas_call | solution.py:382
  74.6 1.6 %shard_map.68 = f32[1024,512]{1,0:T(8,128)} custom-call(f32[256,512]{1,0:T(8,128)S(1)} %collective-permute-done.6.refs_0_, f32[256,512]{1,0:T(8,128)S(1)} %collective-permute-done.7.refs_1_, f32[1,128]{1,0:T(1,128)S(1)} %get-tuple-element.35.refs_2_, s32[1,2]{1,0:T(1,128)S(1)} %copy-done.1, ...), custom_call_target="tpu_custom_call", output_to_operand_aliasing={{}: (4, {})} | custom-call | bytes 1048576 | tf_op jit(solution)/shard_map/pallas_call | solution.py:391
  (32 shorter events, 2.7 us)
Async XLA Ops:
  0.6 6.8 %copy-start = (f32[1,1,512,512]{3,2,1,0:T(8,128)S(1)}, f32[1,1,512,512]{3,2,1,0:T(8,128)}, u32[]{:S(2)}) copy-start(f32[1,1,512,512]{3,2,1,0:T(8,128)} %param.6) | copy-start | bytes 3145732
  2.1 2.2 %collective-permute-start.1 = (f32[1,256,512]{2,1,0:T(8,128)S(1)}, f32[1,256,512]{2,1,0:T(8,128)S(1)}, u32[]{:S(2)}, u32[]{:S(2)}) collective-permute-start(f32[1,256,512]{2,1,0:T(8,128)S(1)} %shard_map.60), channel_id=1, source_target_pairs={{0,8},{8,0},{16,24},{24,16},{1,9},{9,1},{17,25},{25,17},{2,10},{10... | collective-permute-start | bytes 1572872 | tf_op jit(solution)/shard_map/ppermute | solution.py:54
  4.2 3.3 %collective-permute-start = (f32[1,256,512]{2,1,0:T(8,128)S(1)}, f32[1,256,512]{2,1,0:T(8,128)S(1)}, u32[]{:S(2)}, u32[]{:S(2)}) collective-permute-start(f32[1,256,512]{2,1,0:T(8,128)S(1)} %get-tuple-element.21), channel_id=1, source_target_pairs={{0,8},{8,0},{16,24},{24,16},{1,9},{9,1},{17,25},{25,17},{2,10},{10... | collective-permute-start | bytes 1572872 | tf_op jit(solution)/shard_map/ppermute | solution.py:54
  4.4 15.3 %collective-permute-start.2 = (f32[256,512]{1,0:T(8,128)S(1)}, f32[256,512]{1,0:T(8,128)S(1)}, u32[]{:S(2)}, u32[]{:S(2)}) collective-permute-start(f32[256,512]{1,0:T(8,128)S(1)} %add_bitcast_fusion), channel_id=1, source_target_pairs={{0,16},{8,24},{16,0},{24,8},{1,17},{9,25},{17,1},{25,9},{2,18},{10... | collective-permute-start | bytes 1572872 | tf_op jit(solution)/shard_map/ppermute | solution.py:54
  7.5 20.0 %collective-permute-start.4 = (f32[264,512]{1,0:T(8,128)S(1)}, f32[264,512]{1,0:T(8,128)S(1)}, u32[]{:S(2)}, u32[]{:S(2)}) collective-permute-start(f32[264,512]{1,0:T(8,128)S(1)} %get-tuple-element.25), channel_id=1, source_target_pairs={{0,8},{8,24},{16,0},{24,16},{1,9},{9,25},{17,1},{25,17},{2,10},{10... | collective-permute-start | bytes 1622024 | tf_op jit(solution)/shard_map/ppermute | solution.py:339
  20.5 7.0 %collective-permute-start.3 = (f32[256,512]{1,0:T(8,128)S(1)}, f32[256,512]{1,0:T(8,128)S(1)}, u32[]{:S(2)}, u32[]{:S(2)}) collective-permute-start(f32[256,512]{1,0:T(8,128)S(1)} %get-tuple-element.24.half), channel_id=1, source_target_pairs={{0,8},{8,0},{16,24},{24,16},{1,9},{9,1},{17,25},{25,17},{2,10},{10... | collective-permute-start | bytes 1572872 | tf_op jit(solution)/shard_map/ppermute | solution.py:54
  20.5 14.2 %all-to-all-start = ((f32[32,2,128]{2,1,0:T(2,128)}), f32[32,2,128]{2,1,0:T(2,128)S(1)}, u32[]{:S(2)}, u32[]{:S(2)}) async-start(f32[32,2,128]{2,1,0:T(2,128)} %get-tuple-element.30), calls=%async_computation | async-start | bytes 65536 | tf_op jit(solution)/shard_map/all_to_all | solution.py:344
  31.4 1.1 %copy-start.2 = (f32[3,256,512]{2,1,0:T(8,128)}, f32[3,256,512]{2,1,0:T(8,128)S(1)}, u32[]{:S(2)}) copy-start(f32[3,256,512]{2,1,0:T(8,128)S(1)} %get-tuple-element.27.tops) | copy-start | bytes 4718596
  34.7 1.4 %copy-start.3 = (f32[3,256,512]{2,1,0:T(8,128)S(1)}, f32[3,256,512]{2,1,0:T(8,128)}, u32[]{:S(2)}) copy-start(f32[3,256,512]{2,1,0:T(8,128)} %copy-done.2) | copy-start | bytes 4718596
  37.3 2.4 %collective-permute-start.5 = (f32[384,512]{1,0:T(8,128)S(1)}, f32[384,512]{1,0:T(8,128)S(1)}, u32[]{:S(2)}, u32[]{:S(2)}) collective-permute-start(f32[384,512]{1,0:T(8,128)S(1)} %get-tuple-element.31.packed), channel_id=1, source_target_pairs={{0,8},{8,0},{16,24},{24,16},{1,9},{9,1},{17,25},{25,17},{2,10},{10... | collective-permute-start | bytes 2359304 | tf_op jit(solution)/shard_map/ppermute | solution.py:54
  39.7 1.3 %copy-start.5 = (f32[264,512]{1,0:T(8,128)S(1)}, f32[264,512]{1,0:T(8,128)}, u32[]{:S(2)}) copy-start(f32[264,512]{1,0:T(8,128)} %get-tuple-element.37) | copy-start | bytes 1622020
  39.7 33.2 %copy-start.1 = (s32[1,2]{1,0:T(1,128)S(1)}, s32[1,2]{1,0:T(1,128)}, u32[]{:S(2)}) copy-start(s32[1,2]{1,0:T(1,128)} %refs_3_.1) | copy-start | bytes 28
  40.4 14.9 %collective-permute-start.6 = (f32[256,512]{1,0:T(8,128)S(1)}, f32[256,512]{1,0:T(8,128)S(1)}, u32[]{:S(2)}, u32[]{:S(2)}) collective-permute-start(f32[256,512]{1,0:T(8,128)S(1)} %get-tuple-element.32.direct), channel_id=1, source_target_pairs={{0,16},{8,24},{16,0},{24,8},{1,17},{9,25},{17,1},{25,9},{2,18},{10... | collective-permute-start | bytes 1572872 | tf_op jit(solution)/shard_map/ppermute | solution.py:54
  41.0 25.4 %collective-permute-start.12 = (f32[264,512]{1,0:T(8,128)S(1)}, f32[264,512]{1,0:T(8,128)S(1)}, u32[]{:S(2)}, u32[]{:S(2)}) collective-permute-start(f32[264,512]{1,0:T(8,128)S(1)} %copy-done.5), channel_id=1, source_target_pairs={{8,0},{24,8},{0,16},{16,24},{9,1},{25,9},{1,17},{17,25},{10,2},{26... | collective-permute-start | bytes 1622024 | tf_op jit(solution)/shard_map/ppermute | solution.py:354
  42.5 30.4 %collective-permute-start.8 = (f32[256,512]{1,0:T(8,128)S(1)}, f32[256,512]{1,0:T(8,128)S(1)}, u32[]{:S(2)}, u32[]{:S(2)}) collective-permute-start(f32[256,512]{1,0:T(8,128)S(1)} %get-tuple-element.32.direct), channel_id=1, source_target_pairs={{0,8},{8,0},{16,24},{24,16},{1,9},{9,1},{17,25},{25,17},{2,10},{10... | collective-permute-start | bytes 1572872 | tf_op jit(solution)/shard_map/ppermute | solution.py:54
  55.2 19.4 %collective-permute-start.7 = (f32[256,512]{1,0:T(8,128)S(1)}, f32[256,512]{1,0:T(8,128)S(1)}, u32[]{:S(2)}, u32[]{:S(2)}) collective-permute-start(f32[256,512]{1,0:T(8,128)S(1)} %collective-permute-done.6.refs_0_), channel_id=1, source_target_pairs={{0,8},{8,0},{16,24},{24,16},{1,9},{9,1},{17,25},{25,17},{2,10},{10... | collective-permute-start | bytes 1572872 | tf_op jit(solution)/shard_map/ppermute | solution.py:54
  55.3 3.6 %collective-permute-start.10 = (f32[1,128]{1,0:T(1,128)S(1)}, f32[1,128]{1,0:T(1,128)S(1)}, u32[]{:S(2)}, u32[]{:S(2)}) collective-permute-start(f32[1,128]{1,0:T(1,128)S(1)} %get-tuple-element.33), channel_id=1, source_target_pairs={{0,16},{8,24},{16,0},{24,8},{1,17},{9,25},{17,1},{25,9},{2,18},{10... | collective-permute-start | bytes 1544 | tf_op jit(solution)/shard_map/ppermute | solution.py:54
  55.3 4.2 %collective-permute-start.11 = (f32[1,128]{1,0:T(1,128)S(1)}, f32[1,128]{1,0:T(1,128)S(1)}, u32[]{:S(2)}, u32[]{:S(2)}) collective-permute-start(f32[1,128]{1,0:T(1,128)S(1)} %get-tuple-element.33), channel_id=1, source_target_pairs={{0,8},{8,0},{16,24},{24,16},{1,9},{9,1},{17,25},{25,17},{2,10},{10... | collective-permute-start | bytes 1544 | tf_op jit(solution)/shard_map/ppermute | solution.py:54
  58.8 3.0 %collective-permute-start.9 = (f32[1,128]{1,0:T(1,128)S(1)}, f32[1,128]{1,0:T(1,128)S(1)}, u32[]{:S(2)}, u32[]{:S(2)}) collective-permute-start(f32[1,128]{1,0:T(1,128)S(1)} %get-tuple-element.33), channel_id=1, source_target_pairs={{0,24},{8,16},{16,8},{24,0},{1,25},{9,17},{17,9},{25,1},{2,26},{10... | collective-permute-start | bytes 1544 | tf_op jit(solution)/shard_map/ppermute | solution.py:54
  62.4 10.4 %all-to-all-start.1 = ((f32[8,1,128]{2,1,0:T(1,128)}), f32[8,1,128]{2,1,0:T(1,128)S(1)}, u32[]{:S(2)}, u32[]{:S(2)}) async-start(f32[8,1,128]{2,1,0:T(1,128)} %broadcast_in_dim.12), calls=%async_computation.1 | async-start | bytes 8192 | tf_op jit(solution)/shard_map/all_to_all | solution.py:379
  66.4 0.8 %copy-start.4 = (f32[264,512]{1,0:T(8,128)}, f32[264,512]{1,0:T(8,128)S(1)}, u32[]{:S(2)}) copy-start(f32[264,512]{1,0:T(8,128)S(1)} %collective-permute-done.12.source) | copy-start | bytes 1622020

commit v5 on v4

--- a/solution.py
+++ b/solution.py
@@ -12,6 +12,7 @@
 BLOCK = 512
 HALF = BLOCK // 2
 PACKED = HALF + 8
+CHUNK = 64
 
 decay_rate = 0.95
 damping = 0.25
@@ -156,11 +157,19 @@
         g[0, rows], g[1, rows] = split(src[...])
 
 
-def update_powers(half, other, old, tops, corners, facts, out, g_out, gg, s1, s2, stage, sems):
+def update_powers(half, other, old, *refs):
+    top_out, corner_out, cube_top, cube_corner, facts, out, g_out = refs[:7]
+    gg, s1, s2, stage, tops, corners, sems = refs[7:]
     _, core = chip_core()
+
+    def store(k):
+        for n, (src, dst) in enumerate(((tops, top_out), (corners, corner_out))):
+            copies.append(pltpu.make_async_copy(src.at[k], dst.at[k], sems.at[2 + 2 * k + n]))
+            copies[-1].start()
+
     load_gradient(core, half, other, gg.at[0])
-    keep = pltpu.make_async_copy(gg.at[0], g_out, sems.at[0])
-    keep.start()
+    copies = [pltpu.make_async_copy(gg.at[0], g_out, sems.at[0])]
+    copies[0].start()
     for k in range(2):
         gg[1, k] = gg[0, k].T
     top, corner = upper_product(gg.at[1 - core], gg.at[core])
@@ -169,20 +178,22 @@
     s01 = decay_rate * old[LOW, TOP] + top[:, HALF:]
     s11 = decay_rate * sc + corner
     pack_into(stage, s00, s01, s11)
-    copy = pltpu.make_async_copy(stage, out, sems.at[1])
-    copy.start()
+    copies.append(pltpu.make_async_copy(stage, out, sems.at[1]))
+    copies[-1].start()
     i, j = triangle()
     trace = total(jnp.where(i == j, s00 + s11, 0.0))
     norm_sq = total(s00 * s00 + s11 * s11 + 2.0 * (s01 * s01))
     inv = 1.0 / jnp.sqrt(norm_sq + epsilon)
     tops[0, :, LOW], tops[0, :, TOP], corners[0] = s00 * inv, s01 * inv, s11 * inv
+    store(0)
     spread(tops[0], corners[0], s1)
     tops[1], corners[1] = upper_product(s1, s1)
+    store(1)
     spread(tops[1], corners[1], s2)
-    tops[2], corners[2] = upper_product(s1, s2)
+    cube_top[...], cube_corner[...] = upper_product(s1, s2)
     facts[...] = jnp.concatenate([jnp.broadcast_to(x, (1, 128)) for x in (norm_sq, trace)], axis=0)
-    keep.wait()
-    copy.wait()
+    for copy in copies:
+        copy.wait()
 
 
 def coefficients(devices, facts, sums):
@@ -205,9 +216,20 @@
     return k, grad_sq
 
 
-def root(devices, tops, corners, facts, sums, out, totals, inner, cube):
+def root(devices, *refs):
+    top_in, corner_in, cube_top, cube_corner, facts, sums, g_in, out, totals, g_out = refs[:10]
+    inner, cube, top_v, corner_v, sems = refs[10:]
+    copies = [
+        pltpu.make_async_copy(src, dst, sems.at[n])
+        for n, (src, dst) in enumerate(((top_in, top_v), (corner_in, corner_v), (g_in, g_out)))
+    ]
+    for copy in copies:
+        copy.start()
     k, grad_sq = coefficients(devices, facts, sums)
-    spread(tops[2], corners[2], cube)
+    spread(cube_top[...], cube_corner[...], cube)
+    for copy in copies[:2]:
+        copy.wait()
+    tops, corners = (top_v[0], top_v[1], cube_top[...]), (corner_v[0], corner_v[1], cube_corner[...])
     spread(*(k[4] * t[0] + k[5] * t[1] + k[6] * t[2] for t in (tops, corners)), inner)
     top, corner = upper_product(cube, inner)
     i, j = triangle()
@@ -219,18 +241,16 @@
     out[HALF:, LOW] = corner[: HALF // 2]
     out[HALF:, TOP] = corner[HALF // 2 :]
     totals[...] = jnp.broadcast_to(grad_sq, (1, 128))
+    copies[2].wait()
 
 
 def root_corner(packed):
     return jnp.concatenate([packed[HALF:, LOW], packed[HALF:, TOP]], axis=0)
 
 
-def half_way(g_in, packed, out, g, x, sem):
+def half_way(g, packed, out, x):
     _, core = chip_core()
-    copy = pltpu.make_async_copy(g_in, g, sem)
-    copy.start()
     spread(packed[LOW], root_corner(packed), x)
-    copy.wait()
 
     @pl.when(core == 1)
     def _():
@@ -254,13 +274,10 @@
     def _():
         mine[...] = dot3(split(packed[LOW]), (middle[0], middle[1]))
 
-    sums[...] = lanes(mine[...] * mine[...])
-
-
-def unpack_stat(source, out, packed, sem):
-    copy = pltpu.make_async_copy(source, packed, sem)
-    copy.start()
-    copy.wait()
+    sums[...] = jnp.broadcast_to(lanes(mine[...] * mine[...])[None], sums.shape)
+
+
+def unpack_stat(packed, out):
     sa, sc = unpack(packed[LOW, LOW], packed[HALF : HALF + 1, LOW])
     off = packed[LOW, TOP]
     out[LOW, LOW] = sa
@@ -272,11 +289,15 @@
 def write_pieces(chip, core, pieces, scale, owners, out, scaled, sems):
     copies = []
     for n, (j, swapped, src) in enumerate(pieces):
-        scaled[n] = src[...] * scale
         half = 1 - core if swapped else core
-        start = pl.multiple_of(owners[0, chip ^ j] * BLOCK + half * HALF, HALF)
-        copies.append(pltpu.make_async_copy(scaled.at[n], out.at[pl.ds(start, HALF)], sems.at[n]))
-        copies[-1].start()
+        base = owners[0, chip ^ j] * BLOCK + half * HALF
+        for r in range(0, HALF, CHUNK):
+            scaled[n, pl.ds(r, CHUNK)] = src[pl.ds(r, CHUNK)] * scale
+            start = pl.multiple_of(base + r, CHUNK)
+            copies.append(
+                pltpu.make_async_copy(scaled.at[n, pl.ds(r, CHUNK)], out.at[pl.ds(start, CHUNK)], sems.at[len(copies)])
+            )
+            copies[-1].start()
     for copy in copies:
         copy.wait()
 
@@ -289,11 +310,10 @@
     write_pieces(chip, core, ((0, False, direct), (0, True, across)), factor, owners, out, scaled, sems)
 
 
-def place_far(count, *refs):
-    direct, across = refs[:count], refs[count : 2 * count]
-    scale, owners, _, out, scaled, sems = refs[2 * count :]
+def place_more(swapped, count, *refs):
+    scale, owners, _, out, scaled, sems = refs[count:]
     chip, core = chip_core()
-    pieces = [(j + 1, False, x) for j, x in enumerate(direct)] + [(j + 1, True, x) for j, x in enumerate(across)]
+    pieces = [(j + 1, swapped, x) for j, x in enumerate(refs[:count])]
     write_pieces(chip, core, pieces, scale[0:1, 0:1], owners, out, scaled, sems)
 
 
@@ -342,28 +362,28 @@
     )(keep_near, got_near, arrived[0], trace)
     other = flip(half, 1)
     sums = lax.all_to_all(sums, AXES, 0, 0)
-    tops, corners, facts, out_packed, g_split = call(
+    *powers, facts, out_packed, g_split = call(
         update_powers,
-        [(3,) + piece, (3, HALF, HALF), (2, 128), pltpu.HBM((PACKED, BLOCK), f32), pltpu.HBM((2,) + square, bf16)],
+        [pltpu.HBM((2,) + piece, f32), pltpu.HBM((2, HALF, HALF), f32), piece, (HALF, HALF), (2, 128)]
+        + [pltpu.HBM((PACKED, BLOCK), f32), pltpu.HBM((2,) + square, bf16)],
         [VMEM] * 3,
-        [pltpu.VMEM((2, 2) + square, bf16), split_square, split_square]
-        + [packed_buffer, pltpu.SemaphoreType.DMA((2,))],
+        [pltpu.VMEM((2, 2) + square, bf16), split_square, split_square, packed_buffer]
+        + [pltpu.VMEM((2,) + piece, f32), pltpu.VMEM((2, HALF, HALF), f32), pltpu.SemaphoreType.DMA((6,))],
         flops=3 * unit,
-        out_specs=[VMEM] * 3 + [HBM] * 2,
+        out_specs=[HBM] * 2 + [VMEM] * 3 + [HBM] * 2,
     )(half, other, old)
     new_packed = lax.ppermute(out_packed, "rep", [(t, s) for s, t in shuffle])
-    mine_root, totals = call(
+    mine_root, totals, g_split = call(
         functools.partial(root, devices),
-        [(HALF + HALF // 2, BLOCK), (1, 128)],
-        [VMEM] * 4,
-        [split_square] * 2,
+        [(HALF + HALF // 2, BLOCK), (1, 128), whole],
+        [HBM] * 2 + [VMEM] * 4 + [HBM],
+        [split_square] * 2
+        + [pltpu.VMEM((2,) + piece, f32), pltpu.VMEM((2, HALF, HALF), f32), pltpu.SemaphoreType.DMA((3,))],
         flops=unit,
-    )(tops, corners, facts, sums)
+    )(in_hbm(powers[0]), in_hbm(powers[1]), powers[2], powers[3], facts, sums, in_hbm(g_split))
     other_root = flip(mine_root, 1)
-    (middle,) = call(half_way, [whole], [HBM, VMEM], [split_square] * 2 + [pltpu.SemaphoreType.DMA], flops=unit)(
-        in_hbm(g_split), mine_root
-    )
-    mine, prec = call(last_product, [piece, (1, 128)], [VMEM] * 2, [split_square], flops=unit)(middle, other_root)
+    (middle,) = call(half_way, [whole], [VMEM] * 2, [split_square], flops=unit)(g_split, mine_root)
+    mine, prec = call(last_product, [piece, (lax.axis_size("stripe"), 1, 128)], [VMEM] * 2, [split_square], flops=unit)(middle, other_root)
 
     bit = 1
     while bit < rep_count:
@@ -375,27 +395,27 @@
         direct = direct + [flip(x, 2 * m) for x in direct]
         m *= 2
     across = [flip(mine, 1)]
-    stripes = lax.axis_size("stripe")
-    prec = lax.all_to_all(jnp.broadcast_to(prec[None], (stripes, 1, 128)), "stripe", 0, 0)
-    (new_stat,) = call(unpack_stat, [square], [HBM], [packed_buffer, pltpu.SemaphoreType.DMA])(in_hbm(new_packed))
+    prec = lax.all_to_all(prec, "stripe", 0, 0)
+    (new_stat,) = call(unpack_stat, [square], [VMEM])(new_packed)
     slab = (pairs * BLOCK, out_grads.shape[1])
+
+    def landing(count):
+        return [pltpu.VMEM((count,) + piece, f32), pltpu.SemaphoreType.DMA((count * HALF // CHUNK,))]
+
     placed, scale = call(
-        place_near,
-        [slab, (1, 128)],
-        [VMEM] * 4 + [SMEM],
-        [pltpu.VMEM((2,) + piece, f32), pltpu.SemaphoreType.DMA((2,))],
-        out_specs=[HBM, VMEM],
+        place_near, [slab, (1, 128)], [VMEM] * 4 + [SMEM], landing(2), out_specs=[HBM, VMEM]
     )(mine, across[0], prec, totals, owner_blocks)
     across = [flip(x, 1) for x in direct[1:]]
     count = pairs - 1
-    (placed,) = call(
-        functools.partial(place_far, count),
-        [slab],
-        [VMEM] * (2 * count + 1) + [SMEM, HBM],
-        [pltpu.VMEM((2 * count,) + piece, f32), pltpu.SemaphoreType.DMA((2 * count,))],
-        out_specs=[HBM],
-        input_output_aliases={2 * count + 2: 0},
-    )(*direct[1:], *across, scale, owner_blocks, placed)
+    for swapped, found in ((False, direct[1:]), (True, across)):
+        (placed,) = call(
+            functools.partial(place_more, swapped, count),
+            [slab],
+            [VMEM] * (count + 1) + [SMEM, HBM],
+            landing(count),
+            out_specs=[HBM],
+            input_output_aliases={count + 2: 0},
+        )(*found, scale, owner_blocks, placed)
     return placed, new_stat[None, None]
 
 

time: 76.6 us -> 75.2 us (0.982)
  local copies, waits for them, and re-layouts: 3.95 us -> 0.01 us
  waiting for transfers between devices: 36.1 us -> 39.4 us
  starting transfers between devices: 18 us -> 16.7 us
    unnamed x12 -> x6, local copies, waits for them, and re-layouts: 3.35 us -> 0.01 us
    all_to_all x1, waiting for transfers between devices: 3.45 us -> 5.17 us  [per_device(): prec = lax.all_to_all(prec, 'stripe', 0, 0)]
    all_to_all x1, waiting for transfers between devices: 2.19 us -> 3.68 us  [per_device(): sums = lax.all_to_all(sums, AXES, 0, 0)]
    pallas_call x6 -> x7, Pallas kernels: 12.3 us -> 11.1 us  [the longest x1 3.48 us: per_device(): call(update_powers, [pltpu.HBM((2,) + piece, f32), pltpu.HBM((2, HALF, HA...]
    pallas_call x1, Pallas kernels: 1.17 us -> 2.35 us  [per_device(): call(functools.partial(root, devices), [(HALF + HALF // 2, BLOCK), (1, 12...]
  transfers between devices with their start and end apart: 15 -> 15, of which waited for: 6 -> 8; matrix products, arithmetic and copies ran while one was open for 1% -> 1% of each run, Pallas kernels for 16% -> 15%
where the time goes in v5:
time: 75.2 us; the launch traced here: 74.9 us
  waiting for transfers between devices  39.4 us (52%)
  Pallas kernels  17.3 us (23%)
  starting transfers between devices  16.7 us (22%)
  between operations  0.8 us (1%)
    ppermute x11, waiting for transfers between devices, flip(): lax.ppermute(x, 'rep', [(i, i ^ mask) for i in range(lax.axis_size('rep'))])  30.5 us
    all_to_all x1, starting transfers between devices, per_device(): sums = lax.all_to_all(sums, AXES, 0, 0)  6.95 us
    all_to_all x1, waiting for transfers between devices, per_device(): prec = lax.all_to_all(prec, 'stripe', 0, 0)  5.17 us
    ppermute x11, starting transfers between devices, flip(): lax.ppermute(x, 'rep', [(i, i ^ mask) for i in range(lax.axis_size('rep'))])  5.05 us
    all_to_all x1, waiting for transfers between devices, per_device(): sums = lax.all_to_all(sums, AXES, 0, 0)  3.68 us
    pallas_call x1, Pallas kernels, per_device(): call(update_powers, [pltpu.HBM((2,) + piece, f32), pltpu.HBM((2, HALF, HA...  3.48 us
    all_to_all x1, starting transfers between devices, per_device(): prec = lax.all_to_all(prec, 'stripe', 0, 0)  3.31 us
    pallas_call x2, Pallas kernels, terms(): call(functools.partial(grad_terms, plan), [(len(chips),) + piece for chip...  3.04 us
  transfers between devices with their start and end apart: 15, of which 8 were waited for; matrix products, arithmetic and copies ran while one was open for 1% of the time, Pallas kernels for 15%

profile of v5, /device:TPU:0, one launch (start us, length us, event | category | flops | bytes accessed | tf_op | source)
XLA Modules:
  0.0 74.9 jit_solution(14780300675219590229)
XLA Ops:
  0.6 1.5 %shard_map.60 = f32[1,256,512]{2,1,0:T(8,128)S(1)} custom-call(bf16[256,1024]{1,0:T(8,128)(2,1)} %acts.3, bf16[256,512]{1,0:T(8,128)(2,1)} %grads.3, s32[1,2]{1,0:T(1,128)} %refs_2_.3), custom_call_target="tpu_custom_call" | custom-call | flops 67108864 | bytes 1048576 | tf_op jit(solution)/shard_map/pallas_call | solution.py:334
  2.7 1.5 %shard_map.59 = (f32[1,256,512]{2,1,0:T(8,128)S(1)}, f32[1,256,512]{2,1,0:T(8,128)S(1)}, f32[1,256,512]{2,1,0:T(8,128)S(1)}) custom-call(bf16[256,1024]{1,0:T(8,128)(2,1)} %acts.3, bf16[256,512]{1,0:T(8,128)(2,1)} %grads.3, s32[1,2]{1,0:T(1,128)} %refs_2_.3), custom_call_target="tpu_custom_call" | custom-call | flops 201326592 | bytes 1048576 | tf_op jit(solution)/shard_map/pallas_call | solution.py:334
  4.4 3.0 %collective-permute-start.2 = (f32[256,512]{1,0:T(8,128)S(1)}, f32[256,512]{1,0:T(8,128)S(1)}, u32[]{:S(2)}, u32[]{:S(2)}) collective-permute-start(f32[256,512]{1,0:T(8,128)S(1)} %add_bitcast_fusion), channel_id=1, source_target_pairs={{0,16},{8,24},{16,0},{24,8},{1,17},{9,25},{17,1},{25,9},{2,18},{10... | collective-permute-start | bytes 1572872 | tf_op jit(solution)/shard_map/ppermute | solution.py:55
  7.6 12.2 %collective-permute-done.2.rest = f32[256,512]{1,0:T(8,128)S(1)} collective-permute-done((f32[256,512]{1,0:T(8,128)S(1)}, f32[256,512]{1,0:T(8,128)S(1)}, u32[]{:S(2)}, u32[]{:S(2)}) %collective-permute-start.2) | collective-permute-done | bytes 524320 | tf_op jit(solution)/shard_map/ppermute | solution.py:55
  19.8 0.8 %shard_map.62 = (f32[256,512]{1,0:T(8,128)S(1)}, f32[32,2,128]{2,1,0:T(2,128)}) custom-call(f32[1,256,512]{2,1,0:T(8,128)S(1)} %get-tuple-element.23.keep, f32[1,256,512]{2,1,0:T(8,128)S(1)} %collective-permute-done.got, f32[256,512]{1,0:T(8,128)S(1)} %collective-permute-done.2.rest, f32[1,128]{1,0:T(1,128)S(1)} %get-tuple-element.26.trace), custom_call_target="tpu_custom_call" | custom-call | bytes 1048576 | tf_op jit(solution)/shard_map/pallas_call | solution.py:360
  20.5 7.0 %all-to-all-start = ((f32[32,2,128]{2,1,0:T(2,128)}), f32[32,2,128]{2,1,0:T(2,128)S(1)}, u32[]{:S(2)}, u32[]{:S(2)}) async-start(f32[32,2,128]{2,1,0:T(2,128)} %get-tuple-element.34), calls=%async_computation | async-start | bytes 65536 | tf_op jit(solution)/shard_map/all_to_all | solution.py:364
  27.5 3.5 %shard_map.63 = (f32[2,256,512]{2,1,0:T(8,128)}, f32[2,256,256]{2,1,0:T(8,128)}, f32[256,512]{1,0:T(8,128)S(1)}, f32[256,256]{1,0:T(8,128)S(1)}, f32[2,128]{1,0:...) custom-call(f32[256,512]{1,0:T(8,128)S(1)} %get-tuple-element.27.half, ...), custom_call_target="tpu_custom_call" | custom-call | flops 2415919104 | bytes 1048576 | tf_op jit(solution)/shard_map/pallas_call | solution.py:365
  31.0 3.7 %all-to-all-done.refs_5_ = f32[32,2,128]{2,1,0:T(2,128)S(1)} async-done(((f32[32,2,128]{2,1,0:T(2,128)}), f32[32,2,128]{2,1,0:T(2,128)S(1)}, u32[]{:S(2)}, u32[]{:S(2)}) %all-to-all-start) | async-done | bytes 32800 | tf_op jit(solution)/shard_map/all_to_all | solution.py:364
  34.7 2.4 %shard_map.64 = (f32[384,512]{1,0:T(8,128)S(1)}, f32[1,128]{1,0:T(1,128)S(1)}, bf16[2,512,512]{2,1,0:T(8,128)(2,1)S(1)}) custom-call(f32[2,256,512]{2,1,0:T(8,128)} %get-tuple-element.29.refs_0_, f32[2,256,256]{2,1,0:T(8,128)} %get-tuple-element.30.refs_1_, f32[256,512]{1,0:T(8,128)S(1)} %get-tuple-element.31.refs_2_, ...), custom_call_target="tpu_custom_call" | custom-call | flops 805306368 | bytes 1048576 | tf_op jit(solution)/shard_map/pallas_call | solution.py:376
  37.2 1.2 %shard_map.65.middle = bf16[2,512,512]{2,1,0:T(8,128)(2,1)S(1)} custom-call(bf16[2,512,512]{2,1,0:T(8,128)(2,1)S(1)} %get-tuple-element.36.g, f32[384,512]{1,0:T(8,128)S(1)} %get-tuple-element.37.packed), custom_call_target="tpu_custom_call" | custom-call | flops 805306368 | bytes 1048576 | tf_op jit(solution)/shard_map/pallas_call | solution.py:385
  38.4 1.0 %collective-permute-done.5.packed = f32[384,512]{1,0:T(8,128)S(1)} collective-permute-done((f32[384,512]{1,0:T(8,128)S(1)}, f32[384,512]{1,0:T(8,128)S(1)}, u32[]{:S(2)}, u32[]{:S(2)}) %collective-permute-start.5) | collective-permute-done | bytes 786464 | tf_op jit(solution)/shard_map/ppermute | solution.py:55
  39.4 0.6 shard_map.66
  40.0 0.7 collective-permute-start.6
  40.7 1.4 %collective-permute-start.12 = (f32[264,512]{1,0:T(8,128)S(1)}, f32[264,512]{1,0:T(8,128)S(1)}, u32[]{:S(2)}, u32[]{:S(2)}) collective-permute-start(f32[264,512]{1,0:T(8,128)S(1)} %copy-done.2), channel_id=1, source_target_pairs={{8,0},{24,8},{0,16},{16,24},{9,1},{25,9},{1,17},{17,25},{10,2},{26... | collective-permute-start | bytes 1622024 | tf_op jit(solution)/shard_map/ppermute | solution.py:375
  42.1 12.8 %collective-permute-done.6.refs_0_ = f32[256,512]{1,0:T(8,128)S(1)} collective-permute-done((f32[256,512]{1,0:T(8,128)S(1)}, f32[256,512]{1,0:T(8,128)S(1)}, u32[]{:S(2)}, u32[]{:S(2)}) %collective-permute-start.6) | collective-permute-done | bytes 524320 | tf_op jit(solution)/shard_map/ppermute | solution.py:55
  55.4 1.4 %collective-permute-done.11 = f32[8,1,128]{2,1,0:T(1,128)S(1)} collective-permute-done((f32[8,1,128]{2,1,0:T(1,128)S(1)}, f32[8,1,128]{2,1,0:T(1,128)S(1)}, u32[]{:S(2)}, u32[]{:S(2)}) %collective-permute-start.11) | collective-permute-done | bytes 4128 | tf_op jit(solution)/shard_map/ppermute | solution.py:55
  56.8 2.2 %collective-permute-done.10 = f32[8,1,128]{2,1,0:T(1,128)S(1)} collective-permute-done((f32[8,1,128]{2,1,0:T(1,128)S(1)}, f32[8,1,128]{2,1,0:T(1,128)S(1)}, u32[]{:S(2)}, u32[]{:S(2)}) %collective-permute-start.10) | collective-permute-done | bytes 4128 | tf_op jit(solution)/shard_map/ppermute | solution.py:55
  59.1 0.9 %collective-permute-done.9 = f32[8,1,128]{2,1,0:T(1,128)S(1)} collective-permute-done((f32[8,1,128]{2,1,0:T(1,128)S(1)}, f32[8,1,128]{2,1,0:T(1,128)S(1)}, u32[]{:S(2)}, u32[]{:S(2)}) %collective-permute-start.9) | collective-permute-done | bytes 4128 | tf_op jit(solution)/shard_map/ppermute | solution.py:55
  60.6 3.3 %all-to-all-start.1 = ((f32[8,1,128]{2,1,0:T(1,128)}), f32[8,1,128]{2,1,0:T(1,128)S(1)}, u32[]{:S(2)}, u32[]{:S(2)}) async-start(f32[8,1,128]{2,1,0:T(1,128)} %bitcast.8), calls=%async_computation.1 | async-start | bytes 8192 | tf_op jit(solution)/shard_map/all_to_all | solution.py:398
  63.9 1.2 %shard_map.70 = f32[512,512]{1,0:T(8,128)} custom-call(f32[264,512]{1,0:T(8,128)S(1)} %collective-permute-done.12.packed), custom_call_target="tpu_custom_call" | custom-call | bytes 1048576 | tf_op jit(solution)/shard_map/pallas_call | solution.py:399
  65.1 5.2 %all-to-all-done.1.sums = f32[8,1,128]{2,1,0:T(1,128)S(1)} async-done(((f32[8,1,128]{2,1,0:T(1,128)}), f32[8,1,128]{2,1,0:T(1,128)S(1)}, u32[]{:S(2)}, u32[]{:S(2)}) %all-to-all-start.1) | async-done | bytes 4128 | tf_op jit(solution)/shard_map/all_to_all | solution.py:398
  70.3 1.8 %shard_map.67 = (f32[1024,512]{1,0:T(8,128)}, f32[1,128]{1,0:T(1,128)S(1)}) custom-call(f32[256,512]{1,0:T(8,128)S(1)} %get-tuple-element.38.direct, f32[256,512]{1,0:T(8,128)S(1)} %collective-permute-done.8.across, f32[8,1,128]{2,1,0:T(1,128)S(1)} %all-to-all-done.1.sums, f32[1,128]{1,0:T(1,128)S(1)} %get-tuple-element.40.totals, s32[1,2]{1,0:T(1,128)S(1)} %copy-done.1), custom_call_target="tpu_custom_call" | custom-call | bytes 1048576 | tf_op jit(solution)/shard_map/pallas_call | solution.py:405
  72.0 1.4 %shard_map.68.refs_3_ = f32[1024,512]{1,0:T(8,128)} custom-call(f32[256,512]{1,0:T(8,128)S(1)} %collective-permute-done.6.refs_0_, f32[1,128]{1,0:T(1,128)S(1)} %get-tuple-element.41.refs_1_, s32[1,2]{1,0:T(1,128)S(1)} %copy-done.1, f32[1024,512]{1,0:T(8,128)} %get-tuple-element.42.refs_3_), custom_call_target="tpu_custom_call", output_to_operand_aliasing={{}: (3, {})} | custom-call | bytes 1048576 | tf_op jit(solution)/shard_map/pallas_call | solution.py:411
  73.5 1.4 %shard_map.69 = f32[1024,512]{1,0:T(8,128)} custom-call(f32[256,512]{1,0:T(8,128)S(1)} %collective-permute-done.7.refs_0_, f32[1,128]{1,0:T(1,128)S(1)} %get-tuple-element.41.refs_1_, s32[1,2]{1,0:T(1,128)S(1)} %copy-done.1, f32[1024,512]{1,0:T(8,128)} %shard_map.68.refs_3_), custom_call_target="tpu_custom_call", output_to_operand_aliasing={{}: (3, {})} | custom-call | bytes 1048576 | tf_op jit(solution)/shard_map/pallas_call | solution.py:411
  (26 shorter events, 2.1 us)
Async XLA Ops:
  0.6 6.8 %copy-start = (f32[1,1,512,512]{3,2,1,0:T(8,128)S(1)}, f32[1,1,512,512]{3,2,1,0:T(8,128)}, u32[]{:S(2)}) copy-start(f32[1,1,512,512]{3,2,1,0:T(8,128)} %param.6) | copy-start | bytes 3145732
  2.1 2.2 %collective-permute-start.1 = (f32[1,256,512]{2,1,0:T(8,128)S(1)}, f32[1,256,512]{2,1,0:T(8,128)S(1)}, u32[]{:S(2)}, u32[]{:S(2)}) collective-permute-start(f32[1,256,512]{2,1,0:T(8,128)S(1)} %shard_map.60), channel_id=1, source_target_pairs={{0,8},{8,0},{16,24},{24,16},{1,9},{9,1},{17,25},{25,17},{2,10},{10... | collective-permute-start | bytes 1572872 | tf_op jit(solution)/shard_map/ppermute | solution.py:55
  4.2 3.3 %collective-permute-start = (f32[1,256,512]{2,1,0:T(8,128)S(1)}, f32[1,256,512]{2,1,0:T(8,128)S(1)}, u32[]{:S(2)}, u32[]{:S(2)}) collective-permute-start(f32[1,256,512]{2,1,0:T(8,128)S(1)} %get-tuple-element.24), channel_id=1, source_target_pairs={{0,8},{8,0},{16,24},{24,16},{1,9},{9,1},{17,25},{25,17},{2,10},{10... | collective-permute-start | bytes 1572872 | tf_op jit(solution)/shard_map/ppermute | solution.py:55
  4.4 15.3 %collective-permute-start.2 = (f32[256,512]{1,0:T(8,128)S(1)}, f32[256,512]{1,0:T(8,128)S(1)}, u32[]{:S(2)}, u32[]{:S(2)}) collective-permute-start(f32[256,512]{1,0:T(8,128)S(1)} %add_bitcast_fusion), channel_id=1, source_target_pairs={{0,16},{8,24},{16,0},{24,8},{1,17},{9,25},{17,1},{25,9},{2,18},{10... | collective-permute-start | bytes 1572872 | tf_op jit(solution)/shard_map/ppermute | solution.py:55
  7.5 20.0 %collective-permute-start.4 = (f32[264,512]{1,0:T(8,128)S(1)}, f32[264,512]{1,0:T(8,128)S(1)}, u32[]{:S(2)}, u32[]{:S(2)}) collective-permute-start(f32[264,512]{1,0:T(8,128)S(1)} %get-tuple-element.28), channel_id=1, source_target_pairs={{0,8},{8,24},{16,0},{24,16},{1,9},{9,25},{17,1},{25,17},{2,10},{10... | collective-permute-start | bytes 1622024 | tf_op jit(solution)/shard_map/ppermute | solution.py:359
  20.5 7.0 %collective-permute-start.3 = (f32[256,512]{1,0:T(8,128)S(1)}, f32[256,512]{1,0:T(8,128)S(1)}, u32[]{:S(2)}, u32[]{:S(2)}) collective-permute-start(f32[256,512]{1,0:T(8,128)S(1)} %get-tuple-element.27.half), channel_id=1, source_target_pairs={{0,8},{8,0},{16,24},{24,16},{1,9},{9,1},{17,25},{25,17},{2,10},{10... | collective-permute-start | bytes 1572872 | tf_op jit(solution)/shard_map/ppermute | solution.py:55
  20.5 14.2 %all-to-all-start = ((f32[32,2,128]{2,1,0:T(2,128)}), f32[32,2,128]{2,1,0:T(2,128)S(1)}, u32[]{:S(2)}, u32[]{:S(2)}) async-start(f32[32,2,128]{2,1,0:T(2,128)} %get-tuple-element.34), calls=%async_computation | async-start | bytes 65536 | tf_op jit(solution)/shard_map/all_to_all | solution.py:364
  37.0 2.4 %collective-permute-start.5 = (f32[384,512]{1,0:T(8,128)S(1)}, f32[384,512]{1,0:T(8,128)S(1)}, u32[]{:S(2)}, u32[]{:S(2)}) collective-permute-start(f32[384,512]{1,0:T(8,128)S(1)} %get-tuple-element.37.packed), channel_id=1, source_target_pairs={{0,8},{8,0},{16,24},{24,16},{1,9},{9,1},{17,25},{25,17},{2,10},{10... | collective-permute-start | bytes 2359304 | tf_op jit(solution)/shard_map/ppermute | solution.py:55
  38.4 2.3 %copy-start.2 = (f32[264,512]{1,0:T(8,128)S(1)}, f32[264,512]{1,0:T(8,128)}, u32[]{:S(2)}) copy-start(f32[264,512]{1,0:T(8,128)} %get-tuple-element.43) | copy-start | bytes 1622020
  38.4 31.9 %copy-start.1 = (s32[1,2]{1,0:T(1,128)S(1)}, s32[1,2]{1,0:T(1,128)}, u32[]{:S(2)}) copy-start(s32[1,2]{1,0:T(1,128)} %refs_2_.3) | copy-start | bytes 28
  40.0 14.9 %collective-permute-start.6 = (f32[256,512]{1,0:T(8,128)S(1)}, f32[256,512]{1,0:T(8,128)S(1)}, u32[]{:S(2)}, u32[]{:S(2)}) collective-permute-start(f32[256,512]{1,0:T(8,128)S(1)} %get-tuple-element.38.direct), channel_id=1, source_target_pairs={{0,16},{8,24},{16,0},{24,8},{1,17},{9,25},{17,1},{25,9},{2,18},{10... | collective-permute-start | bytes 1572872 | tf_op jit(solution)/shard_map/ppermute | solution.py:55
  40.7 23.2 %collective-permute-start.12 = (f32[264,512]{1,0:T(8,128)S(1)}, f32[264,512]{1,0:T(8,128)S(1)}, u32[]{:S(2)}, u32[]{:S(2)}) collective-permute-start(f32[264,512]{1,0:T(8,128)S(1)} %copy-done.2), channel_id=1, source_target_pairs={{8,0},{24,8},{0,16},{16,24},{9,1},{25,9},{1,17},{17,25},{10,2},{26... | collective-permute-start | bytes 1622024 | tf_op jit(solution)/shard_map/ppermute | solution.py:375
  42.1 28.1 %collective-permute-start.8 = (f32[256,512]{1,0:T(8,128)S(1)}, f32[256,512]{1,0:T(8,128)S(1)}, u32[]{:S(2)}, u32[]{:S(2)}) collective-permute-start(f32[256,512]{1,0:T(8,128)S(1)} %get-tuple-element.38.direct), channel_id=1, source_target_pairs={{0,8},{8,0},{16,24},{24,16},{1,9},{9,1},{17,25},{25,17},{2,10},{10... | collective-permute-start | bytes 1572872 | tf_op jit(solution)/shard_map/ppermute | solution.py:55
  54.9 18.6 %collective-permute-start.7 = (f32[256,512]{1,0:T(8,128)S(1)}, f32[256,512]{1,0:T(8,128)S(1)}, u32[]{:S(2)}, u32[]{:S(2)}) collective-permute-start(f32[256,512]{1,0:T(8,128)S(1)} %collective-permute-done.6.refs_0_), channel_id=1, source_target_pairs={{0,8},{8,0},{16,24},{24,16},{1,9},{9,1},{17,25},{25,17},{2,10},{10... | collective-permute-start | bytes 1572872 | tf_op jit(solution)/shard_map/ppermute | solution.py:55
  54.9 1.9 %collective-permute-start.11 = (f32[8,1,128]{2,1,0:T(1,128)S(1)}, f32[8,1,128]{2,1,0:T(1,128)S(1)}, u32[]{:S(2)}, u32[]{:S(2)}) collective-permute-start(f32[8,1,128]{2,1,0:T(1,128)S(1)} %get-tuple-element.39), channel_id=1, source_target_pairs={{0,8},{8,0},{16,24},{24,16},{1,9},{9,1},{17,25},{25,17},{2,10},{10... | collective-permute-start | bytes 12296 | tf_op jit(solution)/shard_map/ppermute | solution.py:55
  55.4 3.6 %collective-permute-start.10 = (f32[8,1,128]{2,1,0:T(1,128)S(1)}, f32[8,1,128]{2,1,0:T(1,128)S(1)}, u32[]{:S(2)}, u32[]{:S(2)}) collective-permute-start(f32[8,1,128]{2,1,0:T(1,128)S(1)} %get-tuple-element.39), channel_id=1, source_target_pairs={{0,16},{8,24},{16,0},{24,8},{1,17},{9,25},{17,1},{25,9},{2,18},{10... | collective-permute-start | bytes 12296 | tf_op jit(solution)/shard_map/ppermute | solution.py:55
  56.8 3.2 %collective-permute-start.9 = (f32[8,1,128]{2,1,0:T(1,128)S(1)}, f32[8,1,128]{2,1,0:T(1,128)S(1)}, u32[]{:S(2)}, u32[]{:S(2)}) collective-permute-start(f32[8,1,128]{2,1,0:T(1,128)S(1)} %get-tuple-element.39), channel_id=1, source_target_pairs={{0,24},{8,16},{16,8},{24,0},{1,25},{9,17},{17,9},{25,1},{2,26},{10... | collective-permute-start | bytes 12296 | tf_op jit(solution)/shard_map/ppermute | solution.py:55
  60.6 9.7 %all-to-all-start.1 = ((f32[8,1,128]{2,1,0:T(1,128)}), f32[8,1,128]{2,1,0:T(1,128)S(1)}, u32[]{:S(2)}, u32[]{:S(2)}) async-start(f32[8,1,128]{2,1,0:T(1,128)} %bitcast.8), calls=%async_computation.1 | async-start | bytes 8192 | tf_op jit(solution)/shard_map/all_to_all | solution.py:398

commit v6 on v5

--- a/solution.py
+++ b/solution.py
@@ -157,43 +157,24 @@
         g[0, rows], g[1, rows] = split(src[...])
 
 
-def update_powers(half, other, old, *refs):
-    top_out, corner_out, cube_top, cube_corner, facts, out, g_out = refs[:7]
-    gg, s1, s2, stage, tops, corners, sems = refs[7:]
+def update_stat(half, other, old, facts, out, g_out, g, sem):
     _, core = chip_core()
-
-    def store(k):
-        for n, (src, dst) in enumerate(((tops, top_out), (corners, corner_out))):
-            copies.append(pltpu.make_async_copy(src.at[k], dst.at[k], sems.at[2 + 2 * k + n]))
-            copies[-1].start()
-
-    load_gradient(core, half, other, gg.at[0])
-    copies = [pltpu.make_async_copy(gg.at[0], g_out, sems.at[0])]
-    copies[0].start()
+    load_gradient(core, half, other, g.at[0])
+    copy = pltpu.make_async_copy(g.at[0], g_out, sem)
+    copy.start()
     for k in range(2):
-        gg[1, k] = gg[0, k].T
-    top, corner = upper_product(gg.at[1 - core], gg.at[core])
+        g[1, k] = g[0, k].T
+    top, corner = upper_product(g.at[1 - core], g.at[core])
     sa, sc = unpack(old[LOW, LOW], old[HALF : HALF + 1, LOW])
     s00 = decay_rate * sa + top[:, :HALF]
     s01 = decay_rate * old[LOW, TOP] + top[:, HALF:]
     s11 = decay_rate * sc + corner
-    pack_into(stage, s00, s01, s11)
-    copies.append(pltpu.make_async_copy(stage, out, sems.at[1]))
-    copies[-1].start()
+    pack_into(out, s00, s01, s11)
     i, j = triangle()
     trace = total(jnp.where(i == j, s00 + s11, 0.0))
     norm_sq = total(s00 * s00 + s11 * s11 + 2.0 * (s01 * s01))
-    inv = 1.0 / jnp.sqrt(norm_sq + epsilon)
-    tops[0, :, LOW], tops[0, :, TOP], corners[0] = s00 * inv, s01 * inv, s11 * inv
-    store(0)
-    spread(tops[0], corners[0], s1)
-    tops[1], corners[1] = upper_product(s1, s1)
-    store(1)
-    spread(tops[1], corners[1], s2)
-    cube_top[...], cube_corner[...] = upper_product(s1, s2)
     facts[...] = jnp.concatenate([jnp.broadcast_to(x, (1, 128)) for x in (norm_sq, trace)], axis=0)
-    for copy in copies:
-        copy.wait()
+    copy.wait()
 
 
 def coefficients(devices, facts, sums):
@@ -216,20 +197,17 @@
     return k, grad_sq
 
 
-def root(devices, *refs):
-    top_in, corner_in, cube_top, cube_corner, facts, sums, g_in, out, totals, g_out = refs[:10]
-    inner, cube, top_v, corner_v, sems = refs[10:]
-    copies = [
-        pltpu.make_async_copy(src, dst, sems.at[n])
-        for n, (src, dst) in enumerate(((top_in, top_v), (corner_in, corner_v), (g_in, g_out)))
-    ]
-    for copy in copies:
-        copy.start()
+def root(devices, stat, facts, sums, out, totals, first, inner, cube):
     k, grad_sq = coefficients(devices, facts, sums)
-    spread(cube_top[...], cube_corner[...], cube)
-    for copy in copies[:2]:
-        copy.wait()
-    tops, corners = (top_v[0], top_v[1], cube_top[...]), (corner_v[0], corner_v[1], cube_corner[...])
+    inv = 1.0 / jnp.sqrt(facts[0:1, 0:1] + epsilon)
+    s00, s11 = unpack(stat[LOW, LOW], stat[HALF : HALF + 1, LOW])
+    tops, corners = [jnp.concatenate([s00, stat[LOW, TOP]], axis=1) * inv], [s11 * inv]
+    spread(tops[0], corners[0], first)
+    for x in (first, inner):
+        top, corner = upper_product(first, x)
+        tops.append(top)
+        corners.append(corner)
+        spread(top, corner, inner if x is first else cube)
     spread(*(k[4] * t[0] + k[5] * t[1] + k[6] * t[2] for t in (tops, corners)), inner)
     top, corner = upper_product(cube, inner)
     i, j = triangle()
@@ -241,7 +219,6 @@
     out[HALF:, LOW] = corner[: HALF // 2]
     out[HALF:, TOP] = corner[HALF // 2 :]
     totals[...] = jnp.broadcast_to(grad_sq, (1, 128))
-    copies[2].wait()
 
 
 def root_corner(packed):
@@ -286,11 +263,9 @@
     out[TOP, TOP] = sc
 
 
-def write_pieces(chip, core, pieces, scale, owners, out, scaled, sems):
+def write_pieces(pieces, scale, out, scaled, sems):
     copies = []
-    for n, (j, swapped, src) in enumerate(pieces):
-        half = 1 - core if swapped else core
-        base = owners[0, chip ^ j] * BLOCK + half * HALF
+    for n, (base, src) in enumerate(pieces):
         for r in range(0, HALF, CHUNK):
             scaled[n, pl.ds(r, CHUNK)] = src[pl.ds(r, CHUNK)] * scale
             start = pl.multiple_of(base + r, CHUNK)
@@ -302,19 +277,26 @@
         copy.wait()
 
 
-def place_near(direct, across, sums, totals, owners, out, scale, scaled, sems):
+def place_near(pairs, direct, across, sums, totals, owners, out, facts, scaled, sems):
     chip, core = chip_core()
     prec_sq = jnp.sum(jnp.sum(sums[...], axis=0), axis=1, keepdims=True)
-    factor = jnp.sqrt(totals[0:1, 0:1] / (prec_sq + epsilon))
-    scale[...] = jnp.broadcast_to(factor, (1, 128))
-    write_pieces(chip, core, ((0, False, direct), (0, True, across)), factor, owners, out, scaled, sems)
+    scale = jnp.sqrt(totals[0:1, 0:1] / (prec_sq + epsilon))
+    facts[0:1, :] = jnp.broadcast_to(scale, (1, 128))
+    rows = [
+        [owners[0, lax.bitwise_xor(chip, jnp.int32(j))] * BLOCK + half * HALF for j in range(pairs)]
+        for half in (core, 1 - core)
+    ]
+    for n, row in enumerate(rows[0][1:] + rows[1][1:]):
+        facts[n + 1 : n + 2, :] = jnp.full((1, 128), row.astype(f32))
+    write_pieces(((rows[0][0], direct), (rows[1][0], across)), scale, out, scaled, sems)
 
 
 def place_more(swapped, count, *refs):
-    scale, owners, _, out, scaled, sems = refs[count:]
-    chip, core = chip_core()
-    pieces = [(j + 1, swapped, x) for j, x in enumerate(refs[:count])]
-    write_pieces(chip, core, pieces, scale[0:1, 0:1], owners, out, scaled, sems)
+    facts, _, out, scaled, sems = refs[count:]
+    pieces = [
+        (jnp.max(facts[n : n + 1, :]).astype(jnp.int32), x) for n, x in enumerate(refs[:count], 1 + swapped * count)
+    ]
+    write_pieces(pieces, facts[0:1, 0:1], out, scaled, sems)
 
 
 def per_device(activations, out_grads, statistics, owner_blocks):
@@ -327,7 +309,6 @@
 
     whole = jax.ShapeDtypeStruct((2,) + square, bf16)
     split_square = pltpu.VMEM((2,) + square, bf16)
-    packed_buffer = pltpu.VMEM((PACKED, BLOCK), f32)
     m = pairs // 2
 
     def terms(*plan):
@@ -344,10 +325,10 @@
             flops=2 * tokens * HALF * BLOCK * sum(len(chips) for chips, _ in plan),
         )(*(in_hbm(x) for x in (activations, out_grads, owner_blocks)))
 
-    upper, lower = range(m, pairs), range(m)
-    (send_far,) = terms((upper, True))
+    above, below = range(m, pairs), range(m)
+    (send_far,) = terms((above, True))
     got_far = flip(send_far, 1)
-    keep_far, send_near, keep_near = terms((upper, False), (lower, True), (lower, False))
+    keep_far, send_near, keep_near = terms((above, False), (below, True), (below, False))
     got_near = flip(send_near, 1)
     arrived = [flip(keep_far[j] + got_far[j], 2 * m) for j in range(m)]
     while m > 1:
@@ -362,25 +343,22 @@
     )(keep_near, got_near, arrived[0], trace)
     other = flip(half, 1)
     sums = lax.all_to_all(sums, AXES, 0, 0)
-    *powers, facts, out_packed, g_split = call(
-        update_powers,
-        [pltpu.HBM((2,) + piece, f32), pltpu.HBM((2, HALF, HALF), f32), piece, (HALF, HALF), (2, 128)]
-        + [pltpu.HBM((PACKED, BLOCK), f32), pltpu.HBM((2,) + square, bf16)],
+    facts, out_packed, g_split = call(
+        update_stat,
+        [(2, 128), (PACKED, BLOCK), pltpu.HBM((2,) + square, bf16)],
         [VMEM] * 3,
-        [pltpu.VMEM((2, 2) + square, bf16), split_square, split_square, packed_buffer]
-        + [pltpu.VMEM((2,) + piece, f32), pltpu.VMEM((2, HALF, HALF), f32), pltpu.SemaphoreType.DMA((6,))],
-        flops=3 * unit,
-        out_specs=[HBM] * 2 + [VMEM] * 3 + [HBM] * 2,
+        [pltpu.VMEM((2, 2) + square, bf16), pltpu.SemaphoreType.DMA],
+        flops=unit,
+        out_specs=[VMEM] * 2 + [HBM],
     )(half, other, old)
     new_packed = lax.ppermute(out_packed, "rep", [(t, s) for s, t in shuffle])
-    mine_root, totals, g_split = call(
+    mine_root, totals = call(
         functools.partial(root, devices),
-        [(HALF + HALF // 2, BLOCK), (1, 128), whole],
-        [HBM] * 2 + [VMEM] * 4 + [HBM],
-        [split_square] * 2
-        + [pltpu.VMEM((2,) + piece, f32), pltpu.VMEM((2, HALF, HALF), f32), pltpu.SemaphoreType.DMA((3,))],
-        flops=unit,
-    )(in_hbm(powers[0]), in_hbm(powers[1]), powers[2], powers[3], facts, sums, in_hbm(g_split))
+        [(HALF + HALF // 2, BLOCK), (1, 128)],
+        [VMEM] * 3,
+        [split_square] * 3,
+        flops=3 * unit,
+    )(out_packed, facts, sums)
     other_root = flip(mine_root, 1)
     (middle,) = call(half_way, [whole], [VMEM] * 2, [split_square], flops=unit)(g_split, mine_root)
     mine, prec = call(last_product, [piece, (lax.axis_size("stripe"), 1, 128)], [VMEM] * 2, [split_square], flops=unit)(middle, other_root)
@@ -402,20 +380,24 @@
     def landing(count):
         return [pltpu.VMEM((count,) + piece, f32), pltpu.SemaphoreType.DMA((count * HALF // CHUNK,))]
 
-    placed, scale = call(
-        place_near, [slab, (1, 128)], [VMEM] * 4 + [SMEM], landing(2), out_specs=[HBM, VMEM]
+    placed, facts = call(
+        functools.partial(place_near, pairs),
+        [slab, (2 * pairs - 1, 128)],
+        [VMEM] * 4 + [SMEM],
+        landing(2),
+        out_specs=[HBM, VMEM],
     )(mine, across[0], prec, totals, owner_blocks)
     across = [flip(x, 1) for x in direct[1:]]
     count = pairs - 1
-    for swapped, found in ((False, direct[1:]), (True, across)):
+    for swapped, found in ((0, direct[1:]), (1, across)):
         (placed,) = call(
             functools.partial(place_more, swapped, count),
             [slab],
-            [VMEM] * (count + 1) + [SMEM, HBM],
+            [VMEM] * (count + 1) + [HBM],
             landing(count),
             out_specs=[HBM],
-            input_output_aliases={count + 2: 0},
-        )(*found, scale, owner_blocks, placed)
+            input_output_aliases={count + 1: 0},
+        )(*found, facts, placed)
     return placed, new_stat[None, None]
 
 

time: 75.2 us -> 74.7 us (level)
  Pallas kernels: 17.3 us -> 14.7 us
  waiting for transfers between devices: 39.4 us -> 41.5 us
    pallas_call x2, Pallas kernels: 5.23 us -> 3.13 us  [the longest x1 1.75 us: per_device(): call(functools.partial(place_near, pairs), [slab, (2 * pairs - 1, 128)],...]
    all_to_all x1, waiting for transfers between devices: 3.68 us -> 5.78 us  [per_device(): sums = lax.all_to_all(sums, AXES, 0, 0)]
    pallas_call x2, Pallas kernels: 2.88 us -> 1.9 us  [per_device(): call(functools.partial(place_more, swapped, count), [slab], [VMEM] * (cou...]
  transfers between devices with their start and end apart: 15 -> 15, of which waited for: 8 -> 8; matrix products, arithmetic and copies ran while one was open for 1% -> 1% of each run, Pallas kernels for 15% -> 12%
where the time goes in v6:
time: 74.7 us; the launch traced here: 74.5 us
  waiting for transfers between devices  41.5 us (56%)
  starting transfers between devices  16.7 us (22%)
  Pallas kernels  14.7 us (20%)
  between operations  0.79 us (1%)
    ppermute x11, waiting for transfers between devices, flip(): lax.ppermute(x, 'rep', [(i, i ^ mask) for i in range(lax.axis_size('rep'))])  30.5 us
    all_to_all x1, starting transfers between devices, per_device(): sums = lax.all_to_all(sums, AXES, 0, 0)  6.95 us
    all_to_all x1, waiting for transfers between devices, per_device(): sums = lax.all_to_all(sums, AXES, 0, 0)  5.78 us
    all_to_all x1, waiting for transfers between devices, per_device(): prec = lax.all_to_all(prec, 'stripe', 0, 0)  5.17 us
    ppermute x11, starting transfers between devices, flip(): lax.ppermute(x, 'rep', [(i, i ^ mask) for i in range(lax.axis_size('rep'))])  5.06 us
    all_to_all x1, starting transfers between devices, per_device(): prec = lax.all_to_all(prec, 'stripe', 0, 0)  3.31 us
    pallas_call x2, Pallas kernels, terms(): call(functools.partial(grad_terms, plan), [(len(chips),) + piece for chip...  3.04 us
    pallas_call x1, Pallas kernels, per_device(): call(functools.partial(root, devices), [(HALF + HALF // 2, BLOCK), (1, 12...  2.86 us
  transfers between devices with their start and end apart: 15, of which 8 were waited for; matrix products, arithmetic and copies ran while one was open for 1% of the time, Pallas kernels for 12%

profile of v6, /device:TPU:0, one launch (start us, length us, event | category | flops | bytes accessed | tf_op | source)
XLA Modules:
  0.0 74.5 jit_solution(1088152359993479054)
XLA Ops:
  0.6 1.5 %shard_map.60 = f32[1,256,512]{2,1,0:T(8,128)S(1)} custom-call(bf16[256,1024]{1,0:T(8,128)(2,1)} %acts.3, bf16[256,512]{1,0:T(8,128)(2,1)} %grads.3, s32[1,2]{1,0:T(1,128)} %owners.5), custom_call_target="tpu_custom_call" | custom-call | flops 67108864 | bytes 1048576 | tf_op jit(solution)/shard_map/pallas_call | solution.py:315
  2.7 1.5 %shard_map.59 = (f32[1,256,512]{2,1,0:T(8,128)S(1)}, f32[1,256,512]{2,1,0:T(8,128)S(1)}, f32[1,256,512]{2,1,0:T(8,128)S(1)}) custom-call(bf16[256,1024]{1,0:T(8,128)(2,1)} %acts.3, bf16[256,512]{1,0:T(8,128)(2,1)} %grads.3, s32[1,2]{1,0:T(1,128)} %owners.5), custom_call_target="tpu_custom_call" | custom-call | flops 201326592 | bytes 1048576 | tf_op jit(solution)/shard_map/pallas_call | solution.py:315
  4.4 3.0 %collective-permute-start.2 = (f32[256,512]{1,0:T(8,128)S(1)}, f32[256,512]{1,0:T(8,128)S(1)}, u32[]{:S(2)}, u32[]{:S(2)}) collective-permute-start(f32[256,512]{1,0:T(8,128)S(1)} %add_bitcast_fusion), channel_id=1, source_target_pairs={{0,16},{8,24},{16,0},{24,8},{1,17},{9,25},{17,1},{25,9},{2,18},{10... | collective-permute-start | bytes 1572872 | tf_op jit(solution)/shard_map/ppermute | solution.py:55
  7.5 12.2 %collective-permute-done.2.rest = f32[256,512]{1,0:T(8,128)S(1)} collective-permute-done((f32[256,512]{1,0:T(8,128)S(1)}, f32[256,512]{1,0:T(8,128)S(1)}, u32[]{:S(2)}, u32[]{:S(2)}) %collective-permute-start.2) | collective-permute-done | bytes 524320 | tf_op jit(solution)/shard_map/ppermute | solution.py:55
  19.8 0.8 %shard_map.62 = (f32[256,512]{1,0:T(8,128)S(1)}, f32[32,2,128]{2,1,0:T(2,128)}) custom-call(f32[1,256,512]{2,1,0:T(8,128)S(1)} %get-tuple-element.18.keep, f32[1,256,512]{2,1,0:T(8,128)S(1)} %collective-permute-done.got, f32[256,512]{1,0:T(8,128)S(1)} %collective-permute-done.2.rest, f32[1,128]{1,0:T(1,128)S(1)} %get-tuple-element.21.trace), custom_call_target="tpu_custom_call" | custom-call | bytes 1048576 | tf_op jit(solution)/shard_map/pallas_call | solution.py:341
  20.5 7.0 %all-to-all-start = ((f32[32,2,128]{2,1,0:T(2,128)}), f32[32,2,128]{2,1,0:T(2,128)S(1)}, u32[]{:S(2)}, u32[]{:S(2)}) async-start(f32[32,2,128]{2,1,0:T(2,128)} %get-tuple-element.27), calls=%async_computation | async-start | bytes 65536 | tf_op jit(solution)/shard_map/all_to_all | solution.py:345
  27.5 1.4 %shard_map.63 = (f32[2,128]{1,0:T(2,128)S(1)}, f32[264,512]{1,0:T(8,128)S(1)}, bf16[2,512,512]{2,1,0:T(8,128)(2,1)}) custom-call(f32[256,512]{1,0:T(8,128)S(1)} %get-tuple-element.22.half, f32[256,512]{1,0:T(8,128)S(1)} %collective-permute-done.3.other, f32[264,512]{1,0:T(8,128)S(1)} %collective-permute-done.4.old), custom_call_target="tpu_custom_call" | custom-call | flops 805306368 | bytes 1048576 | tf_op jit(solution)/shard_map/pallas_call | solution.py:346
  28.9 5.8 %all-to-all-done.sums = f32[32,2,128]{2,1,0:T(2,128)S(1)} async-done(((f32[32,2,128]{2,1,0:T(2,128)}), f32[32,2,128]{2,1,0:T(2,128)S(1)}, u32[]{:S(2)}, u32[]{:S(2)}) %all-to-all-start) | async-done | bytes 32800 | tf_op jit(solution)/shard_map/all_to_all | solution.py:345
  34.7 2.9 %shard_map.64 = (f32[384,512]{1,0:T(8,128)S(1)}, f32[1,128]{1,0:T(1,128)S(1)}) custom-call(f32[264,512]{1,0:T(8,128)S(1)} %get-tuple-element.25.stat, f32[2,128]{1,0:T(2,128)S(1)} %get-tuple-element.26.facts, f32[32,2,128]{2,1,0:T(2,128)S(1)} %all-to-all-done.sums), custom_call_target="tpu_custom_call" | custom-call | flops 2415919104 | bytes 1048576 | tf_op jit(solution)/shard_map/pallas_call | solution.py:355
  37.8 1.2 %shard_map.65.middle = bf16[2,512,512]{2,1,0:T(8,128)(2,1)S(1)} custom-call(bf16[2,512,512]{2,1,0:T(8,128)(2,1)S(1)} %copy-done.2, f32[384,512]{1,0:T(8,128)S(1)} %get-tuple-element.28.packed), custom_call_target="tpu_custom_call" | custom-call | flops 805306368 | bytes 1048576 | tf_op jit(solution)/shard_map/pallas_call | solution.py:363
  38.9 1.0 %collective-permute-done.5.packed = f32[384,512]{1,0:T(8,128)S(1)} collective-permute-done((f32[384,512]{1,0:T(8,128)S(1)}, f32[384,512]{1,0:T(8,128)S(1)}, u32[]{:S(2)}, u32[]{:S(2)}) %collective-permute-start.5) | collective-permute-done | bytes 786464 | tf_op jit(solution)/shard_map/ppermute | solution.py:55
  39.9 0.6 shard_map.66
  40.6 0.7 collective-permute-start.6
  41.3 1.4 %collective-permute-start.12 = (f32[264,512]{1,0:T(8,128)S(1)}, f32[264,512]{1,0:T(8,128)S(1)}, u32[]{:S(2)}, u32[]{:S(2)}) collective-permute-start(f32[264,512]{1,0:T(8,128)S(1)} %get-tuple-element.25.stat), channel_id=1, source_target_pairs={{8,0},{24,8},{0,16},{16,24},{9,1},{25,9},{1,17},{17,25},{10,2},{26... | collective-permute-start | bytes 1622024 | tf_op jit(solution)/shard_map/ppermute | solution.py:354
  42.7 12.8 %collective-permute-done.6.refs_0_ = f32[256,512]{1,0:T(8,128)S(1)} collective-permute-done((f32[256,512]{1,0:T(8,128)S(1)}, f32[256,512]{1,0:T(8,128)S(1)}, u32[]{:S(2)}, u32[]{:S(2)}) %collective-permute-start.6) | collective-permute-done | bytes 524320 | tf_op jit(solution)/shard_map/ppermute | solution.py:55
  55.9 1.4 %collective-permute-done.11 = f32[8,1,128]{2,1,0:T(1,128)S(1)} collective-permute-done((f32[8,1,128]{2,1,0:T(1,128)S(1)}, f32[8,1,128]{2,1,0:T(1,128)S(1)}, u32[]{:S(2)}, u32[]{:S(2)}) %collective-permute-start.11) | collective-permute-done | bytes 4128 | tf_op jit(solution)/shard_map/ppermute | solution.py:55
  57.3 2.2 %collective-permute-done.10 = f32[8,1,128]{2,1,0:T(1,128)S(1)} collective-permute-done((f32[8,1,128]{2,1,0:T(1,128)S(1)}, f32[8,1,128]{2,1,0:T(1,128)S(1)}, u32[]{:S(2)}, u32[]{:S(2)}) %collective-permute-start.10) | collective-permute-done | bytes 4128 | tf_op jit(solution)/shard_map/ppermute | solution.py:55
  59.6 0.9 %collective-permute-done.9 = f32[8,1,128]{2,1,0:T(1,128)S(1)} collective-permute-done((f32[8,1,128]{2,1,0:T(1,128)S(1)}, f32[8,1,128]{2,1,0:T(1,128)S(1)}, u32[]{:S(2)}, u32[]{:S(2)}) %collective-permute-start.9) | collective-permute-done | bytes 4128 | tf_op jit(solution)/shard_map/ppermute | solution.py:55
  61.1 3.3 %all-to-all-start.1 = ((f32[8,1,128]{2,1,0:T(1,128)}), f32[8,1,128]{2,1,0:T(1,128)S(1)}, u32[]{:S(2)}, u32[]{:S(2)}) async-start(f32[8,1,128]{2,1,0:T(1,128)} %bitcast.8), calls=%async_computation.1 | async-start | bytes 8192 | tf_op jit(solution)/shard_map/all_to_all | solution.py:376
  64.4 1.2 %shard_map.70 = f32[512,512]{1,0:T(8,128)} custom-call(f32[264,512]{1,0:T(8,128)S(1)} %collective-permute-done.12.packed), custom_call_target="tpu_custom_call" | custom-call | bytes 1048576 | tf_op jit(solution)/shard_map/pallas_call | solution.py:377
  65.6 5.2 %all-to-all-done.1.sums = f32[8,1,128]{2,1,0:T(1,128)S(1)} async-done(((f32[8,1,128]{2,1,0:T(1,128)}), f32[8,1,128]{2,1,0:T(1,128)S(1)}, u32[]{:S(2)}, u32[]{:S(2)}) %all-to-all-start.1) | async-done | bytes 4128 | tf_op jit(solution)/shard_map/all_to_all | solution.py:376
  70.8 1.8 %shard_map.67 = (f32[1024,512]{1,0:T(8,128)}, f32[3,128]{1,0:T(4,128)S(1)}) custom-call(f32[256,512]{1,0:T(8,128)S(1)} %get-tuple-element.29.direct, f32[256,512]{1,0:T(8,128)S(1)} %collective-permute-done.8.across, f32[8,1,128]{2,1,0:T(1,128)S(1)} %all-to-all-done.1.sums, f32[1,128]{1,0:T(1,128)S(1)} %get-tuple-element.31.totals, s32[1,2]{1,0:T(1,128)S(1)} %copy-done.1), custom_call_target="tpu_custom_call" | custom-call | bytes 1048576 | tf_op jit(solution)/shard_map/pallas_call | solution.py:383
  72.6 0.9 %shard_map.68.refs_2_ = f32[1024,512]{1,0:T(8,128)} custom-call(f32[256,512]{1,0:T(8,128)S(1)} %collective-permute-done.6.refs_0_, f32[3,128]{1,0:T(4,128)S(1)} %get-tuple-element.32.refs_1_, f32[1024,512]{1,0:T(8,128)} %get-tuple-element.33.refs_2_), custom_call_target="tpu_custom_call", output_to_operand_aliasing={{}: (2, {})} | custom-call | bytes 1048576 | tf_op jit(solution)/shard_map/pallas_call | solution.py:393
  73.5 0.9 %shard_map.69 = f32[1024,512]{1,0:T(8,128)} custom-call(f32[256,512]{1,0:T(8,128)S(1)} %collective-permute-done.7.refs_0_, f32[3,128]{1,0:T(4,128)S(1)} %get-tuple-element.32.refs_1_, f32[1024,512]{1,0:T(8,128)} %shard_map.68.refs_2_), custom_call_target="tpu_custom_call", output_to_operand_aliasing={{}: (2, {})} | custom-call | bytes 1048576 | tf_op jit(solution)/shard_map/pallas_call | solution.py:393
  (26 shorter events, 2.1 us)
Async XLA Ops:
  0.6 6.8 %copy-start = (f32[1,1,512,512]{3,2,1,0:T(8,128)S(1)}, f32[1,1,512,512]{3,2,1,0:T(8,128)}, u32[]{:S(2)}) copy-start(f32[1,1,512,512]{3,2,1,0:T(8,128)} %param.6) | copy-start | bytes 3145732
  2.1 2.2 %collective-permute-start.1 = (f32[1,256,512]{2,1,0:T(8,128)S(1)}, f32[1,256,512]{2,1,0:T(8,128)S(1)}, u32[]{:S(2)}, u32[]{:S(2)}) collective-permute-start(f32[1,256,512]{2,1,0:T(8,128)S(1)} %shard_map.60), channel_id=1, source_target_pairs={{0,8},{8,0},{16,24},{24,16},{1,9},{9,1},{17,25},{25,17},{2,10},{10... | collective-permute-start | bytes 1572872 | tf_op jit(solution)/shard_map/ppermute | solution.py:55
  4.2 3.3 %collective-permute-start = (f32[1,256,512]{2,1,0:T(8,128)S(1)}, f32[1,256,512]{2,1,0:T(8,128)S(1)}, u32[]{:S(2)}, u32[]{:S(2)}) collective-permute-start(f32[1,256,512]{2,1,0:T(8,128)S(1)} %get-tuple-element.19), channel_id=1, source_target_pairs={{0,8},{8,0},{16,24},{24,16},{1,9},{9,1},{17,25},{25,17},{2,10},{10... | collective-permute-start | bytes 1572872 | tf_op jit(solution)/shard_map/ppermute | solution.py:55
  4.4 15.3 %collective-permute-start.2 = (f32[256,512]{1,0:T(8,128)S(1)}, f32[256,512]{1,0:T(8,128)S(1)}, u32[]{:S(2)}, u32[]{:S(2)}) collective-permute-start(f32[256,512]{1,0:T(8,128)S(1)} %add_bitcast_fusion), channel_id=1, source_target_pairs={{0,16},{8,24},{16,0},{24,8},{1,17},{9,25},{17,1},{25,9},{2,18},{10... | collective-permute-start | bytes 1572872 | tf_op jit(solution)/shard_map/ppermute | solution.py:55
  7.5 20.0 %collective-permute-start.4 = (f32[264,512]{1,0:T(8,128)S(1)}, f32[264,512]{1,0:T(8,128)S(1)}, u32[]{:S(2)}, u32[]{:S(2)}) collective-permute-start(f32[264,512]{1,0:T(8,128)S(1)} %get-tuple-element.23), channel_id=1, source_target_pairs={{0,8},{8,24},{16,0},{24,16},{1,9},{9,25},{17,1},{25,17},{2,10},{10... | collective-permute-start | bytes 1622024 | tf_op jit(solution)/shard_map/ppermute | solution.py:340
  20.5 7.0 %collective-permute-start.3 = (f32[256,512]{1,0:T(8,128)S(1)}, f32[256,512]{1,0:T(8,128)S(1)}, u32[]{:S(2)}, u32[]{:S(2)}) collective-permute-start(f32[256,512]{1,0:T(8,128)S(1)} %get-tuple-element.22.half), channel_id=1, source_target_pairs={{0,8},{8,0},{16,24},{24,16},{1,9},{9,1},{17,25},{25,17},{2,10},{10... | collective-permute-start | bytes 1572872 | tf_op jit(solution)/shard_map/ppermute | solution.py:55
  20.5 14.2 %all-to-all-start = ((f32[32,2,128]{2,1,0:T(2,128)}), f32[32,2,128]{2,1,0:T(2,128)S(1)}, u32[]{:S(2)}, u32[]{:S(2)}) async-start(f32[32,2,128]{2,1,0:T(2,128)} %get-tuple-element.27), calls=%async_computation | async-start | bytes 65536 | tf_op jit(solution)/shard_map/all_to_all | solution.py:345
  34.7 3.1 %copy-start.2 = (bf16[2,512,512]{2,1,0:T(8,128)(2,1)S(1)}, bf16[2,512,512]{2,1,0:T(8,128)(2,1)}, u32[]{:S(2)}) copy-start(bf16[2,512,512]{2,1,0:T(8,128)(2,1)} %get-tuple-element.24.g) | copy-start | bytes 3145732
  37.6 2.4 %collective-permute-start.5 = (f32[384,512]{1,0:T(8,128)S(1)}, f32[384,512]{1,0:T(8,128)S(1)}, u32[]{:S(2)}, u32[]{:S(2)}) collective-permute-start(f32[384,512]{1,0:T(8,128)S(1)} %get-tuple-element.28.packed), channel_id=1, source_target_pairs={{0,8},{8,0},{16,24},{24,16},{1,9},{9,1},{17,25},{25,17},{2,10},{10... | collective-permute-start | bytes 2359304 | tf_op jit(solution)/shard_map/ppermute | solution.py:55
  38.9 31.9 %copy-start.1 = (s32[1,2]{1,0:T(1,128)S(1)}, s32[1,2]{1,0:T(1,128)}, u32[]{:S(2)}) copy-start(s32[1,2]{1,0:T(1,128)} %owners.5) | copy-start | bytes 28
  40.6 14.9 %collective-permute-start.6 = (f32[256,512]{1,0:T(8,128)S(1)}, f32[256,512]{1,0:T(8,128)S(1)}, u32[]{:S(2)}, u32[]{:S(2)}) collective-permute-start(f32[256,512]{1,0:T(8,128)S(1)} %get-tuple-element.29.direct), channel_id=1, source_target_pairs={{0,16},{8,24},{16,0},{24,8},{1,17},{9,25},{17,1},{25,9},{2,18},{10... | collective-permute-start | bytes 1572872 | tf_op jit(solution)/shard_map/ppermute | solution.py:55
  41.3 23.2 %collective-permute-start.12 = (f32[264,512]{1,0:T(8,128)S(1)}, f32[264,512]{1,0:T(8,128)S(1)}, u32[]{:S(2)}, u32[]{:S(2)}) collective-permute-start(f32[264,512]{1,0:T(8,128)S(1)} %get-tuple-element.25.stat), channel_id=1, source_target_pairs={{8,0},{24,8},{0,16},{16,24},{9,1},{25,9},{1,17},{17,25},{10,2},{26... | collective-permute-start | bytes 1622024 | tf_op jit(solution)/shard_map/ppermute | solution.py:354
  42.7 28.1 %collective-permute-start.8 = (f32[256,512]{1,0:T(8,128)S(1)}, f32[256,512]{1,0:T(8,128)S(1)}, u32[]{:S(2)}, u32[]{:S(2)}) collective-permute-start(f32[256,512]{1,0:T(8,128)S(1)} %get-tuple-element.29.direct), channel_id=1, source_target_pairs={{0,8},{8,0},{16,24},{24,16},{1,9},{9,1},{17,25},{25,17},{2,10},{10... | collective-permute-start | bytes 1572872 | tf_op jit(solution)/shard_map/ppermute | solution.py:55
  55.4 18.1 %collective-permute-start.7 = (f32[256,512]{1,0:T(8,128)S(1)}, f32[256,512]{1,0:T(8,128)S(1)}, u32[]{:S(2)}, u32[]{:S(2)}) collective-permute-start(f32[256,512]{1,0:T(8,128)S(1)} %collective-permute-done.6.refs_0_), channel_id=1, source_target_pairs={{0,8},{8,0},{16,24},{24,16},{1,9},{9,1},{17,25},{25,17},{2,10},{10... | collective-permute-start | bytes 1572872 | tf_op jit(solution)/shard_map/ppermute | solution.py:55
  55.4 1.9 %collective-permute-start.11 = (f32[8,1,128]{2,1,0:T(1,128)S(1)}, f32[8,1,128]{2,1,0:T(1,128)S(1)}, u32[]{:S(2)}, u32[]{:S(2)}) collective-permute-start(f32[8,1,128]{2,1,0:T(1,128)S(1)} %get-tuple-element.30), channel_id=1, source_target_pairs={{0,8},{8,0},{16,24},{24,16},{1,9},{9,1},{17,25},{25,17},{2,10},{10... | collective-permute-start | bytes 12296 | tf_op jit(solution)/shard_map/ppermute | solution.py:55
  55.9 3.6 %collective-permute-start.10 = (f32[8,1,128]{2,1,0:T(1,128)S(1)}, f32[8,1,128]{2,1,0:T(1,128)S(1)}, u32[]{:S(2)}, u32[]{:S(2)}) collective-permute-start(f32[8,1,128]{2,1,0:T(1,128)S(1)} %get-tuple-element.30), channel_id=1, source_target_pairs={{0,16},{8,24},{16,0},{24,8},{1,17},{9,25},{17,1},{25,9},{2,18},{10... | collective-permute-start | bytes 12296 | tf_op jit(solution)/shard_map/ppermute | solution.py:55
  57.3 3.2 %collective-permute-start.9 = (f32[8,1,128]{2,1,0:T(1,128)S(1)}, f32[8,1,128]{2,1,0:T(1,128)S(1)}, u32[]{:S(2)}, u32[]{:S(2)}) collective-permute-start(f32[8,1,128]{2,1,0:T(1,128)S(1)} %get-tuple-element.30), channel_id=1, source_target_pairs={{0,24},{8,16},{16,8},{24,0},{1,25},{9,17},{17,9},{25,1},{2,26},{10... | collective-permute-start | bytes 12296 | tf_op jit(solution)/shard_map/ppermute | solution.py:55
  61.1 9.7 %all-to-all-start.1 = ((f32[8,1,128]{2,1,0:T(1,128)}), f32[8,1,128]{2,1,0:T(1,128)S(1)}, u32[]{:S(2)}, u32[]{:S(2)}) async-start(f32[8,1,128]{2,1,0:T(1,128)} %bitcast.8), calls=%async_computation.1 | async-start | bytes 8192 | tf_op jit(solution)/shard_map/all_to_all | solution.py:376

commit v7 on v6

--- a/solution.py
+++ b/solution.py
@@ -101,7 +101,12 @@
     return jnp.where(i <= j, u, ut), jnp.where(i > j, u, jnp.where(i < j, ut, diag))
 
 
-def pack_stat(stat, out, trace):
+def pack_stat(pairs, stat, owners, out, trace, rows):
+    chip, core = chip_core()
+    for n in range(2 * pairs):
+        half = core if n < pairs else 1 - core
+        row = owners[0, lax.bitwise_xor(chip, jnp.int32(n % pairs))] * BLOCK + half * HALF
+        rows[n : n + 1, :] = jnp.full((1, 128), row.astype(f32))
     i, j = triangle()
     a, c = stat[LOW, LOW], stat[TOP, TOP]
     pack_into(out, a, stat[LOW, TOP], c)
@@ -157,24 +162,38 @@
         g[0, rows], g[1, rows] = split(src[...])
 
 
-def update_stat(half, other, old, facts, out, g_out, g, sem):
+def unpack_upper(packed):
+    s00, s11 = unpack(packed[LOW, LOW], packed[HALF : HALF + 1, LOW])
+    return jnp.concatenate([s00, packed[LOW, TOP]], axis=1), s11
+
+
+def update_stat(half, other, old, facts, square_out, cube_out, out, g_out, g, s1, s2, stage, sems):
     _, core = chip_core()
     load_gradient(core, half, other, g.at[0])
-    copy = pltpu.make_async_copy(g.at[0], g_out, sem)
-    copy.start()
+    copies = [pltpu.make_async_copy(g.at[0], g_out, sems.at[0]), pltpu.make_async_copy(stage, out, sems.at[1])]
+    copies[0].start()
     for k in range(2):
         g[1, k] = g[0, k].T
     top, corner = upper_product(g.at[1 - core], g.at[core])
-    sa, sc = unpack(old[LOW, LOW], old[HALF : HALF + 1, LOW])
-    s00 = decay_rate * sa + top[:, :HALF]
-    s01 = decay_rate * old[LOW, TOP] + top[:, HALF:]
-    s11 = decay_rate * sc + corner
-    pack_into(out, s00, s01, s11)
+    was_top, was_corner = unpack_upper(old)
+    top = decay_rate * was_top + top
+    corner = decay_rate * was_corner + corner
+    s00, s01 = top[:, :HALF], top[:, HALF:]
+    pack_into(stage, s00, s01, corner)
+    copies[1].start()
     i, j = triangle()
-    trace = total(jnp.where(i == j, s00 + s11, 0.0))
-    norm_sq = total(s00 * s00 + s11 * s11 + 2.0 * (s01 * s01))
+    trace = total(jnp.where(i == j, s00 + corner, 0.0))
+    norm_sq = total(s00 * s00 + corner * corner + 2.0 * (s01 * s01))
+    inv = 1.0 / jnp.sqrt(norm_sq + epsilon)
+    spread(top * inv, corner * inv, s1)
+    top, corner = upper_product(s1, s1)
+    pack_into(square_out, top[:, :HALF], top[:, HALF:], corner)
+    spread(top, corner, s2)
+    top, corner = upper_product(s1, s2)
+    pack_into(cube_out, top[:, :HALF], top[:, HALF:], corner)
     facts[...] = jnp.concatenate([jnp.broadcast_to(x, (1, 128)) for x in (norm_sq, trace)], axis=0)
-    copy.wait()
+    for copy in copies:
+        copy.wait()
 
 
 def coefficients(devices, facts, sums):
@@ -197,17 +216,19 @@
     return k, grad_sq
 
 
-def root(devices, stat, facts, sums, out, totals, first, inner, cube):
+def root(devices, stat_in, g_in, square, cubed, facts, sums, out, totals, g, stat, inner, cube, sems):
+    copy = pltpu.make_async_copy(stat_in, stat, sems.at[0])
+    fetch = pltpu.make_async_copy(g_in, g, sems.at[1])
+    copy.start()
+    fetch.start()
     k, grad_sq = coefficients(devices, facts, sums)
     inv = 1.0 / jnp.sqrt(facts[0:1, 0:1] + epsilon)
-    s00, s11 = unpack(stat[LOW, LOW], stat[HALF : HALF + 1, LOW])
-    tops, corners = [jnp.concatenate([s00, stat[LOW, TOP]], axis=1) * inv], [s11 * inv]
-    spread(tops[0], corners[0], first)
-    for x in (first, inner):
-        top, corner = upper_product(first, x)
-        tops.append(top)
-        corners.append(corner)
-        spread(top, corner, inner if x is first else cube)
+    third = unpack_upper(cubed)
+    spread(*third, cube)
+    second = unpack_upper(square)
+    copy.wait()
+    first = [x * inv for x in unpack_upper(stat)]
+    tops, corners = zip(first, second, third)
     spread(*(k[4] * t[0] + k[5] * t[1] + k[6] * t[2] for t in (tops, corners)), inner)
     top, corner = upper_product(cube, inner)
     i, j = triangle()
@@ -219,6 +240,7 @@
     out[HALF:, LOW] = corner[: HALF // 2]
     out[HALF:, TOP] = corner[HALF // 2 :]
     totals[...] = jnp.broadcast_to(grad_sq, (1, 128))
+    fetch.wait()
 
 
 def root_corner(packed):
@@ -277,26 +299,23 @@
         copy.wait()
 
 
-def place_near(pairs, direct, across, sums, totals, owners, out, facts, scaled, sems):
-    chip, core = chip_core()
+def first_row(rows, n):
+    return jnp.max(rows[n : n + 1, :]).astype(jnp.int32)
+
+
+def place_most(pairs, *refs):
+    direct, (across, sums, totals, rows, out, scale, scaled, sems) = refs[:pairs], refs[pairs:]
     prec_sq = jnp.sum(jnp.sum(sums[...], axis=0), axis=1, keepdims=True)
-    scale = jnp.sqrt(totals[0:1, 0:1] / (prec_sq + epsilon))
-    facts[0:1, :] = jnp.broadcast_to(scale, (1, 128))
-    rows = [
-        [owners[0, lax.bitwise_xor(chip, jnp.int32(j))] * BLOCK + half * HALF for j in range(pairs)]
-        for half in (core, 1 - core)
-    ]
-    for n, row in enumerate(rows[0][1:] + rows[1][1:]):
-        facts[n + 1 : n + 2, :] = jnp.full((1, 128), row.astype(f32))
-    write_pieces(((rows[0][0], direct), (rows[1][0], across)), scale, out, scaled, sems)
-
-
-def place_more(swapped, count, *refs):
-    facts, _, out, scaled, sems = refs[count:]
-    pieces = [
-        (jnp.max(facts[n : n + 1, :]).astype(jnp.int32), x) for n, x in enumerate(refs[:count], 1 + swapped * count)
-    ]
-    write_pieces(pieces, facts[0:1, 0:1], out, scaled, sems)
+    factor = jnp.sqrt(totals[0:1, 0:1] / (prec_sq + epsilon))
+    scale[...] = jnp.broadcast_to(factor, (1, 128))
+    pieces = [(first_row(rows, pairs), across)] + [(first_row(rows, n), x) for n, x in enumerate(direct)]
+    write_pieces(pieces, factor, out, scaled, sems)
+
+
+def place_rest(pairs, *refs):
+    across, (scale, rows, _, out, scaled, sems) = refs[: pairs - 1], refs[pairs - 1 :]
+    pieces = [(first_row(rows, pairs + n), x) for n, x in enumerate(across, 1)]
+    write_pieces(pieces, scale[0:1, 0:1], out, scaled, sems)
 
 
 def per_device(activations, out_grads, statistics, owner_blocks):
@@ -309,6 +328,7 @@
 
     whole = jax.ShapeDtypeStruct((2,) + square, bf16)
     split_square = pltpu.VMEM((2,) + square, bf16)
+    packed_buffer = pltpu.VMEM((PACKED, BLOCK), f32)
     m = pairs // 2
 
     def terms(*plan):
@@ -336,38 +356,41 @@
         held = [keep_near[j] + got_near[j] + arrived[j] for j in range(m, 2 * m)]
         arrived = [x + flip(y, 2 * m) for x, y in zip(arrived, held)]
     shuffle = [(s * pairs + p, 2 * p + 1 - s) for s in range(2) for p in range(pairs)]
-    packed, trace = call(pack_stat, [(PACKED, BLOCK), (1, 128)], [VMEM])(statistics[0, 0])
+    packed, trace, rows = call(
+        functools.partial(pack_stat, pairs), [(PACKED, BLOCK), (1, 128), (2 * pairs, 128)], [VMEM, SMEM]
+    )(statistics[0, 0], owner_blocks)
     old = lax.ppermute(packed, "rep", shuffle)
     half, sums = call(
         functools.partial(finish_half, devices), [piece, (devices, 2, 128)], [VMEM] * 4
     )(keep_near, got_near, arrived[0], trace)
     other = flip(half, 1)
     sums = lax.all_to_all(sums, AXES, 0, 0)
-    facts, out_packed, g_split = call(
+    facts, square_p, cube_p, out_packed, g_split = call(
         update_stat,
-        [(2, 128), (PACKED, BLOCK), pltpu.HBM((2,) + square, bf16)],
+        [(2, 128), (PACKED, BLOCK), (PACKED, BLOCK)]
+        + [pltpu.HBM((PACKED, BLOCK), f32), pltpu.HBM((2,) + square, bf16)],
         [VMEM] * 3,
-        [pltpu.VMEM((2, 2) + square, bf16), pltpu.SemaphoreType.DMA],
-        flops=unit,
-        out_specs=[VMEM] * 2 + [HBM],
+        [pltpu.VMEM((2, 2) + square, bf16), split_square, split_square, packed_buffer, pltpu.SemaphoreType.DMA((2,))],
+        flops=3 * unit,
+        out_specs=[VMEM] * 3 + [HBM] * 2,
     )(half, other, old)
     new_packed = lax.ppermute(out_packed, "rep", [(t, s) for s, t in shuffle])
-    mine_root, totals = call(
+    mine_root, totals, g_split = call(
         functools.partial(root, devices),
-        [(HALF + HALF // 2, BLOCK), (1, 128)],
-        [VMEM] * 3,
-        [split_square] * 3,
-        flops=3 * unit,
-    )(out_packed, facts, sums)
+        [(HALF + HALF // 2, BLOCK), (1, 128), whole],
+        [HBM] * 2 + [VMEM] * 4,
+        [packed_buffer, split_square, split_square, pltpu.SemaphoreType.DMA((2,))],
+        flops=unit,
+    )(in_hbm(out_packed), in_hbm(g_split), square_p, cube_p, facts, sums)
     other_root = flip(mine_root, 1)
     (middle,) = call(half_way, [whole], [VMEM] * 2, [split_square], flops=unit)(g_split, mine_root)
     mine, prec = call(last_product, [piece, (lax.axis_size("stripe"), 1, 128)], [VMEM] * 2, [split_square], flops=unit)(middle, other_root)
 
-    bit = 1
+    bit = 2
     while bit < rep_count:
-        masks = [x for x in (3 * bit, 2 * bit, bit) if x < rep_count]
-        prec = sum((flip(prec, x) for x in masks), prec)
-        bit *= 4
+        prec = prec + flip(prec, bit)
+        bit *= 2
+    prec = prec + flip(prec, 1)
     direct, m = [mine], 1
     while m < pairs:
         direct = direct + [flip(x, 2 * m) for x in direct]
@@ -380,24 +403,22 @@
     def landing(count):
         return [pltpu.VMEM((count,) + piece, f32), pltpu.SemaphoreType.DMA((count * HALF // CHUNK,))]
 
-    placed, facts = call(
-        functools.partial(place_near, pairs),
-        [slab, (2 * pairs - 1, 128)],
-        [VMEM] * 4 + [SMEM],
-        landing(2),
+    forwarded = [flip(x, 1) for x in direct[1:]]
+    placed, scale = call(
+        functools.partial(place_most, pairs),
+        [slab, (1, 128)],
+        [VMEM] * (pairs + 4),
+        landing(pairs + 1),
         out_specs=[HBM, VMEM],
-    )(mine, across[0], prec, totals, owner_blocks)
-    across = [flip(x, 1) for x in direct[1:]]
-    count = pairs - 1
-    for swapped, found in ((0, direct[1:]), (1, across)):
-        (placed,) = call(
-            functools.partial(place_more, swapped, count),
-            [slab],
-            [VMEM] * (count + 1) + [HBM],
-            landing(count),
-            out_specs=[HBM],
-            input_output_aliases={count + 1: 0},
-        )(*found, facts, placed)
+    )(*direct, across[0], prec, totals, rows)
+    (placed,) = call(
+        functools.partial(place_rest, pairs),
+        [slab],
+        [VMEM] * (pairs + 1) + [HBM],
+        landing(pairs - 1),
+        out_specs=[HBM],
+        input_output_aliases={pairs + 1: 0},
+    )(*forwarded, scale, rows, placed)
     return placed, new_stat[None, None]
 
 

time: 74.7 us -> 74.4 us (level)
  waiting for transfers between devices: 41.5 us -> 38.1 us
  local copies, waits for them, and re-layouts: 0.01 us -> 1.87 us
    all_to_all x1, waiting for transfers between devices: 5.78 us -> 2.99 us  [per_device(): sums = lax.all_to_all(sums, AXES, 0, 0)]
    unnamed x6 -> x10, local copies, waits for them, and re-layouts: 0.01 us -> 1.87 us
    pallas_call x5 -> x4, Pallas kernels: 5.08 us -> 6.34 us  [the longest x1 3.36 us: per_device(): call(update_stat, [(2, 128), (PACKED, BLOCK), (PACKED, BLOCK)] + [pltpu.H...]
    pallas_call x1, Pallas kernels: 2.86 us -> 2.07 us  [per_device(): call(functools.partial(root, devices), [(HALF + HALF // 2, BLOCK), (1, 12...]
    ppermute x11 -> x10, starting transfers between devices: 5.06 us -> 5.78 us  [flip(): lax.ppermute(x, 'rep', [(i, i ^ mask) for i in range(lax.axis_size('rep'))])]
    ppermute x11 -> x10, waiting for transfers between devices: 30.5 us -> 29.9 us  [flip(): lax.ppermute(x, 'rep', [(i, i ^ mask) for i in range(lax.axis_size('rep'))])]
  transfers between devices with their start and end apart: 15 -> 14, of which waited for: 8 -> 7; matrix products, arithmetic and copies ran while one was open for 1% -> 1% of each run, Pallas kernels for 12% -> 14%
where the time goes in v7:
time: 74.4 us; the launch traced here: 74.1 us
  waiting for transfers between devices  38.1 us (51%)
  starting transfers between devices  17.4 us (23%)
  Pallas kernels  15.2 us (20%)
  local copies, waits for them, and re-layouts  1.87 us (3%)
  between operations  0.81 us (1%)
    ppermute x10, waiting for transfers between devices, flip(): lax.ppermute(x, 'rep', [(i, i ^ mask) for i in range(lax.axis_size('rep'))])  29.9 us
    all_to_all x1, starting transfers between devices, per_device(): sums = lax.all_to_all(sums, AXES, 0, 0)  6.95 us
    ppermute x10, starting transfers between devices, flip(): lax.ppermute(x, 'rep', [(i, i ^ mask) for i in range(lax.axis_size('rep'))])  5.78 us
    all_to_all x1, waiting for transfers between devices, per_device(): prec = lax.all_to_all(prec, 'stripe', 0, 0)  5.17 us
    pallas_call x1, Pallas kernels, per_device(): call(update_stat, [(2, 128), (PACKED, BLOCK), (PACKED, BLOCK)] + [pltpu.H...  3.36 us
    all_to_all x1, starting transfers between devices, per_device(): prec = lax.all_to_all(prec, 'stripe', 0, 0)  3.31 us
    pallas_call x2, Pallas kernels, terms(): call(functools.partial(grad_terms, plan), [(len(chips),) + piece for chip...  3.04 us
    all_to_all x1, waiting for transfers between devices, per_device(): sums = lax.all_to_all(sums, AXES, 0, 0)  2.99 us
  transfers between devices with their start and end apart: 14, of which 7 were waited for; matrix products, arithmetic and copies ran while one was open for 1% of the time, Pallas kernels for 14%

profile of v7, /device:TPU:0, one launch (start us, length us, event | category | flops | bytes accessed | tf_op | source)
XLA Modules:
  0.0 74.1 jit_solution(7783762378738765621)
XLA Ops:
  0.7 1.5 %shard_map.60 = f32[1,256,512]{2,1,0:T(8,128)S(1)} custom-call(bf16[256,1024]{1,0:T(8,128)(2,1)} %acts.3, bf16[256,512]{1,0:T(8,128)(2,1)} %grads.3, s32[1,2]{1,0:T(1,128)} %owners.5), custom_call_target="tpu_custom_call" | custom-call | flops 67108864 | bytes 1048576 | tf_op jit(solution)/shard_map/pallas_call | solution.py:335
  2.7 1.5 %shard_map.59 = (f32[1,256,512]{2,1,0:T(8,128)S(1)}, f32[1,256,512]{2,1,0:T(8,128)S(1)}, f32[1,256,512]{2,1,0:T(8,128)S(1)}) custom-call(bf16[256,1024]{1,0:T(8,128)(2,1)} %acts.3, bf16[256,512]{1,0:T(8,128)(2,1)} %grads.3, s32[1,2]{1,0:T(1,128)} %owners.5), custom_call_target="tpu_custom_call" | custom-call | flops 201326592 | bytes 1048576 | tf_op jit(solution)/shard_map/pallas_call | solution.py:335
  4.4 3.0 %collective-permute-start.2 = (f32[256,512]{1,0:T(8,128)S(1)}, f32[256,512]{1,0:T(8,128)S(1)}, u32[]{:S(2)}, u32[]{:S(2)}) collective-permute-start(f32[256,512]{1,0:T(8,128)S(1)} %add_bitcast_fusion), channel_id=1, source_target_pairs={{0,16},{8,24},{16,0},{24,8},{1,17},{9,25},{17,1},{25,9},{2,18},{10... | collective-permute-start | bytes 1572872 | tf_op jit(solution)/shard_map/ppermute | solution.py:55
  8.1 11.7 %collective-permute-done.2.rest = f32[256,512]{1,0:T(8,128)S(1)} collective-permute-done((f32[256,512]{1,0:T(8,128)S(1)}, f32[256,512]{1,0:T(8,128)S(1)}, u32[]{:S(2)}, u32[]{:S(2)}) %collective-permute-start.2) | collective-permute-done | bytes 524320 | tf_op jit(solution)/shard_map/ppermute | solution.py:55
  19.8 0.8 %shard_map.62 = (f32[256,512]{1,0:T(8,128)S(1)}, f32[32,2,128]{2,1,0:T(2,128)}) custom-call(f32[1,256,512]{2,1,0:T(8,128)S(1)} %get-tuple-element.22.keep, f32[1,256,512]{2,1,0:T(8,128)S(1)} %collective-permute-done.got, f32[256,512]{1,0:T(8,128)S(1)} %collective-permute-done.2.rest, f32[1,128]{1,0:T(1,128)S(1)} %get-tuple-element.25.trace), custom_call_target="tpu_custom_call" | custom-call | bytes 1048576 | tf_op jit(solution)/shard_map/pallas_call | solution.py:363
  20.6 6.9 %all-to-all-start = ((f32[32,2,128]{2,1,0:T(2,128)}), f32[32,2,128]{2,1,0:T(2,128)S(1)}, u32[]{:S(2)}, u32[]{:S(2)}) async-start(f32[32,2,128]{2,1,0:T(2,128)} %get-tuple-element.33), calls=%async_computation | async-start | bytes 65536 | tf_op jit(solution)/shard_map/all_to_all | solution.py:367
  27.5 3.4 %shard_map.63 = (f32[2,128]{1,0:T(2,128)S(1)}, f32[264,512]{1,0:T(8,128)S(1)}, f32[264,512]{1,0:T(8,128)S(1)}, f32[264,512]{1,0:T(8,128)}, bf16[2,512,512]{2,1,0:T(8,128)(2,1)}) custom-call(f32[256,512]{1,0:T(8,128)S(1)} %get-tuple-element.26.half, f32[256,512]{1,0:T(8,128)S(1)} %collective-permute-done.3.other, f32[264,512]{1,0:T(8,128)S(1)} %collective-permute-done.4.old), custom_call_target="tpu_custom_call" | custom-call | flops 2415919104 | bytes 1048576 | tf_op jit(solution)/shard_map/pallas_call | solution.py:368
  30.9 0.8 %copy-done.2 = f32[264,512]{1,0:T(8,128)} copy-done((f32[264,512]{1,0:T(8,128)}, f32[264,512]{1,0:T(8,128)S(1)}, u32[]{:S(2)}) %copy-start.2) | copy-done | bytes 540696
  31.7 3.0 %all-to-all-done.sums = f32[32,2,128]{2,1,0:T(2,128)S(1)} async-done(((f32[32,2,128]{2,1,0:T(2,128)}), f32[32,2,128]{2,1,0:T(2,128)S(1)}, u32[]{:S(2)}, u32[]{:S(2)}) %all-to-all-start) | async-done | bytes 32800 | tf_op jit(solution)/shard_map/all_to_all | solution.py:367
  34.7 1.0 %copy-done.3 = f32[264,512]{1,0:T(8,128)S(1)} copy-done((f32[264,512]{1,0:T(8,128)S(1)}, f32[264,512]{1,0:T(8,128)}, u32[]{:S(2)}) %copy-start.3) | copy-done | bytes 540696
  35.8 2.1 %shard_map.64 = (f32[384,512]{1,0:T(8,128)S(1)}, f32[1,128]{1,0:T(1,128)S(1)}, bf16[2,512,512]{2,1,0:T(8,128)(2,1)S(1)}) custom-call(f32[264,512]{1,0:T(8,128)} %get-tuple-element.28.stat_in, bf16[2,512,512]{2,1,0:T(8,128)(2,1)} %get-tuple-element.29.g_in, f32[264,512]{1,0:T(8,128)S(1)} %get-tuple-element.30.square, f32[264,512]{1,0:T(8,128)S(1)} %copy-done.3, ...), custom_call_target="tpu_custom_call" | custom-call | flops 805306368 | bytes 1048576 | tf_op jit(solution)/shard_map/pallas_call | solution.py:378
  38.0 1.2 %shard_map.65.middle = bf16[2,512,512]{2,1,0:T(8,128)(2,1)S(1)} custom-call(bf16[2,512,512]{2,1,0:T(8,128)(2,1)S(1)} %get-tuple-element.34.g, f32[384,512]{1,0:T(8,128)S(1)} %get-tuple-element.35.packed), custom_call_target="tpu_custom_call" | custom-call | flops 805306368 | bytes 1048576 | tf_op jit(solution)/shard_map/pallas_call | solution.py:386
  39.2 1.0 %collective-permute-done.5.packed = f32[384,512]{1,0:T(8,128)S(1)} collective-permute-done((f32[384,512]{1,0:T(8,128)S(1)}, f32[384,512]{1,0:T(8,128)S(1)}, u32[]{:S(2)}, u32[]{:S(2)}) %collective-permute-start.5) | collective-permute-done | bytes 786464 | tf_op jit(solution)/shard_map/ppermute | solution.py:55
  40.8 0.7 collective-permute-start.6
  41.5 1.4 %collective-permute-start.11 = (f32[264,512]{1,0:T(8,128)S(1)}, f32[264,512]{1,0:T(8,128)S(1)}, u32[]{:S(2)}, u32[]{:S(2)}) collective-permute-start(f32[264,512]{1,0:T(8,128)S(1)} %copy-done.4), channel_id=1, source_target_pairs={{8,0},{24,8},{0,16},{16,24},{9,1},{25,9},{1,17},{17,25},{10,2},{26... | collective-permute-start | bytes 1622024 | tf_op jit(solution)/shard_map/ppermute | solution.py:377
  42.9 12.8 %collective-permute-done.6.refs_1_ = f32[256,512]{1,0:T(8,128)S(1)} collective-permute-done((f32[256,512]{1,0:T(8,128)S(1)}, f32[256,512]{1,0:T(8,128)S(1)}, u32[]{:S(2)}, u32[]{:S(2)}) %collective-permute-start.6) | collective-permute-done | bytes 524320 | tf_op jit(solution)/shard_map/ppermute | solution.py:55
  55.7 3.6 %collective-permute-done.9 = f32[8,1,128]{2,1,0:T(1,128)S(1)} collective-permute-done((f32[8,1,128]{2,1,0:T(1,128)S(1)}, f32[8,1,128]{2,1,0:T(1,128)S(1)}, u32[]{:S(2)}, u32[]{:S(2)}) %collective-permute-start.9) | collective-permute-done | bytes 4128 | tf_op jit(solution)/shard_map/ppermute | solution.py:55
  59.4 1.2 %collective-permute-start.10 = (f32[8,1,128]{2,1,0:T(1,128)S(1)}, f32[8,1,128]{2,1,0:T(1,128)S(1)}, u32[]{:S(2)}, u32[]{:S(2)}) collective-permute-start(f32[8,1,128]{2,1,0:T(1,128)S(1)} %add.14), channel_id=1, source_target_pairs={{0,8},{8,0},{16,24},{24,16},{1,9},{9,1},{17,25},{25,17},{2,10},{10... | collective-permute-start | bytes 12296 | tf_op jit(solution)/shard_map/ppermute | solution.py:55
  60.6 0.8 %collective-permute-done.10 = f32[8,1,128]{2,1,0:T(1,128)S(1)} collective-permute-done((f32[8,1,128]{2,1,0:T(1,128)S(1)}, f32[8,1,128]{2,1,0:T(1,128)S(1)}, u32[]{:S(2)}, u32[]{:S(2)}) %collective-permute-start.10) | collective-permute-done | bytes 4128 | tf_op jit(solution)/shard_map/ppermute | solution.py:55
  62.0 3.3 %all-to-all-start.1 = ((f32[8,1,128]{2,1,0:T(1,128)}), f32[8,1,128]{2,1,0:T(1,128)S(1)}, u32[]{:S(2)}, u32[]{:S(2)}) async-start(f32[8,1,128]{2,1,0:T(1,128)} %add.15), calls=%async_computation.1 | async-start | bytes 8192 | tf_op jit(solution)/shard_map/all_to_all | solution.py:399
  65.3 1.2 %shard_map.69 = f32[512,512]{1,0:T(8,128)} custom-call(f32[264,512]{1,0:T(8,128)S(1)} %collective-permute-done.11.packed), custom_call_target="tpu_custom_call" | custom-call | bytes 1048576 | tf_op jit(solution)/shard_map/pallas_call | solution.py:400
  66.5 5.2 %all-to-all-done.1.refs_3_ = f32[8,1,128]{2,1,0:T(1,128)S(1)} async-done(((f32[8,1,128]{2,1,0:T(1,128)}), f32[8,1,128]{2,1,0:T(1,128)S(1)}, u32[]{:S(2)}, u32[]{:S(2)}) %all-to-all-start.1) | async-done | bytes 4128 | tf_op jit(solution)/shard_map/all_to_all | solution.py:399
  71.7 1.4 %shard_map.67 = (f32[1024,512]{1,0:T(8,128)}, f32[1,128]{1,0:T(1,128)S(1)}) custom-call(f32[256,512]{1,0:T(8,128)S(1)} %get-tuple-element.36.refs_0_, f32[256,512]{1,0:T(8,128)S(1)} %collective-permute-done.6.refs_1_, f32[256,512]{1,0:T(8,128)S(1)} %collective-permute-done.8.refs_2_, f32[8,1,128]{2,1,0:T(1,128)S(1)} %all-to-all-done.1.refs_3_, ...), custom_call_target="tpu_custom_call" | custom-call | bytes 1048576 | tf_op jit(solution)/shard_map/pallas_call | solution.py:407
  73.1 1.0 %shard_map.68 = f32[1024,512]{1,0:T(8,128)} custom-call(f32[256,512]{1,0:T(8,128)S(1)} %collective-permute-done.7.refs_0_, f32[1,128]{1,0:T(1,128)S(1)} %get-tuple-element.40.refs_1_, f32[4,128]{1,0:T(4,128)S(1)} %get-tuple-element.39.refs_5_.refs_2_, f32[1024,512]{1,0:T(8,128)} %get-tuple-element.41.refs_3_), custom_call_target="tpu_custom_call", output_to_operand_aliasing={{}: (3, {})} | custom-call | bytes 1048576 | tf_op jit(solution)/shard_map/pallas_call | solution.py:414
  (28 shorter events, 2.8 us)
Async XLA Ops:
  0.6 6.8 %copy-start.1 = (s32[1,2]{1,0:T(1,128)S(1)}, s32[1,2]{1,0:T(1,128)}, u32[]{:S(2)}) copy-start(s32[1,2]{1,0:T(1,128)} %owners.5) | copy-start | bytes 28
  0.6 6.8 %copy-start = (f32[1,1,512,512]{3,2,1,0:T(8,128)S(1)}, f32[1,1,512,512]{3,2,1,0:T(8,128)}, u32[]{:S(2)}) copy-start(f32[1,1,512,512]{3,2,1,0:T(8,128)} %param.6) | copy-start | bytes 3145732
  2.1 2.2 %collective-permute-start.1 = (f32[1,256,512]{2,1,0:T(8,128)S(1)}, f32[1,256,512]{2,1,0:T(8,128)S(1)}, u32[]{:S(2)}, u32[]{:S(2)}) collective-permute-start(f32[1,256,512]{2,1,0:T(8,128)S(1)} %shard_map.60), channel_id=1, source_target_pairs={{0,8},{8,0},{16,24},{24,16},{1,9},{9,1},{17,25},{25,17},{2,10},{10... | collective-permute-start | bytes 1572872 | tf_op jit(solution)/shard_map/ppermute | solution.py:55
  4.3 3.8 %collective-permute-start = (f32[1,256,512]{2,1,0:T(8,128)S(1)}, f32[1,256,512]{2,1,0:T(8,128)S(1)}, u32[]{:S(2)}, u32[]{:S(2)}) collective-permute-start(f32[1,256,512]{2,1,0:T(8,128)S(1)} %get-tuple-element.23), channel_id=1, source_target_pairs={{0,8},{8,0},{16,24},{24,16},{1,9},{9,1},{17,25},{25,17},{2,10},{10... | collective-permute-start | bytes 1572872 | tf_op jit(solution)/shard_map/ppermute | solution.py:55
  4.4 15.3 %collective-permute-start.2 = (f32[256,512]{1,0:T(8,128)S(1)}, f32[256,512]{1,0:T(8,128)S(1)}, u32[]{:S(2)}, u32[]{:S(2)}) collective-permute-start(f32[256,512]{1,0:T(8,128)S(1)} %add_bitcast_fusion), channel_id=1, source_target_pairs={{0,16},{8,24},{16,0},{24,8},{1,17},{9,25},{17,1},{25,9},{2,18},{10... | collective-permute-start | bytes 1572872 | tf_op jit(solution)/shard_map/ppermute | solution.py:55
  8.1 19.5 %collective-permute-start.4 = (f32[264,512]{1,0:T(8,128)S(1)}, f32[264,512]{1,0:T(8,128)S(1)}, u32[]{:S(2)}, u32[]{:S(2)}) collective-permute-start(f32[264,512]{1,0:T(8,128)S(1)} %get-tuple-element.27), channel_id=1, source_target_pairs={{0,8},{8,24},{16,0},{24,16},{1,9},{9,25},{17,1},{25,17},{2,10},{10... | collective-permute-start | bytes 1622024 | tf_op jit(solution)/shard_map/ppermute | solution.py:362
  20.6 7.0 %collective-permute-start.3 = (f32[256,512]{1,0:T(8,128)S(1)}, f32[256,512]{1,0:T(8,128)S(1)}, u32[]{:S(2)}, u32[]{:S(2)}) collective-permute-start(f32[256,512]{1,0:T(8,128)S(1)} %get-tuple-element.26.half), channel_id=1, source_target_pairs={{0,8},{8,0},{16,24},{24,16},{1,9},{9,1},{17,25},{25,17},{2,10},{10... | collective-permute-start | bytes 1572872 | tf_op jit(solution)/shard_map/ppermute | solution.py:55
  20.6 14.1 %all-to-all-start = ((f32[32,2,128]{2,1,0:T(2,128)}), f32[32,2,128]{2,1,0:T(2,128)S(1)}, u32[]{:S(2)}, u32[]{:S(2)}) async-start(f32[32,2,128]{2,1,0:T(2,128)} %get-tuple-element.33), calls=%async_computation | async-start | bytes 65536 | tf_op jit(solution)/shard_map/all_to_all | solution.py:367
  30.9 0.8 %copy-start.2 = (f32[264,512]{1,0:T(8,128)}, f32[264,512]{1,0:T(8,128)S(1)}, u32[]{:S(2)}) copy-start(f32[264,512]{1,0:T(8,128)S(1)} %get-tuple-element.31.cubed) | copy-start | bytes 1622020
  34.7 1.0 %copy-start.3 = (f32[264,512]{1,0:T(8,128)S(1)}, f32[264,512]{1,0:T(8,128)}, u32[]{:S(2)}) copy-start(f32[264,512]{1,0:T(8,128)} %copy-done.2) | copy-start | bytes 1622020
  37.8 2.4 %collective-permute-start.5 = (f32[384,512]{1,0:T(8,128)S(1)}, f32[384,512]{1,0:T(8,128)S(1)}, u32[]{:S(2)}, u32[]{:S(2)}) collective-permute-start(f32[384,512]{1,0:T(8,128)S(1)} %get-tuple-element.35.packed), channel_id=1, source_target_pairs={{0,8},{8,0},{16,24},{24,16},{1,9},{9,1},{17,25},{25,17},{2,10},{10... | collective-permute-start | bytes 2359304 | tf_op jit(solution)/shard_map/ppermute | solution.py:55
  39.2 2.3 %copy-start.4 = (f32[264,512]{1,0:T(8,128)S(1)}, f32[264,512]{1,0:T(8,128)}, u32[]{:S(2)}) copy-start(f32[264,512]{1,0:T(8,128)} %get-tuple-element.28.stat_in) | copy-start | bytes 1622020
  40.8 14.9 %collective-permute-start.6 = (f32[256,512]{1,0:T(8,128)S(1)}, f32[256,512]{1,0:T(8,128)S(1)}, u32[]{:S(2)}, u32[]{:S(2)}) collective-permute-start(f32[256,512]{1,0:T(8,128)S(1)} %get-tuple-element.36.refs_0_), channel_id=1, source_target_pairs={{0,16},{8,24},{16,0},{24,8},{1,17},{9,25},{17,1},{25,9},{2,18},{10... | collective-permute-start | bytes 1572872 | tf_op jit(solution)/shard_map/ppermute | solution.py:55
  41.5 23.8 %collective-permute-start.11 = (f32[264,512]{1,0:T(8,128)S(1)}, f32[264,512]{1,0:T(8,128)S(1)}, u32[]{:S(2)}, u32[]{:S(2)}) collective-permute-start(f32[264,512]{1,0:T(8,128)S(1)} %copy-done.4), channel_id=1, source_target_pairs={{8,0},{24,8},{0,16},{16,24},{9,1},{25,9},{1,17},{17,25},{10,2},{26... | collective-permute-start | bytes 1622024 | tf_op jit(solution)/shard_map/ppermute | solution.py:377
  42.9 28.7 %collective-permute-start.8 = (f32[256,512]{1,0:T(8,128)S(1)}, f32[256,512]{1,0:T(8,128)S(1)}, u32[]{:S(2)}, u32[]{:S(2)}) collective-permute-start(f32[256,512]{1,0:T(8,128)S(1)} %get-tuple-element.36.refs_0_), channel_id=1, source_target_pairs={{0,8},{8,0},{16,24},{24,16},{1,9},{9,1},{17,25},{25,17},{2,10},{10... | collective-permute-start | bytes 1572872 | tf_op jit(solution)/shard_map/ppermute | solution.py:55
  55.7 17.4 %collective-permute-start.7 = (f32[256,512]{1,0:T(8,128)S(1)}, f32[256,512]{1,0:T(8,128)S(1)}, u32[]{:S(2)}, u32[]{:S(2)}) collective-permute-start(f32[256,512]{1,0:T(8,128)S(1)} %collective-permute-done.6.refs_1_), channel_id=1, source_target_pairs={{0,8},{8,0},{16,24},{24,16},{1,9},{9,1},{17,25},{25,17},{2,10},{10... | collective-permute-start | bytes 1572872 | tf_op jit(solution)/shard_map/ppermute | solution.py:55
  55.7 3.6 %collective-permute-start.9 = (f32[8,1,128]{2,1,0:T(1,128)S(1)}, f32[8,1,128]{2,1,0:T(1,128)S(1)}, u32[]{:S(2)}, u32[]{:S(2)}) collective-permute-start(f32[8,1,128]{2,1,0:T(1,128)S(1)} %get-tuple-element.37), channel_id=1, source_target_pairs={{0,16},{8,24},{16,0},{24,8},{1,17},{9,25},{17,1},{25,9},{2,18},{10... | collective-permute-start | bytes 12296 | tf_op jit(solution)/shard_map/ppermute | solution.py:55
  59.4 2.0 %collective-permute-start.10 = (f32[8,1,128]{2,1,0:T(1,128)S(1)}, f32[8,1,128]{2,1,0:T(1,128)S(1)}, u32[]{:S(2)}, u32[]{:S(2)}) collective-permute-start(f32[8,1,128]{2,1,0:T(1,128)S(1)} %add.14), channel_id=1, source_target_pairs={{0,8},{8,0},{16,24},{24,16},{1,9},{9,1},{17,25},{25,17},{2,10},{10... | collective-permute-start | bytes 12296 | tf_op jit(solution)/shard_map/ppermute | solution.py:55
  62.0 9.7 %all-to-all-start.1 = ((f32[8,1,128]{2,1,0:T(1,128)}), f32[8,1,128]{2,1,0:T(1,128)S(1)}, u32[]{:S(2)}, u32[]{:S(2)}) async-start(f32[8,1,128]{2,1,0:T(1,128)} %add.15), calls=%async_computation.1 | async-start | bytes 8192 | tf_op jit(solution)/shard_map/all_to_all | solution.py:399

commit v8 on v7

--- a/solution.py
+++ b/solution.py
@@ -322,6 +322,7 @@
     rep_count = lax.axis_size("rep")
     pairs = rep_count // 2
     devices = rep_count * lax.axis_size("stripe")
+    stripes = lax.axis_size("stripe")
     tokens = activations.shape[0]
     piece, square = (HALF, BLOCK), (BLOCK, BLOCK)
     unit = 6 * BLOCK**3
@@ -373,6 +374,7 @@
         [pltpu.VMEM((2, 2) + square, bf16), split_square, split_square, packed_buffer, pltpu.SemaphoreType.DMA((2,))],
         flops=3 * unit,
         out_specs=[VMEM] * 3 + [HBM] * 2,
+        input_output_aliases={2: 1},
     )(half, other, old)
     new_packed = lax.ppermute(out_packed, "rep", [(t, s) for s, t in shuffle])
     mine_root, totals, g_split = call(
@@ -384,19 +386,20 @@
     )(in_hbm(out_packed), in_hbm(g_split), square_p, cube_p, facts, sums)
     other_root = flip(mine_root, 1)
     (middle,) = call(half_way, [whole], [VMEM] * 2, [split_square], flops=unit)(g_split, mine_root)
-    mine, prec = call(last_product, [piece, (lax.axis_size("stripe"), 1, 128)], [VMEM] * 2, [split_square], flops=unit)(middle, other_root)
+    mine, prec = call(last_product, [piece, (2 * stripes, 1, 128)], [VMEM] * 2, [split_square], flops=unit)(middle, other_root)
 
     bit = 2
     while bit < rep_count:
         prec = prec + flip(prec, bit)
         bit *= 2
-    prec = prec + flip(prec, 1)
     direct, m = [mine], 1
     while m < pairs:
         direct = direct + [flip(x, 2 * m) for x in direct]
         m *= 2
     across = [flip(mine, 1)]
-    prec = lax.all_to_all(prec, "stripe", 0, 0)
+    near = [(s + stripes // 4) % stripes for s in range(stripes)]
+    groups = [[(2 * q + c) * stripes + s for s in near for c in range(2)] for q in range(pairs)]
+    prec = lax.all_to_all(prec, AXES, 0, 0, axis_index_groups=groups)
     (new_stat,) = call(unpack_stat, [square], [VMEM])(new_packed)
     slab = (pairs * BLOCK, out_grads.shape[1])
 

time: 74.4 us -> 70.9 us (0.953)
  local copies, waits for them, and re-layouts: 1.87 us -> 0.02 us
  waiting for transfers between devices: 38.1 us -> 36.8 us
    unnamed x10 -> x6, local copies, waits for them, and re-layouts: 1.87 us -> 0.02 us
    all_to_all x1, waiting for transfers between devices: 5.17 us -> 3.81 us  [per_device(): prec = lax.all_to_all(prec, AXES, 0, 0, axis_index_groups=groups)]
    ppermute x10 -> x9, starting transfers between devices: 5.78 us -> 4.55 us  [flip(): lax.ppermute(x, 'rep', [(i, i ^ mask) for i in range(lax.axis_size('rep'))])]
    all_to_all x1, starting transfers between devices: 3.31 us -> 4.25 us  [per_device(): prec = lax.all_to_all(prec, AXES, 0, 0, axis_index_groups=groups)]
    all_to_all x1, waiting for transfers between devices: 2.99 us -> 3.8 us  [per_device(): sums = lax.all_to_all(sums, AXES, 0, 0)]
    ppermute x10 -> x9, waiting for transfers between devices: 29.9 us -> 29.2 us  [flip(): lax.ppermute(x, 'rep', [(i, i ^ mask) for i in range(lax.axis_size('rep'))])]
  transfers between devices with their start and end apart: 14 -> 13, of which waited for: 7 -> 6; matrix products, arithmetic and copies ran while one was open for 1% -> 1% of each run, Pallas kernels for 14% -> 14%
where the time goes in v8:
time: 70.9 us; the launch traced here: 70.7 us
  waiting for transfers between devices  36.8 us (52%)
  starting transfers between devices  17.2 us (24%)
  Pallas kernels  15.2 us (21%)
  between operations  0.78 us (1%)
    ppermute x9, waiting for transfers between devices, flip(): lax.ppermute(x, 'rep', [(i, i ^ mask) for i in range(lax.axis_size('rep'))])  29.2 us
    all_to_all x1, starting transfers between devices, per_device(): sums = lax.all_to_all(sums, AXES, 0, 0)  6.95 us
    ppermute x9, starting transfers between devices, flip(): lax.ppermute(x, 'rep', [(i, i ^ mask) for i in range(lax.axis_size('rep'))])  4.55 us
    all_to_all x1, starting transfers between devices, per_device(): prec = lax.all_to_all(prec, AXES, 0, 0, axis_index_groups=groups)  4.25 us
    all_to_all x1, waiting for transfers between devices, per_device(): prec = lax.all_to_all(prec, AXES, 0, 0, axis_index_groups=groups)  3.81 us
    all_to_all x1, waiting for transfers between devices, per_device(): sums = lax.all_to_all(sums, AXES, 0, 0)  3.8 us
    pallas_call x1, Pallas kernels, per_device(): call(update_stat, [(2, 128), (PACKED, BLOCK), (PACKED, BLOCK)] + [pltpu.H...  3.36 us
    pallas_call x2, Pallas kernels, terms(): call(functools.partial(grad_terms, plan), [(len(chips),) + piece for chip...  3.04 us
  transfers between devices with their start and end apart: 13, of which 6 were waited for; matrix products, arithmetic and copies ran while one was open for 1% of the time, Pallas kernels for 14%

profile of v8, /device:TPU:0, one launch (start us, length us, event | category | flops | bytes accessed | tf_op | source)
XLA Modules:
  0.0 70.7 jit_solution(10225319914265456119)
XLA Ops:
  0.7 1.5 %shard_map.60 = f32[1,256,512]{2,1,0:T(8,128)S(1)} custom-call(bf16[256,1024]{1,0:T(8,128)(2,1)} %acts.3, bf16[256,512]{1,0:T(8,128)(2,1)} %grads.3, s32[1,2]{1,0:T(1,128)} %owners.5), custom_call_target="tpu_custom_call" | custom-call | flops 67108864 | bytes 1048576 | tf_op jit(solution)/shard_map/pallas_call | solution.py:336
  2.1 0.6 collective-permute-start.1
  2.7 1.5 %shard_map.59 = (f32[1,256,512]{2,1,0:T(8,128)S(1)}, f32[1,256,512]{2,1,0:T(8,128)S(1)}, f32[1,256,512]{2,1,0:T(8,128)S(1)}) custom-call(bf16[256,1024]{1,0:T(8,128)(2,1)} %acts.3, bf16[256,512]{1,0:T(8,128)(2,1)} %grads.3, s32[1,2]{1,0:T(1,128)} %owners.5), custom_call_target="tpu_custom_call" | custom-call | flops 201326592 | bytes 1048576 | tf_op jit(solution)/shard_map/pallas_call | solution.py:336
  4.4 3.0 %collective-permute-start.2 = (f32[256,512]{1,0:T(8,128)S(1)}, f32[256,512]{1,0:T(8,128)S(1)}, u32[]{:S(2)}, u32[]{:S(2)}) collective-permute-start(f32[256,512]{1,0:T(8,128)S(1)} %add_bitcast_fusion), channel_id=1, source_target_pairs={{0,16},{8,24},{16,0},{24,8},{1,17},{9,25},{17,1},{25,9},{2,18},{10... | collective-permute-start | bytes 1572872 | tf_op jit(solution)/shard_map/ppermute | solution.py:55
  7.5 0.6 shard_map.61
  8.1 11.7 %collective-permute-done.2.rest = f32[256,512]{1,0:T(8,128)S(1)} collective-permute-done((f32[256,512]{1,0:T(8,128)S(1)}, f32[256,512]{1,0:T(8,128)S(1)}, u32[]{:S(2)}, u32[]{:S(2)}) %collective-permute-start.2) | collective-permute-done | bytes 524320 | tf_op jit(solution)/shard_map/ppermute | solution.py:55
  19.8 0.8 %shard_map.62 = (f32[256,512]{1,0:T(8,128)S(1)}, f32[32,2,128]{2,1,0:T(2,128)}) custom-call(f32[1,256,512]{2,1,0:T(8,128)S(1)} %get-tuple-element.22.keep, f32[1,256,512]{2,1,0:T(8,128)S(1)} %collective-permute-done.got, f32[256,512]{1,0:T(8,128)S(1)} %collective-permute-done.2.rest, f32[1,128]{1,0:T(1,128)S(1)} %get-tuple-element.25.trace), custom_call_target="tpu_custom_call" | custom-call | bytes 1048576 | tf_op jit(solution)/shard_map/pallas_call | solution.py:364
  20.6 6.9 %all-to-all-start = ((f32[32,2,128]{2,1,0:T(2,128)}), f32[32,2,128]{2,1,0:T(2,128)S(1)}, u32[]{:S(2)}, u32[]{:S(2)}) async-start(f32[32,2,128]{2,1,0:T(2,128)} %get-tuple-element.33), calls=%async_computation | async-start | bytes 65536 | tf_op jit(solution)/shard_map/all_to_all | solution.py:368
  27.6 3.4 %shard_map.63 = (f32[2,128]{1,0:T(2,128)S(1)}, f32[264,512]{1,0:T(8,128)S(1)}, f32[264,512]{1,0:T(8,128)S(1)}, f32[264,512]{1,0:T(8,128)}, bf16[2,512,512]{2,1,0:T(8,128)(2,1)}) custom-call(f32[256,512]{1,0:T(8,128)S(1)} %get-tuple-element.26.half, f32[256,512]{1,0:T(8,128)S(1)} %collective-permute-done.3.other, ...), custom_call_target="tpu_custom_call", output_to_operand_aliasing={{1}: (2, {})} | custom-call | flops 2415919104 | bytes 1048576 | tf_op jit(solution)/shard_map/pallas_call | solution.py:369
  30.9 3.8 %all-to-all-done.sums = f32[32,2,128]{2,1,0:T(2,128)S(1)} async-done(((f32[32,2,128]{2,1,0:T(2,128)}), f32[32,2,128]{2,1,0:T(2,128)S(1)}, u32[]{:S(2)}, u32[]{:S(2)}) %all-to-all-start) | async-done | bytes 32800 | tf_op jit(solution)/shard_map/all_to_all | solution.py:368
  34.7 2.1 %shard_map.64 = (f32[384,512]{1,0:T(8,128)S(1)}, f32[1,128]{1,0:T(1,128)S(1)}, bf16[2,512,512]{2,1,0:T(8,128)(2,1)S(1)}) custom-call(f32[264,512]{1,0:T(8,128)} %get-tuple-element.28.stat_in, bf16[2,512,512]{2,1,0:T(8,128)(2,1)} %get-tuple-element.29.g_in, f32[264,512]{1,0:T(8,128)S(1)} %get-tuple-element.30.square, f32[264,512]{1,0:T(8,128)S(1)} %get-tuple-element.31.cubed, ...), custom_call_target="tpu_custom_call" | custom-call | flops 805306368 | bytes 1048576 | tf_op jit(solution)/shard_map/pallas_call | solution.py:380
  37.0 1.2 %shard_map.65.middle = bf16[2,512,512]{2,1,0:T(8,128)(2,1)S(1)} custom-call(bf16[2,512,512]{2,1,0:T(8,128)(2,1)S(1)} %get-tuple-element.34.g, f32[384,512]{1,0:T(8,128)S(1)} %get-tuple-element.35.packed), custom_call_target="tpu_custom_call" | custom-call | flops 805306368 | bytes 1048576 | tf_op jit(solution)/shard_map/pallas_call | solution.py:388
  38.2 1.0 %collective-permute-done.5.packed = f32[384,512]{1,0:T(8,128)S(1)} collective-permute-done((f32[384,512]{1,0:T(8,128)S(1)}, f32[384,512]{1,0:T(8,128)S(1)}, u32[]{:S(2)}, u32[]{:S(2)}) %collective-permute-start.5) | collective-permute-done | bytes 786464 | tf_op jit(solution)/shard_map/ppermute | solution.py:55
  39.2 0.6 shard_map.66
  39.8 0.7 collective-permute-start.6
  40.5 1.4 %collective-permute-start.10 = (f32[264,512]{1,0:T(8,128)S(1)}, f32[264,512]{1,0:T(8,128)S(1)}, u32[]{:S(2)}, u32[]{:S(2)}) collective-permute-start(f32[264,512]{1,0:T(8,128)S(1)} %copy-done.2), channel_id=1, source_target_pairs={{8,0},{24,8},{0,16},{16,24},{9,1},{25,9},{1,17},{17,25},{10,2},{26... | collective-permute-start | bytes 1622024 | tf_op jit(solution)/shard_map/ppermute | solution.py:379
  41.9 12.8 %collective-permute-done.6.refs_1_ = f32[256,512]{1,0:T(8,128)S(1)} collective-permute-done((f32[256,512]{1,0:T(8,128)S(1)}, f32[256,512]{1,0:T(8,128)S(1)}, u32[]{:S(2)}, u32[]{:S(2)}) %collective-permute-start.6) | collective-permute-done | bytes 524320 | tf_op jit(solution)/shard_map/ppermute | solution.py:55
  54.7 3.7 %collective-permute-done.9 = f32[16,1,128]{2,1,0:T(1,128)S(1)} collective-permute-done((f32[16,1,128]{2,1,0:T(1,128)S(1)}, f32[16,1,128]{2,1,0:T(1,128)S(1)}, u32[]{:S(2)}, u32[]{:S(2)}) %collective-permute-start.9) | collective-permute-done | bytes 8224 | tf_op jit(solution)/shard_map/ppermute | solution.py:55
  58.4 0.6 add.11
  59.0 4.2 %all-to-all-start.1 = ((f32[16,1,128]{2,1,0:T(1,128)}), f32[16,1,128]{2,1,0:T(1,128)S(1)}, u32[]{:S(2)}, u32[]{:S(2)}) async-start(f32[16,1,128]{2,1,0:T(1,128)} %add.11), calls=%async_computation.1 | async-start | bytes 16384 | tf_op jit(solution)/shard_map/all_to_all | solution.py:402
  63.3 1.2 %shard_map.69 = f32[512,512]{1,0:T(8,128)} custom-call(f32[264,512]{1,0:T(8,128)S(1)} %collective-permute-done.10.packed), custom_call_target="tpu_custom_call" | custom-call | bytes 1048576 | tf_op jit(solution)/shard_map/pallas_call | solution.py:403
  64.4 3.8 %all-to-all-done.1.refs_3_ = f32[16,1,128]{2,1,0:T(1,128)S(1)} async-done(((f32[16,1,128]{2,1,0:T(1,128)}), f32[16,1,128]{2,1,0:T(1,128)S(1)}, u32[]{:S(2)}, u32[]{:S(2)}) %all-to-all-start.1) | async-done | bytes 8224 | tf_op jit(solution)/shard_map/all_to_all | solution.py:402
  68.3 1.4 %shard_map.67 = (f32[1024,512]{1,0:T(8,128)}, f32[1,128]{1,0:T(1,128)S(1)}) custom-call(f32[256,512]{1,0:T(8,128)S(1)} %get-tuple-element.36.refs_0_, f32[256,512]{1,0:T(8,128)S(1)} %collective-permute-done.6.refs_1_, f32[256,512]{1,0:T(8,128)S(1)} %collective-permute-done.8.refs_2_, f32[16,1,128]{2,1,0:T(1,128)S(1)} %all-to-all-done.1.refs_3_, ...), custom_call_target="tpu_custom_call" | custom-call | bytes 1048576 | tf_op jit(solution)/shard_map/pallas_call | solution.py:410
  69.7 1.0 %shard_map.68 = f32[1024,512]{1,0:T(8,128)} custom-call(f32[256,512]{1,0:T(8,128)S(1)} %collective-permute-done.7.refs_0_, f32[1,128]{1,0:T(1,128)S(1)} %get-tuple-element.40.refs_1_, f32[4,128]{1,0:T(4,128)S(1)} %get-tuple-element.39.refs_5_.refs_2_, f32[1024,512]{1,0:T(8,128)} %get-tuple-element.41.refs_3_), custom_call_target="tpu_custom_call", output_to_operand_aliasing={{}: (3, {})} | custom-call | bytes 1048576 | tf_op jit(solution)/shard_map/pallas_call | solution.py:417
  (21 shorter events, 0.4 us)
Async XLA Ops:
  0.6 6.8 %copy-start.1 = (s32[1,2]{1,0:T(1,128)S(1)}, s32[1,2]{1,0:T(1,128)}, u32[]{:S(2)}) copy-start(s32[1,2]{1,0:T(1,128)} %owners.5) | copy-start | bytes 28
  0.6 6.8 %copy-start = (f32[1,1,512,512]{3,2,1,0:T(8,128)S(1)}, f32[1,1,512,512]{3,2,1,0:T(8,128)}, u32[]{:S(2)}) copy-start(f32[1,1,512,512]{3,2,1,0:T(8,128)} %param.6) | copy-start | bytes 3145732
  2.1 2.2 %collective-permute-start.1 = (f32[1,256,512]{2,1,0:T(8,128)S(1)}, f32[1,256,512]{2,1,0:T(8,128)S(1)}, u32[]{:S(2)}, u32[]{:S(2)}) collective-permute-start(f32[1,256,512]{2,1,0:T(8,128)S(1)} %shard_map.60), channel_id=1, source_target_pairs={{0,8},{8,0},{16,24},{24,16},{1,9},{9,1},{17,25},{25,17},{2,10},{10... | collective-permute-start | bytes 1572872 | tf_op jit(solution)/shard_map/ppermute | solution.py:55
  4.3 3.8 %collective-permute-start = (f32[1,256,512]{2,1,0:T(8,128)S(1)}, f32[1,256,512]{2,1,0:T(8,128)S(1)}, u32[]{:S(2)}, u32[]{:S(2)}) collective-permute-start(f32[1,256,512]{2,1,0:T(8,128)S(1)} %get-tuple-element.23), channel_id=1, source_target_pairs={{0,8},{8,0},{16,24},{24,16},{1,9},{9,1},{17,25},{25,17},{2,10},{10... | collective-permute-start | bytes 1572872 | tf_op jit(solution)/shard_map/ppermute | solution.py:55
  4.4 15.3 %collective-permute-start.2 = (f32[256,512]{1,0:T(8,128)S(1)}, f32[256,512]{1,0:T(8,128)S(1)}, u32[]{:S(2)}, u32[]{:S(2)}) collective-permute-start(f32[256,512]{1,0:T(8,128)S(1)} %add_bitcast_fusion), channel_id=1, source_target_pairs={{0,16},{8,24},{16,0},{24,8},{1,17},{9,25},{17,1},{25,9},{2,18},{10... | collective-permute-start | bytes 1572872 | tf_op jit(solution)/shard_map/ppermute | solution.py:55
  8.1 19.5 %collective-permute-start.4 = (f32[264,512]{1,0:T(8,128)S(1)}, f32[264,512]{1,0:T(8,128)S(1)}, u32[]{:S(2)}, u32[]{:S(2)}) collective-permute-start(f32[264,512]{1,0:T(8,128)S(1)} %get-tuple-element.27), channel_id=1, source_target_pairs={{0,8},{8,24},{16,0},{24,16},{1,9},{9,25},{17,1},{25,17},{2,10},{10... | collective-permute-start | bytes 1622024 | tf_op jit(solution)/shard_map/ppermute | solution.py:363
  20.6 7.0 %collective-permute-start.3 = (f32[256,512]{1,0:T(8,128)S(1)}, f32[256,512]{1,0:T(8,128)S(1)}, u32[]{:S(2)}, u32[]{:S(2)}) collective-permute-start(f32[256,512]{1,0:T(8,128)S(1)} %get-tuple-element.26.half), channel_id=1, source_target_pairs={{0,8},{8,0},{16,24},{24,16},{1,9},{9,1},{17,25},{25,17},{2,10},{10... | collective-permute-start | bytes 1572872 | tf_op jit(solution)/shard_map/ppermute | solution.py:55
  20.6 14.1 %all-to-all-start = ((f32[32,2,128]{2,1,0:T(2,128)}), f32[32,2,128]{2,1,0:T(2,128)S(1)}, u32[]{:S(2)}, u32[]{:S(2)}) async-start(f32[32,2,128]{2,1,0:T(2,128)} %get-tuple-element.33), calls=%async_computation | async-start | bytes 65536 | tf_op jit(solution)/shard_map/all_to_all | solution.py:368
  36.8 2.4 %collective-permute-start.5 = (f32[384,512]{1,0:T(8,128)S(1)}, f32[384,512]{1,0:T(8,128)S(1)}, u32[]{:S(2)}, u32[]{:S(2)}) collective-permute-start(f32[384,512]{1,0:T(8,128)S(1)} %get-tuple-element.35.packed), channel_id=1, source_target_pairs={{0,8},{8,0},{16,24},{24,16},{1,9},{9,1},{17,25},{25,17},{2,10},{10... | collective-permute-start | bytes 2359304 | tf_op jit(solution)/shard_map/ppermute | solution.py:55
  38.2 2.3 %copy-start.2 = (f32[264,512]{1,0:T(8,128)S(1)}, f32[264,512]{1,0:T(8,128)}, u32[]{:S(2)}) copy-start(f32[264,512]{1,0:T(8,128)} %get-tuple-element.28.stat_in) | copy-start | bytes 1622020
  39.8 14.9 %collective-permute-start.6 = (f32[256,512]{1,0:T(8,128)S(1)}, f32[256,512]{1,0:T(8,128)S(1)}, u32[]{:S(2)}, u32[]{:S(2)}) collective-permute-start(f32[256,512]{1,0:T(8,128)S(1)} %get-tuple-element.36.refs_0_), channel_id=1, source_target_pairs={{0,16},{8,24},{16,0},{24,8},{1,17},{9,25},{17,1},{25,9},{2,18},{10... | collective-permute-start | bytes 1572872 | tf_op jit(solution)/shard_map/ppermute | solution.py:55
  40.5 22.8 %collective-permute-start.10 = (f32[264,512]{1,0:T(8,128)S(1)}, f32[264,512]{1,0:T(8,128)S(1)}, u32[]{:S(2)}, u32[]{:S(2)}) collective-permute-start(f32[264,512]{1,0:T(8,128)S(1)} %copy-done.2), channel_id=1, source_target_pairs={{8,0},{24,8},{0,16},{16,24},{9,1},{25,9},{1,17},{17,25},{10,2},{26... | collective-permute-start | bytes 1622024 | tf_op jit(solution)/shard_map/ppermute | solution.py:379
  41.9 26.4 %collective-permute-start.8 = (f32[256,512]{1,0:T(8,128)S(1)}, f32[256,512]{1,0:T(8,128)S(1)}, u32[]{:S(2)}, u32[]{:S(2)}) collective-permute-start(f32[256,512]{1,0:T(8,128)S(1)} %get-tuple-element.36.refs_0_), channel_id=1, source_target_pairs={{0,8},{8,0},{16,24},{24,16},{1,9},{9,1},{17,25},{25,17},{2,10},{10... | collective-permute-start | bytes 1572872 | tf_op jit(solution)/shard_map/ppermute | solution.py:55
  54.7 15.0 %collective-permute-start.7 = (f32[256,512]{1,0:T(8,128)S(1)}, f32[256,512]{1,0:T(8,128)S(1)}, u32[]{:S(2)}, u32[]{:S(2)}) collective-permute-start(f32[256,512]{1,0:T(8,128)S(1)} %collective-permute-done.6.refs_1_), channel_id=1, source_target_pairs={{0,8},{8,0},{16,24},{24,16},{1,9},{9,1},{17,25},{25,17},{2,10},{10... | collective-permute-start | bytes 1572872 | tf_op jit(solution)/shard_map/ppermute | solution.py:55
  54.7 3.7 %collective-permute-start.9 = (f32[16,1,128]{2,1,0:T(1,128)S(1)}, f32[16,1,128]{2,1,0:T(1,128)S(1)}, u32[]{:S(2)}, u32[]{:S(2)}) collective-permute-start(f32[16,1,128]{2,1,0:T(1,128)S(1)} %get-tuple-element.37), channel_id=1, source_target_pairs={{0,16},{8,24},{16,0},{24,8},{1,17},{9,25},{17,1},{25,9},{2,18},{10... | collective-permute-start | bytes 24584 | tf_op jit(solution)/shard_map/ppermute | solution.py:55
  59.0 9.2 %all-to-all-start.1 = ((f32[16,1,128]{2,1,0:T(1,128)}), f32[16,1,128]{2,1,0:T(1,128)S(1)}, u32[]{:S(2)}, u32[]{:S(2)}) async-start(f32[16,1,128]{2,1,0:T(1,128)} %add.11), calls=%async_computation.1 | async-start | bytes 16384 | tf_op jit(solution)/shard_map/all_to_all | solution.py:402
